TPU v7x, 32 devices: a whole 2x2x4 slice. The times are simulated.
32 devices in a mesh: dp: 32 (over z, y, x, core).
Axes of the slice: x: 2, y: 2, z: 4, core: 2. Of those that a mesh axis runs over, the one named last changes fastest.
Arguments:
- hidden: float32 [16384, 1536], P('dp'), may hold values from -6 to 6
- cotangent: float32 [16384, 1536], P('dp'), may hold values from -6 to 6
- block_ids: int32 [64, 256], P('dp'), may hold values from 0 to 3, never falling along the last dimension, each value on 1 to 128 neighbouring positions
- routes: int32 [16384, 8], P('dp'), may hold values from 0 to 31, all different within a row
- pair_rank: int32 [64, 2048], P('dp'), may hold values from 0 to 2047, each once within a row
- norm1_gain: bfloat16 [1536], P('dp'), may hold values from 0.5 to 1.5
- norm2_gain: bfloat16 [1536], P('dp'), may hold values from 0.5 to 1.5
- w_query: bfloat16 [1536, 1536], P('dp'), may hold values from -0.625 to 0.625
- w_key: bfloat16 [1536, 512], P('dp'), may hold values from -0.625 to 0.625
- w_value: bfloat16 [1536, 512], P('dp'), may hold values from -0.625 to 0.625
- w_out: bfloat16 [1536, 1536], P('dp'), may hold values from -0.875 to 0.875
- w_router: bfloat16 [1536, 32], P('dp'), may hold values from -0.078125 to 0.078125
- w_gate: bfloat16 [32, 1536, 512], P('dp'), may hold values from -0.15625 to 0.15625
- w_up: bfloat16 [32, 1536, 512], P('dp'), may hold values from -0.625 to 0.625
- w_down: bfloat16 [32, 512, 1536], P('dp'), may hold values from -1.5 to 1.5
Outputs:
- output: float32 [16384, 1536], P('dp')
- grad_hidden: float32 [16384, 1536], P('dp')
- grad_norm1: float32 [1536], P('dp')
- grad_norm2: float32 [1536], P('dp')
- grad_query: float32 [1536, 1536], P('dp')
- grad_key: float32 [1536, 512], P('dp')
- grad_value: float32 [1536, 512], P('dp')
- grad_out: float32 [1536, 1536], P('dp')
- grad_router: float32 [1536, 32], P('dp')
- grad_gate: float32 [32, 1536, 512], P('dp')
- grad_up: float32 [32, 1536, 512], P('dp')
- grad_down: float32 [32, 512, 1536], P('dp')
Inputs may be any that keep to these rules, and one draw needn't show every extreme that they name: `block_ids`: within a sequence block numbers never fall; each block holds 1 to 128 tokens, one exactly 128. `routes`: each token names 8 different experts. `pair_rank`: each row is a permutation; pair t * 8 + k is the k-th route of the row's t-th token.
All inputs are finite; a program needn't handle non-finite values.
Results may differ from a plain program's by a relative error of at most 0.017.
The roundings to bfloat16 on the way count: a program that leaves them out, or rounds other values in their place, can miss the bound.
Values may be sent and summed in bfloat16 or wider, within the bound.
No kernel may reach another device: no remote copies, remote signals or barrier semaphores. Data moves between devices by JAX's collectives and lax.ppermute only.
A program may use at most 320 MiB of HBM per device.

v0:
```python
import jax
import jax.numpy as jnp
from jax import lax
from jax.sharding import PartitionSpec as P

H = 24
KVH = 8
HD = 64


res_scale = 0.22
attn_scale = 0.015625
norm_eps = 1e-06
rope_base = 10000.0


def rotary_tables(length, head_size):
    half_size = head_size // 2
    frequency = rope_base ** (-(jnp.arange(half_size, dtype=jnp.float32) * 2.0) / head_size)
    angles = jnp.arange(length, dtype=jnp.float32)[:, None] * frequency[None, :]
    return (jnp.cos(angles)[:, None, :], jnp.sin(angles)[:, None, :])


def rotate(operand, cos_table, sin_table):
    half_size = operand.shape[-1] // 2
    lower_half = operand[..., :half_size]
    upper_half = operand[..., half_size:]
    return jnp.concatenate(
        [
            lower_half * cos_table - upper_half * sin_table,
            upper_half * cos_table + lower_half * sin_table,
        ],
        axis=-1,
    )


def unrotate(operand, cos_table, sin_table):
    half_size = operand.shape[-1] // 2
    lower_half = operand[..., :half_size]
    upper_half = operand[..., half_size:]
    return jnp.concatenate(
        [
            lower_half * cos_table + upper_half * sin_table,
            upper_half * cos_table - lower_half * sin_table,
        ],
        axis=-1,
    )


def slot_table(route_rows, rank_row, experts, capacity):
    flat_routes = route_rows.reshape(-1)
    pair_count = flat_routes.shape[0]
    served_order = jnp.argsort(rank_row)
    ranked = flat_routes[served_order]
    labels = jnp.arange(experts, dtype=jnp.int32)
    onehot = (ranked[:, None] == labels[None, :]).astype(jnp.int32)
    before = jnp.cumsum(onehot, axis=0) - onehot
    ranked_slot = jnp.sum(before * onehot, axis=1)
    pair_slot = ranked_slot[rank_row]
    is_kept = pair_slot < capacity
    slot_dest = jnp.where(is_kept, flat_routes * capacity + pair_slot, experts * capacity)
    slot_pair = jnp.full((experts * capacity + 1,), pair_count, jnp.int32)
    slot_pair = slot_pair.at[slot_dest].set(jnp.arange(pair_count, dtype=jnp.int32))
    return (slot_dest, slot_pair[: experts * capacity])


def norm_backward(grad_normed, source, recip, gain):
    scaled_grad = grad_normed * gain
    grad_source = recip * scaled_grad - source * (recip * recip * recip) * jnp.mean(
        scaled_grad * source, axis=1, keepdims=True
    )
    return (grad_source, jnp.sum(grad_normed * source * recip, axis=0))


def expert_backward(grad_arrived, gate_flat, up_flat, down_local, gate_local, up_local):
    grad_inner = jnp.einsum(
        "rd,fd->rf", grad_arrived, down_local, preferred_element_type=jnp.float32
    )
    logistic = jax.nn.sigmoid(gate_flat)
    grad_gate_pre = (
        grad_inner * up_flat * (logistic * (1.0 + gate_flat * (1.0 - logistic)))
    ).astype(jnp.bfloat16)
    grad_up_pre = (grad_inner * jax.nn.silu(gate_flat)).astype(jnp.bfloat16)
    grad_rows = jnp.einsum(
        "rf,df->rd", grad_gate_pre, gate_local, preferred_element_type=jnp.float32
    )
    grad_rows = grad_rows + jnp.einsum(
        "rf,df->rd", grad_up_pre, up_local, preferred_element_type=jnp.float32
    )
    return (grad_gate_pre, grad_up_pre, grad_rows.astype(jnp.bfloat16))


def on_device(
    hidden,
    cotangent,
    block_ids,
    routes,
    pair_rank,
    norm1_gain,
    norm2_gain,
    w_query,
    w_key,
    w_value,
    w_out,
    w_router,
    w_gate,
    w_up,
    w_down,
):
    micro_count, seq_len = block_ids.shape
    model_width = hidden.shape[1]
    top_count = routes.shape[1]
    experts = lax.axis_size("dp")
    capacity = (9 * seq_len * top_count + 8 * experts - 1) // (8 * experts)
    groups = H // KVH
    cos_table, sin_table = rotary_tables(seq_len, HD)
    gate_local = w_gate[0]
    up_local = w_up[0]
    down_local = w_down[0]
    ff_width = gate_local.shape[1]
    labels = jnp.arange(experts, dtype=jnp.int32)
    bf16 = jnp.bfloat16
    f32 = jnp.float32
    shared = (
        lax.all_gather(norm1_gain, "dp", axis=0, tiled=True),
        lax.all_gather(norm2_gain, "dp", axis=0, tiled=True),
        lax.all_gather(w_query, "dp", axis=0, tiled=True),
        lax.all_gather(w_key, "dp", axis=0, tiled=True),
        lax.all_gather(w_value, "dp", axis=0, tiled=True),
        lax.all_gather(w_out, "dp", axis=0, tiled=True),
        lax.all_gather(w_router, "dp", axis=0, tiled=True),
    )

    def run_expert(arrived):
        item_count = arrived.shape[1]
        flat_in = arrived.reshape(-1, model_width)
        gate_pre = jnp.dot(flat_in, gate_local, preferred_element_type=f32)
        up_pre = jnp.dot(flat_in, up_local, preferred_element_type=f32)
        hidden_act = (jax.nn.silu(gate_pre) * up_pre).astype(bf16)
        produced = (
            jnp.dot(hidden_act, down_local, preferred_element_type=f32)
            .astype(bf16)
            .reshape(experts, item_count, model_width)
        )
        returned = lax.all_to_all(produced, "dp", split_axis=0, concat_axis=0, tiled=True)
        return (
            returned,
            arrived,
            gate_pre.reshape(experts, item_count, ff_width),
            up_pre.reshape(experts, item_count, ff_width),
            hidden_act.reshape(experts, item_count, ff_width),
        )

    def micro_step(totals, inputs):
        tokens_in, cotan_in, blocks, route_rows, rank_row = inputs
        gain_first = shared[0].astype(f32)
        gain_second = shared[1].astype(f32)
        recip_first = lax.rsqrt(jnp.mean(tokens_in * tokens_in, axis=1, keepdims=True) + norm_eps)
        normed_in = (tokens_in * recip_first * gain_first).astype(bf16)
        queries = jnp.dot(normed_in, shared[2], preferred_element_type=f32).reshape(seq_len, H, HD)
        keys_raw = jnp.dot(normed_in, shared[3], preferred_element_type=f32).reshape(
            seq_len, KVH, HD
        )
        values = (
            jnp.dot(normed_in, shared[4], preferred_element_type=f32)
            .astype(bf16)
            .reshape(seq_len, KVH, HD)
        )
        query_rot = (
            rotate(queries, cos_table, sin_table).astype(bf16).reshape(seq_len, KVH, groups, HD)
        )
        key_rot = rotate(keys_raw, cos_table, sin_table).astype(bf16)
        visible = blocks[None, :] <= blocks[:, None]
        scores = attn_scale * jnp.einsum(
            "qhgd,khd->hgqk", query_rot, key_rot, preferred_element_type=f32
        )
        scores = jnp.where(visible, scores, -1e30)
        row_peak = jnp.max(scores, axis=3, keepdims=True)
        shifted_exp = jnp.exp(scores - row_peak)
        row_total = jnp.sum(shifted_exp, axis=3, keepdims=True)
        attn_probs = shifted_exp / row_total
        log_total = row_peak + jnp.log(row_total)
        mixture = (
            jnp.einsum(
                "hgqk,khd->qhgd", attn_probs.astype(bf16), values, preferred_element_type=f32
            )
            .reshape(seq_len, H * HD)
            .astype(bf16)
        )
        attn_out = jnp.dot(mixture, shared[5], preferred_element_type=f32)
        residual = tokens_in + res_scale * attn_out
        recip_second = lax.rsqrt(jnp.mean(residual * residual, axis=1, keepdims=True) + norm_eps)
        normed_mid = (residual * recip_second * gain_second).astype(bf16)
        logits = jnp.dot(normed_mid, shared[6], preferred_element_type=f32)
        picked_mask = route_rows[:, :, None] == labels[None, None, :]
        chosen = jnp.sum(jnp.where(picked_mask, logits[:, None, :], 0.0), axis=2)
        chosen_peak = jnp.max(chosen, axis=1, keepdims=True)
        chosen_exp = jnp.exp(chosen - chosen_peak)
        gate_probs = chosen_exp / jnp.sum(chosen_exp, axis=1, keepdims=True)
        slot_dest, slot_pair = slot_table(route_rows, rank_row, experts, capacity)
        padded_rows = jnp.concatenate([normed_mid, jnp.zeros((1, model_width), bf16)], axis=0)
        outgoing = padded_rows[slot_pair // top_count].reshape(experts, capacity, model_width)
        grad_blend = res_scale * cotan_in
        grad_pairs = (
            (gate_probs[:, :, None] * grad_blend[:, None, :]).astype(bf16).reshape(-1, model_width)
        )
        grad_pairs = jnp.concatenate([grad_pairs, jnp.zeros((1, model_width), bf16)], axis=0)
        grad_outgoing = grad_pairs[slot_pair].reshape(experts, capacity, model_width)
        returned, arrived, gate_pre, up_pre, hidden_act = run_expert(
            lax.all_to_all(outgoing, "dp", split_axis=0, concat_axis=0, tiled=True)
        )
        grad_arrived = lax.all_to_all(
            grad_outgoing, "dp", split_axis=0, concat_axis=0, tiled=True
        ).reshape(-1, model_width)
        grad_gate_pre, grad_up_pre, grad_rows = expert_backward(
            grad_arrived,
            gate_pre.reshape(-1, ff_width),
            up_pre.reshape(-1, ff_width),
            down_local,
            gate_local,
            up_local,
        )
        grad_back = lax.all_to_all(
            grad_rows.reshape(experts, capacity, model_width),
            "dp",
            split_axis=0,
            concat_axis=0,
            tiled=True,
        )
        padded_out = jnp.concatenate(
            [returned.reshape(-1, model_width), jnp.zeros((1, model_width), bf16)], axis=0
        )
        pair_values = padded_out[slot_dest].reshape(seq_len, top_count, model_width).astype(f32)
        blended = jnp.einsum("tk,tkd->td", gate_probs, pair_values)
        output_rows = residual + res_scale * blended
        gain_first = shared[0].astype(f32)
        gain_second = shared[1].astype(f32)
        grad_gates = jnp.sum(pair_values * grad_blend[:, None, :], axis=2)
        act_flat = hidden_act.reshape(-1, ff_width)
        in_flat = arrived.reshape(-1, model_width)
        grad_down_w = jnp.einsum("rf,rd->fd", act_flat, grad_arrived, preferred_element_type=f32)
        grad_gate_w = jnp.einsum("rd,rf->df", in_flat, grad_gate_pre, preferred_element_type=f32)
        grad_up_w = jnp.einsum("rd,rf->df", in_flat, grad_up_pre, preferred_element_type=f32)
        padded_grad = jnp.concatenate(
            [grad_back.reshape(-1, model_width), jnp.zeros((1, model_width), bf16)], axis=0
        )
        grad_mid = jnp.sum(
            padded_grad[slot_dest].reshape(seq_len, top_count, model_width).astype(f32), axis=1
        )
        grad_chosen = gate_probs * (
            grad_gates - jnp.sum(gate_probs * grad_gates, axis=1, keepdims=True)
        )
        grad_logits = jnp.sum(jnp.where(picked_mask, grad_chosen[:, :, None], 0.0), axis=1).astype(
            bf16
        )
        grad_router_w = jnp.einsum("td,te->de", normed_mid, grad_logits, preferred_element_type=f32)
        grad_mid = grad_mid + jnp.einsum(
            "te,de->td", grad_logits, shared[6], preferred_element_type=f32
        )
        grad_residual, grad_gain_second = norm_backward(
            grad_mid, residual, recip_second, gain_second
        )
        grad_residual = cotan_in + grad_residual
        grad_attn = (res_scale * grad_residual).astype(bf16)
        grad_out_w = jnp.einsum("tc,td->cd", mixture, grad_attn, preferred_element_type=f32)
        grad_mixture = (
            jnp.einsum("td,cd->tc", grad_attn, shared[5], preferred_element_type=f32)
            .astype(bf16)
            .reshape(seq_len, KVH, groups, HD)
        )
        scores_again = attn_scale * jnp.einsum(
            "qhgd,khd->hgqk", query_rot, key_rot, preferred_element_type=f32
        )
        scores_again = jnp.where(visible, scores_again, -1e30)
        probs_again = jnp.exp(scores_again - log_total)
        grad_probs = jnp.einsum("qhgd,khd->hgqk", grad_mixture, values, preferred_element_type=f32)
        grad_values = (
            jnp.einsum(
                "hgqk,qhgd->khd", probs_again.astype(bf16), grad_mixture, preferred_element_type=f32
            )
            .astype(bf16)
            .reshape(seq_len, KVH * HD)
        )
        grad_scores = (
            probs_again * (grad_probs - jnp.sum(probs_again * grad_probs, axis=3, keepdims=True))
        ).astype(bf16)
        grad_query_rot = attn_scale * jnp.einsum(
            "hgqk,khd->qhgd", grad_scores, key_rot, preferred_element_type=f32
        )
        grad_key_rot = attn_scale * jnp.einsum(
            "hgqk,qhgd->khd", grad_scores, query_rot, preferred_element_type=f32
        )
        grad_queries = (
            unrotate(grad_query_rot.reshape(seq_len, H, HD), cos_table, sin_table)
            .astype(bf16)
            .reshape(seq_len, H * HD)
        )
        grad_keys = (
            unrotate(grad_key_rot, cos_table, sin_table).astype(bf16).reshape(seq_len, KVH * HD)
        )
        grad_query_w = jnp.einsum("td,tc->dc", normed_in, grad_queries, preferred_element_type=f32)
        grad_key_w = jnp.einsum("td,tc->dc", normed_in, grad_keys, preferred_element_type=f32)
        grad_value_w = jnp.einsum("td,tc->dc", normed_in, grad_values, preferred_element_type=f32)
        grad_normed = jnp.einsum("tc,dc->td", grad_queries, shared[2], preferred_element_type=f32)
        grad_normed = grad_normed + jnp.einsum(
            "tc,dc->td", grad_keys, shared[3], preferred_element_type=f32
        )
        grad_normed = grad_normed + jnp.einsum(
            "tc,dc->td", grad_values, shared[4], preferred_element_type=f32
        )
        grad_source, grad_gain_first = norm_backward(
            grad_normed, tokens_in, recip_first, gain_first
        )
        grad_tokens = grad_residual + grad_source
        updated = (
            totals[0] + grad_gain_first,
            totals[1] + grad_gain_second,
            totals[2] + grad_query_w,
            totals[3] + grad_key_w,
            totals[4] + grad_value_w,
            totals[5] + grad_out_w,
            totals[6] + grad_router_w,
            totals[7] + grad_gate_w,
            totals[8] + grad_up_w,
            totals[9] + grad_down_w,
        )
        return (updated, (output_rows, grad_tokens))

    query_width = w_query.shape[1]
    kv_width = w_key.shape[1]
    start_totals = (
        jnp.zeros((model_width,), f32),
        jnp.zeros((model_width,), f32),
        jnp.zeros((model_width, query_width), f32),
        jnp.zeros((model_width, kv_width), f32),
        jnp.zeros((model_width, kv_width), f32),
        jnp.zeros((query_width, model_width), f32),
        jnp.zeros((model_width, experts), f32),
        jnp.zeros(gate_local.shape, f32),
        jnp.zeros(up_local.shape, f32),
        jnp.zeros(down_local.shape, f32),
    )
    scan_inputs = (
        hidden.reshape(micro_count, seq_len, model_width),
        cotangent.reshape(micro_count, seq_len, model_width),
        block_ids,
        routes.reshape(micro_count, seq_len, top_count),
        pair_rank,
    )
    totals, produced_rows = lax.scan(micro_step, start_totals, scan_inputs)
    reduced = (
        lax.psum_scatter(totals[0], "dp", scatter_dimension=0, tiled=True),
        lax.psum_scatter(totals[1], "dp", scatter_dimension=0, tiled=True),
        lax.psum_scatter(totals[2], "dp", scatter_dimension=0, tiled=True),
        lax.psum_scatter(totals[3], "dp", scatter_dimension=0, tiled=True),
        lax.psum_scatter(totals[4], "dp", scatter_dimension=0, tiled=True),
        lax.psum_scatter(totals[5], "dp", scatter_dimension=0, tiled=True),
        lax.psum_scatter(totals[6], "dp", scatter_dimension=0, tiled=True),
    )
    output_all = produced_rows[0].reshape(-1, model_width)
    grad_all = produced_rows[1].reshape(-1, model_width)
    return (
        output_all,
        grad_all,
        reduced[0],
        reduced[1],
        reduced[2],
        reduced[3],
        reduced[4],
        reduced[5],
        reduced[6],
        totals[7][None],
        totals[8][None],
        totals[9][None],
    )


def solution(mesh):
    return jax.shard_map(
        on_device,
        mesh=mesh,
        in_specs=(
            P("dp", None),
            P("dp", None),
            P("dp", None),
            P("dp", None),
            P("dp", None),
            P("dp"),
            P("dp"),
            P("dp", None),
            P("dp", None),
            P("dp", None),
            P("dp", None),
            P("dp", None),
            P("dp", None, None),
            P("dp", None, None),
            P("dp", None, None),
        ),
        out_specs=(
            P("dp", None),
            P("dp", None),
            P("dp"),
            P("dp"),
            P("dp", None),
            P("dp", None),
            P("dp", None),
            P("dp", None),
            P("dp", None),
            P("dp", None, None),
            P("dp", None, None),
            P("dp", None, None),
        ),
        check_vma=False,
    )
```

profile of v0, /device:TPU:0, one launch (start us, length us, event | category | flops | bytes accessed | tf_op | source)
XLA Modules:
  0.0 2657.8 jit_solution(9015337977634815410)
XLA Ops:
  10.1 44.3 %all-gather = bf16[32,48,32]{1,2,0:T(8,128)(2,1)S(1)} all-gather(bf16[1,48,32]{1,2,0:T(8,128)(2,1)} %bitcast.505), channel_id=1, replica_groups=mesh['dp'=32] {'dp'}, dimensions={0}, use_global_device_ids=true | all-gather | bytes 101376 | tf_op jit(solution)/shard_map/all_gather | solution.py:131
  57.1 37.1 %all-reduce.9 = (bf16[1536]{0:T(1024)(128)(2,1)}, bf16[1536]{0:T(1024)(128)(2,1)}) all-reduce(bf16[1536]{0:T(1024)(128)(2,1)S(1)} %dynamic-update-slice, bf16[1536]{0:T(1024)(128)(2,1)S(1)} %dynamic-update-slice.1), channel_id=1, replica_groups=mesh['dp'=32] {'dp'}, use_global_device_ids=true, to_apply=%add.4 | all-reduce | flops 3072 | bytes 12288
  96.8 37.6 %all-gather.8.cloned.1.call-done = bf16[1536,1536]{1,0:T(8,128)(2,1)} async-done(((bf16[48,1536]{1,0:T(8,128)(2,1)}), bf16[1536,1536]{1,0:T(8,128)(2,1)}) %all-gather.8.cloned.1.call-update) | async-done | bytes 4718608 | tf_op jit(solution)/shard_map/all_gather | solution.py:127
  141.1 49.4 %all-gather.10.cloned.1.call-done = bf16[1536,512]{1,0:T(8,128)(2,1)} async-done(((bf16[48,512]{1,0:T(8,128)(2,1)}), bf16[1536,512]{1,0:T(8,128)(2,1)}) %all-gather.10.cloned.1.call-update) | async-done | bytes 1572880 | tf_op jit(solution)/shard_map/all_gather | solution.py:129
  190.5 65.4 %all-gather.12.cloned.1.call-done = bf16[1536,1536]{1,0:T(8,128)(2,1)} async-done(((bf16[48,1536]{1,0:T(8,128)(2,1)}), bf16[1536,1536]{1,0:T(8,128)(2,1)}) %all-gather.12.cloned.1.call-update) | async-done | bytes 4718608 | tf_op jit(solution)/shard_map/all_gather | solution.py:130
  255.9 1801.1 %while.38 = (s32[]{:T(128)}, f32[1536]{0:T(1024)}, f32[1536]{0:T(1024)}, f32[1536,1536]{1,0:T(8,128)}, f32[1536,512]{1,0:T(8,128)}, /*index=5*/f32[1536,512]{1,0...) while((s32[]{:T(128)}, f32[1536]{0:T(1024)}, ...), condition=%wide.region_22.23_spmd.clone.clone.clone.clone, body=%wide.region_0.22_spmd.clone.clone.clone.clone.sunk | while | flops 43707883520 | bytes 1208352256 | solution.py:350
  347.4 158.9 %all_to_all.52 = bf16[32,72,1536]{2,1,0:T(8,128)(2,1)S(1)} all-to-all(bf16[32,72,1536]{2,1,0:T(8,128)(2,1)} %bitcast.448), channel_id=1, replica_groups=mesh['dp'=32] {'dp'}, dimensions={0} | all-to-all | bytes 14155776 | tf_op jit(solution)/shard_map/while/body/eval_jaxpr/all_to_all | solution.py:210
  529.1 153.9 %all-to-all-done.1 = bf16[32,72,1536]{2,1,0:T(8,128)(2,1)} async-done(((bf16[32,72,1536]{2,1,0:T(8,128)(2,1)}), bf16[32,72,1536]{2,1,0:T(8,128)(2,1)}, u32[]{:S(2)}, u32[]{:S(2)}) %all-to-all-start.1) | async-done | bytes 7077920 | tf_op jit(solution)/shard_map/while/body/eval_jaxpr/all_to_all | solution.py:145
  717.8 18.5 gather_fusion.4
  736.3 158.3 %all_to_all.53 = bf16[32,72,1536]{2,1,0:T(8,128)(2,1)S(1)} all-to-all(bf16[32,72,1536]{2,1,0:T(8,128)(2,1)} %bitcast.449), channel_id=1, replica_groups=mesh['dp'=32] {'dp'}, dimensions={0} | all-to-all | bytes 14155776 | tf_op jit(solution)/shard_map/while/body/eval_jaxpr/all_to_all | solution.py:212
  949.3 133.3 %all-to-all-done.3 = bf16[32,72,1536]{2,1,0:T(8,128)(2,1)} async-done(((bf16[32,72,1536]{2,1,0:T(8,128)(2,1)}), bf16[32,72,1536]{2,1,0:T(8,128)(2,1)}, u32[]{:S(2)}, u32[]{:S(2)}) %all-to-all-start.3) | async-done | bytes 7077920 | tf_op jit(solution)/shard_map/while/body/eval_jaxpr/all_to_all | solution.py:223
  1088.9 17.6 gather_fusion.5
  1247.2 158.5 %all_to_all.52 = bf16[32,72,1536]{2,1,0:T(8,128)(2,1)S(1)} all-to-all(bf16[32,72,1536]{2,1,0:T(8,128)(2,1)} %bitcast.448), channel_id=1, replica_groups=mesh['dp'=32] {'dp'}, dimensions={0} | all-to-all | bytes 14155776 | tf_op jit(solution)/shard_map/while/body/eval_jaxpr/all_to_all | solution.py:210
  1428.4 154.0 %all-to-all-done.1 = bf16[32,72,1536]{2,1,0:T(8,128)(2,1)} async-done(((bf16[32,72,1536]{2,1,0:T(8,128)(2,1)}), bf16[32,72,1536]{2,1,0:T(8,128)(2,1)}, u32[]{:S(2)}, u32[]{:S(2)}) %all-to-all-start.1) | async-done | bytes 7077920 | tf_op jit(solution)/shard_map/while/body/eval_jaxpr/all_to_all | solution.py:145
  1617.1 18.5 gather_fusion.4
  1635.6 158.3 %all_to_all.53 = bf16[32,72,1536]{2,1,0:T(8,128)(2,1)S(1)} all-to-all(bf16[32,72,1536]{2,1,0:T(8,128)(2,1)} %bitcast.449), channel_id=1, replica_groups=mesh['dp'=32] {'dp'}, dimensions={0} | all-to-all | bytes 14155776 | tf_op jit(solution)/shard_map/while/body/eval_jaxpr/all_to_all | solution.py:212
  1850.2 131.9 %all-to-all-done.3 = bf16[32,72,1536]{2,1,0:T(8,128)(2,1)} async-done(((bf16[32,72,1536]{2,1,0:T(8,128)(2,1)}), bf16[32,72,1536]{2,1,0:T(8,128)(2,1)}, u32[]{:S(2)}, u32[]{:S(2)}) %all-to-all-start.3) | async-done | bytes 7077920 | tf_op jit(solution)/shard_map/while/body/eval_jaxpr/all_to_all | solution.py:223
  1988.5 17.4 gather_fusion.5
  2062.0 37.0 %all-reduce.8 = (f32[1536]{0:T(1024)S(1)}, f32[1536]{0:T(1024)S(1)}) all-reduce(f32[1536]{0:T(1024)S(1)} %copy-done.56, f32[1536]{0:T(1024)S(1)} %copy-done.53), channel_id=2, replica_groups=mesh['dp'=32] {'dp'}, use_global_device_ids=true, to_apply=%region_23.24.clone | all-reduce | flops 3072 | bytes 24576
  2100.2 53.1 %reduce-scatter.16.cloned.1.call-done = f32[48,32]{1,0:T(8,128)} async-done(((f32[1536,32]{1,0:T(8,128)}), f32[48,32]{1,0:T(8,128)}) %reduce-scatter.16.cloned.1.call-update) | async-done | bytes 6160
  2154.7 105.7 %reduce-scatter.10.cloned.1.call-done = f32[48,512]{1,0:T(8,128)} async-done(((f32[1536,512]{1,0:T(8,128)}), f32[48,512]{1,0:T(8,128)}) %reduce-scatter.10.cloned.1.call-update) | async-done | bytes 98320 | tf_op jit(solution)/shard_map/reduce_scatter | solution.py:355
  2260.5 107.3 %reduce-scatter.12.cloned.1.call-done = f32[48,512]{1,0:T(8,128)} async-done(((f32[1536,512]{1,0:T(8,128)}), f32[48,512]{1,0:T(8,128)}) %reduce-scatter.12.cloned.1.call-update) | async-done | bytes 98320 | tf_op jit(solution)/shard_map/reduce_scatter | solution.py:356
  2367.8 141.7 %reduce-scatter.8.cloned.1.call-done = f32[48,1536]{1,0:T(8,128)} async-done(((f32[1536,1536]{1,0:T(8,128)}), f32[48,1536]{1,0:T(8,128)}) %reduce-scatter.8.cloned.1.call-update) | async-done | bytes 294928 | tf_op jit(solution)/shard_map/reduce_scatter | solution.py:354
  2509.5 141.6 %reduce-scatter.14.cloned.1.call-done = f32[48,1536]{1,0:T(8,128)} async-done(((f32[1536,1536]{1,0:T(8,128)}), f32[48,1536]{1,0:T(8,128)}) %reduce-scatter.14.cloned.1.call-update) | async-done | bytes 294928 | tf_op jit(solution)/shard_map/reduce_scatter | solution.py:357
  (641 shorter events, 538.5 us)
Async XLA Ops:
  7.2 87.0 %all-gather.6.cloned.1.call-start = ((), (), s32[]{:S(2)}) async-start(), calls=%async_computation.9 | async-start | bytes 1622016 | tf_op jit(solution)/shard_map/all_gather | solution.py:128
  7.9 126.5 %all-gather.8.cloned.1.call-start = ((), (), s32[]{:S(2)}) async-start(), calls=%async_computation.10 | async-start | bytes 4866048 | tf_op jit(solution)/shard_map/all_gather | solution.py:127
  8.7 181.8 %all-gather.10.cloned.1.call-start = ((), (), s32[]{:S(2)}) async-start(), calls=%async_computation.11 | async-start | bytes 1622016 | tf_op jit(solution)/shard_map/all_gather | solution.py:129
  9.4 246.5 %all-gather.12.cloned.1.call-start = ((), (), s32[]{:S(2)}) async-start(), calls=%async_computation.12 | async-start | bytes 4866048 | tf_op jit(solution)/shard_map/all_gather | solution.py:130
  10.0 2143.4 %reduce-scatter.16.cloned.1.call-start = ((), (), s32[]{:S(2)}) async-start(), calls=%async_computation.17 | async-start | bytes 811008
  96.8 159.1 %copy-start.4 = (f32[512,1536]{1,0:T(8,128)S(1)}, f32[512,1536]{1,0:T(8,128)}, u32[]{:S(2)}) copy-start(f32[512,1536]{1,0:T(8,128)} %param.17) | copy-start | bytes 9437188
  258.4 61.3 %copy-start.42 = (f32[1536]{0:T(1024)}, f32[1536]{0:T(1024)S(1)}, u32[]{:S(2)}) copy-start(f32[1536]{0:T(1024)S(1)} %convert_element_type.440) | copy-start | bytes 18436 | tf_op jit(solution)/shard_map/while
  259.0 79.3 %copy-start.44 = (f32[1536]{0:T(1024)}, f32[1536]{0:T(1024)S(1)}, u32[]{:S(2)}) copy-start(f32[1536]{0:T(1024)S(1)} %convert_element_type.441) | copy-start | bytes 18436 | tf_op jit(solution)/shard_map/while
  267.1 61.1 %copy-start.32 = (f32[256,32]{0,1:T(8,128)}, f32[256,32]{0,1:T(8,128)S(1)}, u32[]{:S(2)}) copy-start(f32[256,32]{0,1:T(8,128)S(1)} %get-tuple-element.1206) | copy-start | bytes 98308 | tf_op jit(solution)/shard_map/while
  267.1 61.1 %copy-start.34 = (f32[256,32]{0,1:T(8,128)}, f32[256,32]{0,1:T(8,128)S(1)}, u32[]{:S(2)}) copy-start(f32[256,32]{0,1:T(8,128)S(1)} %get-tuple-element.1205) | copy-start | bytes 98308 | tf_op jit(solution)/shard_map/while
  347.4 158.9 %copy-start.67 = (bf16[1536,512]{1,0:T(8,128)(2,1)S(1)}, bf16[1536,512]{1,0:T(8,128)(2,1)}, u32[]{:S(2)}) copy-start(bf16[1536,512]{1,0:T(8,128)(2,1)} %get-tuple-element.1340) | copy-start | bytes 4718596 | tf_op jit(solution)/shard_map/while
  522.0 161.0 %all-to-all-start.1 = ((bf16[32,72,1536]{2,1,0:T(8,128)(2,1)}), bf16[32,72,1536]{2,1,0:T(8,128)(2,1)}, u32[]{:S(2)}, u32[]{:S(2)}) async-start(bf16[32,72,1536]{2,1,0:T(8,128)(2,1)} %bitcast.468), calls=%async_computation.1 | async-start | bytes 14155776 | tf_op jit(solution)/shard_map/while/body/eval_jaxpr/all_to_all | solution.py:145
  736.3 158.4 %copy-start.64 = (bf16[512,1536]{1,0:T(8,128)(2,1)S(1)}, bf16[512,1536]{1,0:T(8,128)(2,1)}, u32[]{:S(2)}) copy-start(bf16[512,1536]{1,0:T(8,128)(2,1)} %get-tuple-element.1338) | copy-start | bytes 4718596 | tf_op jit(solution)/shard_map/while
  921.4 161.1 %all-to-all-start.3 = ((bf16[32,72,1536]{2,1,0:T(8,128)(2,1)}), bf16[32,72,1536]{2,1,0:T(8,128)(2,1)}, u32[]{:S(2)}, u32[]{:S(2)}) async-start(bf16[32,72,1536]{2,1,0:T(8,128)(2,1)} %bitcast.467), calls=%async_computation.3 | async-start | bytes 14155776 | tf_op jit(solution)/shard_map/while/body/eval_jaxpr/all_to_all | solution.py:223
  1158.1 61.3 %copy-start.42 = (f32[1536]{0:T(1024)}, f32[1536]{0:T(1024)S(1)}, u32[]{:S(2)}) copy-start(f32[1536]{0:T(1024)S(1)} %convert_element_type.440) | copy-start | bytes 18436 | tf_op jit(solution)/shard_map/while
  1158.8 79.3 %copy-start.44 = (f32[1536]{0:T(1024)}, f32[1536]{0:T(1024)S(1)}, u32[]{:S(2)}) copy-start(f32[1536]{0:T(1024)S(1)} %convert_element_type.441) | copy-start | bytes 18436 | tf_op jit(solution)/shard_map/while
  1247.2 158.5 %copy-start.67 = (bf16[1536,512]{1,0:T(8,128)(2,1)S(1)}, bf16[1536,512]{1,0:T(8,128)(2,1)}, u32[]{:S(2)}) copy-start(bf16[1536,512]{1,0:T(8,128)(2,1)} %get-tuple-element.1340) | copy-start | bytes 4718596 | tf_op jit(solution)/shard_map/while
  1421.4 161.0 %all-to-all-start.1 = ((bf16[32,72,1536]{2,1,0:T(8,128)(2,1)}), bf16[32,72,1536]{2,1,0:T(8,128)(2,1)}, u32[]{:S(2)}, u32[]{:S(2)}) async-start(bf16[32,72,1536]{2,1,0:T(8,128)(2,1)} %bitcast.468), calls=%async_computation.1 | async-start | bytes 14155776 | tf_op jit(solution)/shard_map/while/body/eval_jaxpr/all_to_all | solution.py:145
  1635.6 158.4 %copy-start.64 = (bf16[512,1536]{1,0:T(8,128)(2,1)S(1)}, bf16[512,1536]{1,0:T(8,128)(2,1)}, u32[]{:S(2)}) copy-start(bf16[512,1536]{1,0:T(8,128)(2,1)} %get-tuple-element.1338) | copy-start | bytes 4718596 | tf_op jit(solution)/shard_map/while
  1820.8 161.4 %all-to-all-start.3 = ((bf16[32,72,1536]{2,1,0:T(8,128)(2,1)}), bf16[32,72,1536]{2,1,0:T(8,128)(2,1)}, u32[]{:S(2)}, u32[]{:S(2)}) async-start(bf16[32,72,1536]{2,1,0:T(8,128)(2,1)} %bitcast.467), calls=%async_computation.3 | async-start | bytes 14155776 | tf_op jit(solution)/shard_map/while/body/eval_jaxpr/all_to_all | solution.py:223
  2059.2 201.3 %reduce-scatter.10.cloned.1.call-start = ((), (), s32[]{:S(2)}) async-start(), calls=%async_computation.14 | async-start | bytes 3244032 | tf_op jit(solution)/shard_map/reduce_scatter | solution.py:355
  2059.7 308.0 %reduce-scatter.12.cloned.1.call-start = ((), (), s32[]{:S(2)}) async-start(), calls=%async_computation.15 | async-start | bytes 3244032 | tf_op jit(solution)/shard_map/reduce_scatter | solution.py:356
  2060.5 449.0 %reduce-scatter.8.cloned.1.call-start = ((), (), s32[]{:S(2)}) async-start(), calls=%async_computation.13 | async-start | bytes 9732096 | tf_op jit(solution)/shard_map/reduce_scatter | solution.py:354
  2061.2 589.9 %reduce-scatter.14.cloned.1.call-start = ((), (), s32[]{:S(2)}) async-start(), calls=%async_computation.16 | async-start | bytes 9732096 | tf_op jit(solution)/shard_map/reduce_scatter | solution.py:357
  (174 other events, 885.9 us)
Sparse Core Ops, SparseCore 0:
  10.8 57.9 all-gather.5
  71.8 62.6 all-gather.7
  137.3 53.1 all-gather.9
  193.2 62.5 all-gather.11
  2059.3 93.9 reduce-scatter.15
  2159.2 101.2 reduce-scatter.9
  2266.5 101.2 reduce-scatter.11
  2374.2 135.2 reduce-scatter.7
  2516.0 135.0 reduce-scatter.13
where the time goes:
time: 2670 us; the launch traced here: 2660 us
  waiting for transfers between devices  1280 us (48%)
  blocking collectives  753 us (28%)
  local copies, waits for them, and re-layouts  279 us (10%)
  matrix products  204 us (8%)
  other arithmetic  106 us (4%)
    all_to_all x2, blocking collectives, micro_step(): lax.all_to_all(outgoing, 'dp', split_axis=0, concat_axis=0, tiled=True)  317 us
    all_to_all x2, blocking collectives, micro_step(): lax.all_to_all(grad_outgoing, 'dp', split_axis=0, concat_axis=0, tiled=True)  317 us
    all_to_all x2, waiting for transfers between devices, run_expert(): lax.all_to_all(produced, 'dp', split_axis=0, concat_axis=0, tiled=True)  308 us
    all_to_all x2, waiting for transfers between devices, micro_step(): lax.all_to_all(grad_rows.reshape(experts, capacity, model_width), 'dp', s...  265 us
    reduce_scatter x1, waiting for transfers between devices, on_device(): lax.psum_scatter(totals[2], 'dp', scatter_dimension=0, tiled=True)  142 us
    reduce_scatter x1, waiting for transfers between devices, on_device(): lax.psum_scatter(totals[5], 'dp', scatter_dimension=0, tiled=True)  142 us
    reduce_scatter x1, waiting for transfers between devices, on_device(): lax.psum_scatter(totals[4], 'dp', scatter_dimension=0, tiled=True)  107 us
    reduce_scatter x1, waiting for transfers between devices, on_device(): lax.psum_scatter(totals[3], 'dp', scatter_dimension=0, tiled=True)  106 us
  transfers between devices with their start and end apart: 13, of which 12 were waited for; matrix products, arithmetic and copies ran while one was open for 2% of the time, Pallas kernels for 0%

commit v1 on v0

v1 whole, which is shorter than its diff:
```python
import jax
import jax.numpy as jnp
from jax import lax
from jax.sharding import PartitionSpec as P

H = 24
KVH = 8
HD = 64


res_scale = 0.22
attn_scale = 0.015625
norm_eps = 1e-06
rope_base = 10000.0


def rotary_tables(length, head_size):
    half_size = head_size // 2
    frequency = rope_base ** (-(jnp.arange(half_size, dtype=jnp.float32) * 2.0) / head_size)
    angles = jnp.arange(length, dtype=jnp.float32)[:, None] * frequency[None, :]
    return (jnp.cos(angles)[:, None, :], jnp.sin(angles)[:, None, :])


def rotate(operand, cos_table, sin_table):
    half_size = operand.shape[-1] // 2
    lower_half = operand[..., :half_size]
    upper_half = operand[..., half_size:]
    return jnp.concatenate(
        [
            lower_half * cos_table - upper_half * sin_table,
            upper_half * cos_table + lower_half * sin_table,
        ],
        axis=-1,
    )


def unrotate(operand, cos_table, sin_table):
    half_size = operand.shape[-1] // 2
    lower_half = operand[..., :half_size]
    upper_half = operand[..., half_size:]
    return jnp.concatenate(
        [
            lower_half * cos_table + upper_half * sin_table,
            upper_half * cos_table - lower_half * sin_table,
        ],
        axis=-1,
    )


LINES = 4


def norm_backward(grad_normed, source, recip, gain):
    scaled_grad = grad_normed * gain
    grad_source = recip * scaled_grad - source * (recip * recip * recip) * jnp.mean(
        scaled_grad * source, axis=1, keepdims=True
    )
    return (grad_source, jnp.sum(grad_normed * source * recip, axis=0))


def masked_gates(logits, routed):
    peak = jnp.max(jnp.where(routed, logits, -jnp.inf), axis=-2, keepdims=True)
    shifted = jnp.where(routed, jnp.exp(jnp.minimum(logits - peak, 0.0)), 0.0)
    return shifted / jnp.sum(shifted, axis=-2, keepdims=True)


def on_device(
    hidden,
    cotangent,
    block_ids,
    routes,
    pair_rank,
    norm1_gain,
    norm2_gain,
    w_query,
    w_key,
    w_value,
    w_out,
    w_router,
    w_gate,
    w_up,
    w_down,
):
    micro_count, seq_len = block_ids.shape
    model_width = hidden.shape[1]
    top_count = routes.shape[1]
    devices = lax.axis_size("dp")
    experts = w_router.shape[1]
    plane = devices // LINES
    capacity = (9 * seq_len * top_count + 8 * experts - 1) // (8 * experts)
    groups = H // KVH
    query_width = w_query.shape[1]
    kv_width = w_key.shape[1]
    qkv_width = query_width + 2 * kv_width
    cos_table, sin_table = rotary_tables(seq_len, HD)
    gate_local = w_gate[0]
    up_local = w_up[0]
    down_local = w_down[0]
    bf16 = jnp.bfloat16
    f32 = jnp.float32
    here = lax.axis_index("dp") // plane
    plane_groups = [[line * plane + i for i in range(plane)] for line in range(LINES)]

    def line_shift(step):
        return [
            (i, ((i // plane + step) % LINES) * plane + i % plane) for i in range(devices)
        ]

    def spread(block):
        return [block] + [
            lax.ppermute(block, "dp", line_shift(step)) for step in range(1, LINES)
        ]

    def give_back(blocks):
        return [blocks[0]] + [
            lax.ppermute(blocks[step], "dp", line_shift(-step)) for step in range(1, LINES)
        ]

    def exchange(block):
        return lax.all_to_all(
            block, "dp", split_axis=0, concat_axis=0, tiled=True, axis_index_groups=plane_groups
        )

    small = jnp.concatenate([norm1_gain[:, None], norm2_gain[:, None], w_router], axis=1)
    pad = -small.shape[1] % 128
    first = lax.all_gather(
        jnp.concatenate(
            [w_query, w_key, w_value, jnp.pad(small, ((0, 0), (0, pad)))], axis=1
        ),
        "dp",
        axis=0,
        tiled=True,
    )
    out_proj = lax.all_gather(w_out, "dp", axis=0, tiled=True)
    qkv_proj = first[:, :qkv_width]
    gain_first = first[:, qkv_width].astype(f32)
    gain_second = first[:, qkv_width + 1].astype(f32)
    router = first[:, qkv_width + 2 : qkv_width + 2 + experts]

    labels = jnp.arange(experts, dtype=jnp.int32)
    route_seq = routes.reshape(micro_count, seq_len, top_count)
    rank_seq = pair_rank.reshape(micro_count, seq_len, top_count)
    named = route_seq[:, None, :, :] == labels[None, :, None, None]
    routed = jnp.any(named, axis=3)
    rank_of = jnp.where(
        routed, jnp.sum(jnp.where(named, rank_seq[:, None], 0), axis=3), seq_len * top_count
    )
    ahead = jnp.sum((rank_of[:, :, :, None] < rank_of[:, :, None, :]).astype(jnp.int32), axis=2)
    slot_of = jnp.where(routed, ahead, -1)
    slot_blocks = jnp.stack(spread(slot_of))
    slots_here = lax.dynamic_slice_in_dim(slot_blocks, here * plane, plane, axis=2)
    places = jnp.arange(capacity, dtype=jnp.int32)
    picks = [
        (slots_here[:, micro, :, None, :] == places[None, None, :, None]).astype(bf16)
        for micro in range(micro_count)
    ]

    cotan_seq = cotangent.reshape(micro_count, seq_len, model_width)
    hidden_seq = hidden.reshape(micro_count, seq_len, model_width)

    def dispatch(micro, blocks):
        rows = jnp.einsum(
            "ject,jtd->ejcd", picks[micro], jnp.stack(blocks), preferred_element_type=f32
        ).astype(bf16)
        return exchange(rows.reshape(plane, LINES * capacity, model_width)).reshape(
            -1, model_width
        )

    def combine(micro, rows):
        arrived = exchange(rows.reshape(plane, LINES * capacity, model_width)).reshape(
            plane, LINES, capacity, model_width
        )
        sums = jnp.einsum(
            "ject,ejcd->jtd", picks[micro], arrived, preferred_element_type=f32
        ).astype(bf16)
        back = give_back([sums[step] for step in range(LINES)])
        total = back[0].astype(f32)
        for part in back[1:]:
            total = total + part.astype(f32)
        return total

    grad_arrived = [
        dispatch(micro, spread((res_scale * cotan_seq[micro]).astype(bf16)))
        for micro in range(micro_count)
    ]

    kept = []
    for micro in range(micro_count):
        tokens_in = hidden_seq[micro]
        blocks = block_ids[micro]
        recip_first = lax.rsqrt(jnp.mean(tokens_in * tokens_in, axis=1, keepdims=True) + norm_eps)
        normed_in = (tokens_in * recip_first * gain_first).astype(bf16)
        projected = jnp.dot(normed_in, qkv_proj, preferred_element_type=f32)
        queries = projected[:, :query_width].reshape(seq_len, H, HD)
        keys_raw = projected[:, query_width : query_width + kv_width].reshape(seq_len, KVH, HD)
        values = projected[:, query_width + kv_width :].astype(bf16).reshape(seq_len, KVH, HD)
        query_rot = (
            rotate(queries, cos_table, sin_table).astype(bf16).reshape(seq_len, KVH, groups, HD)
        )
        key_rot = rotate(keys_raw, cos_table, sin_table).astype(bf16)
        visible = blocks[None, :] <= blocks[:, None]
        scores = attn_scale * jnp.einsum(
            "qhgd,khd->hgqk", query_rot, key_rot, preferred_element_type=f32
        )
        scores = jnp.where(visible, scores, -1e30)
        row_peak = jnp.max(scores, axis=3, keepdims=True)
        shifted_exp = jnp.exp(scores - row_peak)
        row_total = jnp.sum(shifted_exp, axis=3, keepdims=True)
        attn_probs = shifted_exp / row_total
        log_total = row_peak + jnp.log(row_total)
        mixture = (
            jnp.einsum(
                "hgqk,khd->qhgd", attn_probs.astype(bf16), values, preferred_element_type=f32
            )
            .reshape(seq_len, H * HD)
            .astype(bf16)
        )
        attn_out = jnp.dot(mixture, out_proj, preferred_element_type=f32)
        residual = tokens_in + res_scale * attn_out
        recip_second = lax.rsqrt(jnp.mean(residual * residual, axis=1, keepdims=True) + norm_eps)
        normed_mid = (residual * recip_second * gain_second).astype(bf16)
        kept.append(
            (
                recip_first,
                normed_in,
                values,
                query_rot,
                key_rot,
                visible,
                log_total,
                mixture,
                residual,
                recip_second,
                normed_mid,
            )
        )

    returned = []
    grad_down_w = grad_gate_w = grad_up_w = 0.0
    for micro in range(micro_count):
        normed_mid = kept[micro][-1]
        blocks = spread(normed_mid)
        logits = jnp.einsum(
            "de,jtd->jet", router, jnp.stack(blocks), preferred_element_type=f32
        )
        gates = masked_gates(logits, slot_blocks[:, micro] >= 0)
        gates_here = lax.dynamic_slice_in_dim(gates, here * plane, plane, axis=1)
        slot_gates = jnp.sum(
            jnp.where(picks[micro] > 0, gates_here[:, :, None, :], 0.0), axis=3
        ).transpose(1, 0, 2)
        gate_rows = exchange(slot_gates.reshape(plane, LINES * capacity)).reshape(-1, 1)
        arrived = dispatch(micro, blocks)
        blend_rows = grad_arrived[micro]
        gate_pre = jnp.dot(arrived, gate_local, preferred_element_type=f32)
        up_pre = jnp.dot(arrived, up_local, preferred_element_type=f32)
        logistic = jax.nn.sigmoid(gate_pre)
        silu = gate_pre * logistic
        hidden_act = (silu * up_pre).astype(bf16)
        produced = jnp.dot(hidden_act, down_local, preferred_element_type=f32)
        pair_grads = jnp.sum(produced * blend_rows.astype(f32), axis=1)
        scaled = (gate_rows * produced).astype(bf16)
        grad_produced = (gate_rows * blend_rows.astype(f32)).astype(bf16)
        grad_inner = jnp.einsum(
            "rd,fd->rf", grad_produced, down_local, preferred_element_type=f32
        )
        grad_gate_pre = (
            grad_inner * up_pre * (logistic * (1.0 + gate_pre * (1.0 - logistic)))
        ).astype(bf16)
        grad_up_pre = (grad_inner * silu).astype(bf16)
        grad_rows = jnp.einsum(
            "rf,df->rd", grad_gate_pre, gate_local, preferred_element_type=f32
        )
        grad_rows = grad_rows + jnp.einsum(
            "rf,df->rd", grad_up_pre, up_local, preferred_element_type=f32
        )
        pair_back = exchange(pair_grads.reshape(plane, LINES * capacity)).reshape(
            plane, LINES, capacity
        )
        token_grads = jnp.sum(
            jnp.where(picks[micro] > 0, pair_back.transpose(1, 0, 2)[:, :, :, None], 0.0), axis=2
        )
        pair_blocks = give_back([token_grads[step] for step in range(LINES)])
        grad_mid_sum = combine(micro, grad_rows.astype(bf16))
        blended = combine(micro, scaled)
        returned.append((grad_mid_sum, blended, pair_blocks, gates[0]))
        grad_down_w = grad_down_w + jnp.einsum(
            "rf,rd->fd", hidden_act, grad_produced, preferred_element_type=f32
        )
        grad_gate_w = grad_gate_w + jnp.einsum(
            "rd,rf->df", arrived, grad_gate_pre, preferred_element_type=f32
        )
        grad_up_w = grad_up_w + jnp.einsum(
            "rd,rf->df", arrived, grad_up_pre, preferred_element_type=f32
        )

    outputs = []
    token_grads_out = []
    gain_first_w = gain_second_w = qkv_w = out_w = router_w = 0.0
    for micro in range(micro_count):
        (
            recip_first,
            normed_in,
            values,
            query_rot,
            key_rot,
            visible,
            log_total,
            mixture,
            residual,
            recip_second,
            normed_mid,
        ) = kept[micro]
        grad_mid_sum, blended, pair_blocks, gates = returned[micro]
        tokens_in = hidden_seq[micro]
        cotan_in = cotan_seq[micro]
        outputs.append(residual + blended * res_scale)
        pair_grads = jnp.zeros((experts, seq_len), f32)
        for step in range(LINES):
            pair_grads = lax.dynamic_update_slice_in_dim(
                pair_grads, pair_blocks[step], ((here + step) % LINES) * plane, axis=0
            )
        grad_logits = (
            gates * (pair_grads - jnp.sum(gates * pair_grads, axis=0, keepdims=True))
        ).astype(bf16)
        router_w = router_w + jnp.einsum(
            "td,et->de", normed_mid, grad_logits, preferred_element_type=f32
        )
        grad_mid = grad_mid_sum + jnp.einsum(
            "et,de->td", grad_logits, router, preferred_element_type=f32
        )
        grad_residual, grad_gain = norm_backward(grad_mid, residual, recip_second, gain_second)
        gain_second_w = gain_second_w + grad_gain
        grad_residual = cotan_in + grad_residual
        grad_attn = (res_scale * grad_residual).astype(bf16)
        out_w = out_w + jnp.einsum("tc,td->cd", mixture, grad_attn, preferred_element_type=f32)
        grad_mixture = (
            jnp.einsum("td,cd->tc", grad_attn, out_proj, preferred_element_type=f32)
            .astype(bf16)
            .reshape(seq_len, KVH, groups, HD)
        )
        scores_again = attn_scale * jnp.einsum(
            "qhgd,khd->hgqk", query_rot, key_rot, preferred_element_type=f32
        )
        scores_again = jnp.where(visible, scores_again, -1e30)
        probs_again = jnp.exp(scores_again - log_total)
        grad_probs = jnp.einsum("qhgd,khd->hgqk", grad_mixture, values, preferred_element_type=f32)
        grad_values = (
            jnp.einsum(
                "hgqk,qhgd->khd", probs_again.astype(bf16), grad_mixture, preferred_element_type=f32
            )
            .astype(bf16)
            .reshape(seq_len, KVH * HD)
        )
        grad_scores = (
            probs_again * (grad_probs - jnp.sum(probs_again * grad_probs, axis=3, keepdims=True))
        ).astype(bf16)
        grad_query_rot = attn_scale * jnp.einsum(
            "hgqk,khd->qhgd", grad_scores, key_rot, preferred_element_type=f32
        )
        grad_key_rot = attn_scale * jnp.einsum(
            "hgqk,qhgd->khd", grad_scores, query_rot, preferred_element_type=f32
        )
        grad_queries = (
            unrotate(grad_query_rot.reshape(seq_len, H, HD), cos_table, sin_table)
            .astype(bf16)
            .reshape(seq_len, H * HD)
        )
        grad_keys = (
            unrotate(grad_key_rot, cos_table, sin_table).astype(bf16).reshape(seq_len, KVH * HD)
        )
        grad_qkv = jnp.concatenate([grad_queries, grad_keys, grad_values], axis=1)
        qkv_w = qkv_w + jnp.einsum("td,tc->dc", normed_in, grad_qkv, preferred_element_type=f32)
        grad_normed = jnp.einsum("tc,dc->td", grad_qkv, qkv_proj, preferred_element_type=f32)
        grad_source, grad_gain = norm_backward(grad_normed, tokens_in, recip_first, gain_first)
        gain_first_w = gain_first_w + grad_gain
        token_grads_out.append(grad_residual + grad_source)

    small_w = jnp.concatenate([gain_second_w[:, None], router_w], axis=1)
    small_w = jnp.pad(small_w, ((0, 0), (0, -small_w.shape[1] % 128)))
    out_sum = lax.psum_scatter(
        jnp.concatenate([out_w, small_w], axis=1).astype(bf16),
        "dp",
        scatter_dimension=0,
        tiled=True,
    ).astype(f32)
    qkv_sum = lax.psum_scatter(
        jnp.concatenate([qkv_w, jnp.pad(gain_first_w[:, None], ((0, 0), (0, 127)))], axis=1).astype(
            bf16
        ),
        "dp",
        scatter_dimension=0,
        tiled=True,
    ).astype(f32)
    return (
        jnp.concatenate(outputs, axis=0),
        jnp.concatenate(token_grads_out, axis=0),
        qkv_sum[:, qkv_width],
        out_sum[:, model_width],
        qkv_sum[:, :query_width],
        qkv_sum[:, query_width : query_width + kv_width],
        qkv_sum[:, query_width + kv_width : qkv_width],
        out_sum[:, :model_width],
        out_sum[:, model_width + 1 : model_width + 1 + experts],
        grad_gate_w[None],
        grad_up_w[None],
        grad_down_w[None],
    )


def solution(mesh):
    return jax.shard_map(
        on_device,
        mesh=mesh,
        in_specs=(
            P("dp", None),
            P("dp", None),
            P("dp", None),
            P("dp", None),
            P("dp", None),
            P("dp"),
            P("dp"),
            P("dp", None),
            P("dp", None),
            P("dp", None),
            P("dp", None),
            P("dp", None),
            P("dp", None, None),
            P("dp", None, None),
            P("dp", None, None),
        ),
        out_specs=(
            P("dp", None),
            P("dp", None),
            P("dp"),
            P("dp"),
            P("dp", None),
            P("dp", None),
            P("dp", None),
            P("dp", None),
            P("dp", None),
            P("dp", None, None),
            P("dp", None, None),
            P("dp", None, None),
        ),
        check_vma=False,
    )
```

time: 2670 us -> 1630 us (0.61)
  blocking collectives: 753 us -> 15.9 us
  waiting for transfers between devices: 1280 us -> 1010 us
  local copies, waits for them, and re-layouts: 279 us -> 90.6 us
  starting transfers between devices: 16.1 us -> 96.5 us
  matrix products: 204 us -> 283 us
    all_to_all x4 -> x2, blocking collectives: 634 us -> 15.9 us  [exchange(): lax.all_to_all(block, 'dp', split_axis=0, concat_axis=0, tiled=True, axis...]
    ppermute x0 -> x33, waiting for transfers between devices: none -> 423 us  [the longest x15 264 us: spread(): lax.ppermute(block, 'dp', line_shift(step))]
    reduce_scatter x4 -> x1, waiting for transfers between devices: 496 us -> 131 us  [on_device(): lax.psum_scatter(jnp.concatenate([qkv_w, jnp.pad(gain_first_w[:, None], (...]
    all_to_all x4 -> x10, waiting for transfers between devices: 573 us -> 346 us  [exchange(): lax.all_to_all(block, 'dp', split_axis=0, concat_axis=0, tiled=True, axis...]
    gather x12 -> x0, local copies, waits for them, and re-layouts: 171 us -> none  [the longest x2 37 us: micro_step(): grad_pairs[slot_pair].reshape(experts, capacity, model_width)]
    dot_general x62 -> x56, matrix products: 204 us -> 283 us  [the longest x4 22.6 us: combine(): jnp.einsum('ject,ejcd->jtd', picks[micro], arrived, preferred_element_typ...]
    unnamed x2 -> x0, blocking collectives: 74.1 us -> none
    all_gather x4 -> x2, waiting for transfers between devices: 152 us -> 95.7 us  [the longest x1 65.7 us: on_device(): lax.all_gather(jnp.concatenate([w_query, w_key, w_value, jnp.pad(small, (...]
  transfers between devices with their start and end apart: 13 -> 47, of which waited for: 12 -> 30; matrix products, arithmetic and copies ran while one was open for 2% -> 18% of each run, Pallas kernels for 0% -> 0%
where the time goes in v1:
time: 1630 us; the launch traced here: 1620 us
  waiting for transfers between devices  1010 us (62%)
  matrix products  283 us (17%)
  other arithmetic  104 us (6%)
  starting transfers between devices  96.5 us (6%)
  local copies, waits for them, and re-layouts  90.6 us (6%)
    all_to_all x10, waiting for transfers between devices, exchange(): lax.all_to_all(block, 'dp', split_axis=0, concat_axis=0, tiled=True, axis...  346 us
    ppermute x15, waiting for transfers between devices, spread(): lax.ppermute(block, 'dp', line_shift(step))  264 us
    ppermute x18, waiting for transfers between devices, give_back(): lax.ppermute(blocks[step], 'dp', line_shift(-step))  159 us
    reduce_scatter x1, waiting for transfers between devices, on_device(): lax.psum_scatter(jnp.concatenate([qkv_w, jnp.pad(gain_first_w[:, None], (...  131 us
    all_gather x1, waiting for transfers between devices, on_device(): lax.all_gather(jnp.concatenate([w_query, w_key, w_value, jnp.pad(small, (...  65.7 us
    all_to_all x10, starting transfers between devices, exchange(): lax.all_to_all(block, 'dp', split_axis=0, concat_axis=0, tiled=True, axis...  46.7 us
    unnamed x282, local copies, waits for them, and re-layouts  35.5 us
    convert_element_type x4, other arithmetic, on_device(): grad_produced = (gate_rows * blend_rows.astype(f32)).astype(bf16)  33.9 us
  transfers between devices with their start and end apart: 47, of which 30 were waited for; matrix products, arithmetic and copies ran while one was open for 18% of the time, Pallas kernels for 0%

profile of v1, /device:TPU:0, one launch (start us, length us, event | category | flops | bytes accessed | tf_op | source)
XLA Modules:
  0.0 1619.4 jit_solution(5683930262644730436)
XLA Ops:
  28.3 65.7 %all-gather.3.cloned.1.call-done = bf16[1536,2688]{1,0:T(8,128)(2,1)} async-done(((bf16[48,2688]{1,0:T(8,128)(2,1)}), bf16[1536,2688]{1,0:T(8,128)(2,1)}) %all-gather.3.cloned.1.call-update) | async-done | bytes 8257552 | tf_op jit(solution)/shard_map/all_gather | solution.py:126
  129.2 29.9 %all-gather.5.cloned.1.call-done = bf16[1536,1536]{1,0:T(8,128)(2,1)} async-done(((bf16[48,1536]{1,0:T(8,128)(2,1)}), bf16[1536,1536]{1,0:T(8,128)(2,1)}) %all-gather.5.cloned.1.call-update) | async-done | bytes 4718608 | tf_op jit(solution)/shard_map/all_gather | solution.py:134
  171.8 13.7 collective-permute-done.5
  185.4 51.4 %collective-permute-done.4 = bf16[256,1536]{1,0:T(8,128)(2,1)} collective-permute-done((bf16[256,1536]{1,0:T(8,128)(2,1)}, bf16[256,1536]{1,0:T(8,128)(2,1)}, u32[]{:S(2)}, u32[]{:S(2)}) %collective-permute-start.4) | collective-permute-done | bytes 786464 | tf_op jit(solution)/shard_map/ppermute | solution.py:111
  255.8 16.4 %collective-permute-done.17 = bf16[256,1536]{1,0:T(8,128)(2,1)S(1)} collective-permute-done((bf16[256,1536]{1,0:T(8,128)(2,1)S(1)}, bf16[256,1536]{1,0:T(8,128)(2,1)S(1)}, u32[]{:S(2)}, u32[]{:S(2)}) %collective-permute-start.17) | collective-permute-done | bytes 786464 | tf_op jit(solution)/shard_map/ppermute | solution.py:111
  272.2 50.2 %collective-permute-done.16 = bf16[256,1536]{1,0:T(8,128)(2,1)S(1)} collective-permute-done((bf16[256,1536]{1,0:T(8,128)(2,1)S(1)}, bf16[256,1536]{1,0:T(8,128)(2,1)S(1)}, u32[]{:S(2)}, u32[]{:S(2)}) %collective-permute-start.16) | collective-permute-done | bytes 786464 | tf_op jit(solution)/shard_map/ppermute | solution.py:111
  357.2 56.5 %all-to-all-done.6 = bf16[8,288,1536]{2,1,0:T(8,128)(2,1)} async-done(((bf16[8,288,1536]{2,1,0:T(8,128)(2,1)}), bf16[8,288,1536]{2,1,0:T(8,128)(2,1)}, u32[]{:S(2)}, u32[]{:S(2)}) %all-to-all-start.6) | async-done | bytes 7077920 | tf_op jit(solution)/shard_map/all_to_all | solution.py:120
  454.2 12.7 fusion.8
  501.8 50.0 %all-to-all-done.2 = bf16[8,288,1536]{2,1,0:T(8,128)(2,1)} async-done(((bf16[8,288,1536]{2,1,0:T(8,128)(2,1)}), bf16[8,288,1536]{2,1,0:T(8,128)(2,1)}, u32[]{:S(2)}, u32[]{:S(2)}) %all-to-all-start.2) | async-done | bytes 7077920 | tf_op jit(solution)/shard_map/all_to_all | solution.py:120
  588.2 48.6 %all-to-all-done.7 = bf16[8,288,1536]{2,1,0:T(8,128)(2,1)} async-done(((bf16[8,288,1536]{2,1,0:T(8,128)(2,1)}), bf16[8,288,1536]{2,1,0:T(8,128)(2,1)}, u32[]{:S(2)}, u32[]{:S(2)}) %all-to-all-start.7) | async-done | bytes 7077920 | tf_op jit(solution)/shard_map/all_to_all | solution.py:120
  649.0 32.1 %collective-permute-done.7 = bf16[256,1536]{1,0:T(8,128)(2,1)S(1)} collective-permute-done((bf16[256,1536]{1,0:T(8,128)(2,1)S(1)}, bf16[256,1536]{1,0:T(8,128)(2,1)S(1)}, u32[]{:S(2)}, u32[]{:S(2)}) %collective-permute-start.7) | collective-permute-done | bytes 786464 | tf_op jit(solution)/shard_map/ppermute | solution.py:116
  698.0 46.4 %collective-permute-done.19 = bf16[256,1536]{1,0:T(8,128)(2,1)S(1)} collective-permute-done((bf16[256,1536]{1,0:T(8,128)(2,1)S(1)}, bf16[256,1536]{1,0:T(8,128)(2,1)S(1)}, u32[]{:S(2)}, u32[]{:S(2)}) %collective-permute-start.19) | collective-permute-done | bytes 786464 | tf_op jit(solution)/shard_map/ppermute | solution.py:116
  752.2 18.7 %collective-permute-done.11 = bf16[256,1536]{1,0:T(8,128)(2,1)S(1)} collective-permute-done((bf16[256,1536]{1,0:T(8,128)(2,1)S(1)}, bf16[256,1536]{1,0:T(8,128)(2,1)S(1)}, u32[]{:S(2)}, u32[]{:S(2)}) %collective-permute-start.11) | collective-permute-done | bytes 786464 | tf_op jit(solution)/shard_map/ppermute | solution.py:111
  770.9 47.1 %collective-permute-done.10 = bf16[256,1536]{1,0:T(8,128)(2,1)S(1)} collective-permute-done((bf16[256,1536]{1,0:T(8,128)(2,1)S(1)}, bf16[256,1536]{1,0:T(8,128)(2,1)S(1)}, u32[]{:S(2)}, u32[]{:S(2)}) %collective-permute-start.10) | collective-permute-done | bytes 786464 | tf_op jit(solution)/shard_map/ppermute | solution.py:111
  834.3 14.7 collective-permute-done.26
  849.0 52.2 %collective-permute-done.25 = bf16[256,1536]{1,0:T(8,128)(2,1)S(1)} collective-permute-done((bf16[256,1536]{1,0:T(8,128)(2,1)}, bf16[256,1536]{1,0:T(8,128)(2,1)S(1)}, u32[]{:S(2)}, u32[]{:S(2)}) %collective-permute-start.25) | collective-permute-done | bytes 786464 | tf_op jit(solution)/shard_map/ppermute | solution.py:111
  934.9 58.8 %all-to-all-done.9 = bf16[8,288,1536]{2,1,0:T(8,128)(2,1)} async-done(((bf16[8,288,1536]{2,1,0:T(8,128)(2,1)}), bf16[8,288,1536]{2,1,0:T(8,128)(2,1)}, u32[]{:S(2)}, u32[]{:S(2)}) %all-to-all-start.9) | async-done | bytes 7077920 | tf_op jit(solution)/shard_map/all_to_all | solution.py:120
  1055.5 12.8 fusion.5
  1068.3 67.1 %all-to-all-done.10 = bf16[8,288,1536]{2,1,0:T(8,128)(2,1)} async-done(((bf16[8,288,1536]{2,1,0:T(8,128)(2,1)}), bf16[8,288,1536]{2,1,0:T(8,128)(2,1)}, u32[]{:S(2)}, u32[]{:S(2)}) %all-to-all-start.10) | async-done | bytes 7077920 | tf_op jit(solution)/shard_map/all_to_all | solution.py:120
  1164.6 55.8 %all-to-all-done.5 = bf16[8,288,1536]{2,1,0:T(8,128)(2,1)} async-done(((bf16[8,288,1536]{2,1,0:T(8,128)(2,1)}), bf16[8,288,1536]{2,1,0:T(8,128)(2,1)}, u32[]{:S(2)}, u32[]{:S(2)}) %all-to-all-start.5) | async-done | bytes 7077920 | tf_op jit(solution)/shard_map/all_to_all | solution.py:120
  1235.3 26.1 %collective-permute-done.12 = bf16[256,1536]{1,0:T(8,128)(2,1)S(1)} collective-permute-done((bf16[256,1536]{1,0:T(8,128)(2,1)S(1)}, bf16[256,1536]{1,0:T(8,128)(2,1)S(1)}, u32[]{:S(2)}, u32[]{:S(2)}) %collective-permute-start.12) | collective-permute-done | bytes 786464 | tf_op jit(solution)/shard_map/ppermute | solution.py:116
  1266.7 30.5 %collective-permute-done.13 = bf16[256,1536]{1,0:T(8,128)(2,1)S(1)} collective-permute-done((bf16[256,1536]{1,0:T(8,128)(2,1)S(1)}, bf16[256,1536]{1,0:T(8,128)(2,1)S(1)}, u32[]{:S(2)}, u32[]{:S(2)}) %collective-permute-start.13) | collective-permute-done | bytes 786464 | tf_op jit(solution)/shard_map/ppermute | solution.py:116
  1455.2 16.6 %reduce-scatter.7.cloned.1.call-done = bf16[48,1664]{1,0:T(8,128)(2,1)} async-done(((bf16[1536,1664]{1,0:T(8,128)(2,1)}), bf16[48,1664]{1,0:T(8,128)(2,1)}) %reduce-scatter.7.cloned.1.call-update) | async-done | bytes 159760
  1476.9 130.9 %reduce-scatter.5.cloned.1.call-done = bf16[48,2688]{1,0:T(8,128)(2,1)} async-done(((bf16[1536,2688]{1,0:T(8,128)(2,1)}), bf16[48,2688]{1,0:T(8,128)(2,1)}) %reduce-scatter.5.cloned.1.call-update) | async-done | bytes 258064 | tf_op jit(solution)/shard_map/reduce_scatter | solution.py:386
  (555 shorter events, 598.2 us)
Async XLA Ops:
  7.2 86.8 %all-gather.3.cloned.1.call-start = ((), (), s32[]{:S(2)}) async-start(), calls=%async_computation.14 | async-start | bytes 8515584 | tf_op jit(solution)/shard_map/all_gather | solution.py:126
  11.5 147.7 %all-gather.5.cloned.1.call-start = ((), (), s32[]{:S(2)}) async-start(), calls=%async_computation.15 | async-start | bytes 4866048 | tf_op jit(solution)/shard_map/all_gather | solution.py:134
  18.5 149.8 %collective-permute-start.2 = (s32[2,32,256]{2,1,0:T(8,128)}, s32[2,32,256]{2,1,0:T(8,128)}, u32[]{:S(2)}, u32[]{:S(2)}) collective-permute-start(s32[2,32,256]{2,1,0:T(8,128)} %broadcast_select_fusion), channel_id=1, source_target_pairs={{0,24},{1,25},{2,26},{3,27},{4,28},{5,29},{6,30},{7,31},{8,0},{9,1... | collective-permute-start | bytes 196616 | tf_op jit(solution)/shard_map/ppermute | solution.py:111
  23.5 145.7 %collective-permute-start.1 = (s32[2,32,256]{2,1,0:T(8,128)}, s32[2,32,256]{2,1,0:T(8,128)}, u32[]{:S(2)}, u32[]{:S(2)}) collective-permute-start(s32[2,32,256]{2,1,0:T(8,128)} %broadcast_select_fusion), channel_id=1, source_target_pairs={{0,16},{1,17},{2,18},{3,19},{4,20},{5,21},{6,22},{7,23},{8,24},{9,... | collective-permute-start | bytes 196616 | tf_op jit(solution)/shard_map/ppermute | solution.py:111
  23.6 145.7 %collective-permute-start = (s32[2,32,256]{2,1,0:T(8,128)}, s32[2,32,256]{2,1,0:T(8,128)}, u32[]{:S(2)}, u32[]{:S(2)}) collective-permute-start(s32[2,32,256]{2,1,0:T(8,128)} %broadcast_select_fusion), channel_id=1, source_target_pairs={{0,8},{1,9},{2,10},{3,11},{4,12},{5,13},{6,14},{7,15},{8,16},{9,17... | collective-permute-start | bytes 196616 | tf_op jit(solution)/shard_map/ppermute | solution.py:111
  167.1 69.8 %collective-permute-start.4 = (bf16[256,1536]{1,0:T(8,128)(2,1)}, bf16[256,1536]{1,0:T(8,128)(2,1)}, u32[]{:S(2)}, u32[]{:S(2)}) collective-permute-start(bf16[256,1536]{1,0:T(8,128)(2,1)} %multiply_convert_fusion.14), channel_id=1, source_target_pairs={{0,16},{1,17},{2,18},{3,19},{4,20},{5,21},{6,22},{7,23},{8,24},{9,... | collective-permute-start | bytes 2359304 | tf_op jit(solution)/shard_map/ppermute | solution.py:111
  244.1 84.8 %all-to-all-start.1 = ((bf16[8,288,1536]{2,1,0:T(8,128)(2,1)}), bf16[8,288,1536]{2,1,0:T(8,128)(2,1)}, u32[]{:S(2)}, u32[]{:S(2)}) async-start(bf16[8,288,1536]{2,1,0:T(8,128)(2,1)} %bitcast.426), calls=%async_computation.1 | async-start | bytes 14155776 | tf_op jit(solution)/shard_map/all_to_all | solution.py:120
  252.1 70.4 %collective-permute-start.16 = (bf16[256,1536]{1,0:T(8,128)(2,1)S(1)}, bf16[256,1536]{1,0:T(8,128)(2,1)S(1)}, u32[]{:S(2)}, u32[]{:S(2)}) collective-permute-start(bf16[256,1536]{1,0:T(8,128)(2,1)S(1)} %get-tuple-element.107), channel_id=1, source_target_pairs={{0,16},{1,17},{2,18},{3,19},{4,20},{5,21},{6,22},{7,23},{8,24},{9,... | collective-permute-start | bytes 2359304 | tf_op jit(solution)/shard_map/ppermute | solution.py:111
  328.9 84.8 %all-to-all-start.6 = ((bf16[8,288,1536]{2,1,0:T(8,128)(2,1)}), bf16[8,288,1536]{2,1,0:T(8,128)(2,1)}, u32[]{:S(2)}, u32[]{:S(2)}) async-start(bf16[8,288,1536]{2,1,0:T(8,128)(2,1)} %bitcast.428), calls=%async_computation.6 | async-start | bytes 14155776 | tf_op jit(solution)/shard_map/all_to_all | solution.py:120
  467.0 84.8 %all-to-all-start.2 = ((bf16[8,288,1536]{2,1,0:T(8,128)(2,1)}), bf16[8,288,1536]{2,1,0:T(8,128)(2,1)}, u32[]{:S(2)}, u32[]{:S(2)}) async-start(bf16[8,288,1536]{2,1,0:T(8,128)(2,1)} %bitcast.430), calls=%async_computation.2 | async-start | bytes 14155776 | tf_op jit(solution)/shard_map/all_to_all | solution.py:120
  551.8 85.0 %all-to-all-start.7 = ((bf16[8,288,1536]{2,1,0:T(8,128)(2,1)}), bf16[8,288,1536]{2,1,0:T(8,128)(2,1)}, u32[]{:S(2)}, u32[]{:S(2)}) async-start(bf16[8,288,1536]{2,1,0:T(8,128)(2,1)} %bitcast.435), calls=%async_computation.7 | async-start | bytes 14155776 | tf_op jit(solution)/shard_map/all_to_all | solution.py:120
  572.7 70.0 %collective-permute-start.23 = (f32[8,256]{1,0:T(8,128)S(1)}, f32[8,256]{1,0:T(8,128)S(1)}, u32[]{:S(2)}, u32[]{:S(2)}) collective-permute-start(f32[8,256]{1,0:T(8,128)S(1)} %get-tuple-element.144), channel_id=1, source_target_pairs={{0,8},{1,9},{2,10},{3,11},{4,12},{5,13},{6,14},{7,15},{8,16},{9,17... | collective-permute-start | bytes 24584 | tf_op jit(solution)/shard_map/ppermute | solution.py:116
  572.7 72.6 %collective-permute-start.22 = (f32[8,256]{1,0:T(8,128)S(1)}, f32[8,256]{1,0:T(8,128)S(1)}, u32[]{:S(2)}, u32[]{:S(2)}) collective-permute-start(f32[8,256]{1,0:T(8,128)S(1)} %get-tuple-element.145), channel_id=1, source_target_pairs={{0,16},{1,17},{2,18},{3,19},{4,20},{5,21},{6,22},{7,23},{8,24},{9,... | collective-permute-start | bytes 24584 | tf_op jit(solution)/shard_map/ppermute | solution.py:116
  574.5 71.3 %collective-permute-start.21 = (f32[8,256]{1,0:T(8,128)S(1)}, f32[8,256]{1,0:T(8,128)S(1)}, u32[]{:S(2)}, u32[]{:S(2)}) collective-permute-start(f32[8,256]{1,0:T(8,128)S(1)} %get-tuple-element.146), channel_id=1, source_target_pairs={{0,24},{1,25},{2,26},{3,27},{4,28},{5,29},{6,30},{7,31},{8,0},{9,1... | collective-permute-start | bytes 24584 | tf_op jit(solution)/shard_map/ppermute | solution.py:116
  647.8 96.7 %collective-permute-start.19 = (bf16[256,1536]{1,0:T(8,128)(2,1)S(1)}, bf16[256,1536]{1,0:T(8,128)(2,1)S(1)}, u32[]{:S(2)}, u32[]{:S(2)}) collective-permute-start(bf16[256,1536]{1,0:T(8,128)(2,1)S(1)} %get-tuple-element.100), channel_id=1, source_target_pairs={{0,16},{1,17},{2,18},{3,19},{4,20},{5,21},{6,22},{7,23},{8,24},{9,... | collective-permute-start | bytes 2359304 | tf_op jit(solution)/shard_map/ppermute | solution.py:116
  823.9 85.0 %all-to-all-start.4 = ((bf16[8,288,1536]{2,1,0:T(8,128)(2,1)}), bf16[8,288,1536]{2,1,0:T(8,128)(2,1)}, u32[]{:S(2)}, u32[]{:S(2)}) async-start(bf16[8,288,1536]{2,1,0:T(8,128)(2,1)} %bitcast.427), calls=%async_computation.4 | async-start | bytes 14155776 | tf_op jit(solution)/shard_map/all_to_all | solution.py:120
  828.8 72.4 %collective-permute-start.25 = (bf16[256,1536]{1,0:T(8,128)(2,1)}, bf16[256,1536]{1,0:T(8,128)(2,1)S(1)}, u32[]{:S(2)}, u32[]{:S(2)}) collective-permute-start(bf16[256,1536]{1,0:T(8,128)(2,1)} %get-tuple-element.108), channel_id=1, source_target_pairs={{0,16},{1,17},{2,18},{3,19},{4,20},{5,21},{6,22},{7,23},{8,24},{9,... | collective-permute-start | bytes 2359304 | tf_op jit(solution)/shard_map/ppermute | solution.py:111
  908.9 84.8 %all-to-all-start.9 = ((bf16[8,288,1536]{2,1,0:T(8,128)(2,1)}), bf16[8,288,1536]{2,1,0:T(8,128)(2,1)}, u32[]{:S(2)}, u32[]{:S(2)}) async-start(bf16[8,288,1536]{2,1,0:T(8,128)(2,1)} %bitcast.429), calls=%async_computation.9 | async-start | bytes 14155776 | tf_op jit(solution)/shard_map/all_to_all | solution.py:120
  1050.6 84.8 %all-to-all-start.10 = ((bf16[8,288,1536]{2,1,0:T(8,128)(2,1)}), bf16[8,288,1536]{2,1,0:T(8,128)(2,1)}, u32[]{:S(2)}, u32[]{:S(2)}) async-start(bf16[8,288,1536]{2,1,0:T(8,128)(2,1)} %bitcast.436), calls=%async_computation.10 | async-start | bytes 14155776 | tf_op jit(solution)/shard_map/all_to_all | solution.py:120
  1135.4 85.0 %all-to-all-start.5 = ((bf16[8,288,1536]{2,1,0:T(8,128)(2,1)}), bf16[8,288,1536]{2,1,0:T(8,128)(2,1)}, u32[]{:S(2)}, u32[]{:S(2)}) async-start(bf16[8,288,1536]{2,1,0:T(8,128)(2,1)} %bitcast.425), calls=%async_computation.5 | async-start | bytes 14155776 | tf_op jit(solution)/shard_map/all_to_all | solution.py:120
  1140.4 331.5 %reduce-scatter.7.cloned.1.call-start = ((), (), s32[]{:S(2)}) async-start(), calls=%async_computation.17 | async-start | bytes 5271552
  1162.1 70.0 %collective-permute-start.29 = (bf16[256,1536]{1,0:T(8,128)(2,1)}, bf16[256,1536]{1,0:T(8,128)(2,1)}, u32[]{:S(2)}, u32[]{:S(2)}) collective-permute-start(bf16[256,1536]{1,0:T(8,128)(2,1)} %get-tuple-element.102), channel_id=1, source_target_pairs={{0,8},{1,9},{2,10},{3,11},{4,12},{5,13},{6,14},{7,15},{8,16},{9,17... | collective-permute-start | bytes 2359304 | tf_op jit(solution)/shard_map/ppermute | solution.py:116
  1162.1 70.0 %collective-permute-start.28 = (bf16[256,1536]{1,0:T(8,128)(2,1)}, bf16[256,1536]{1,0:T(8,128)(2,1)}, u32[]{:S(2)}, u32[]{:S(2)}) collective-permute-start(bf16[256,1536]{1,0:T(8,128)(2,1)} %get-tuple-element.103), channel_id=1, source_target_pairs={{0,16},{1,17},{2,18},{3,19},{4,20},{5,21},{6,22},{7,23},{8,24},{9,... | collective-permute-start | bytes 2359304 | tf_op jit(solution)/shard_map/ppermute | solution.py:116
  1362.0 245.7 %reduce-scatter.5.cloned.1.call-start = ((), (), s32[]{:S(2)}) async-start(), calls=%async_computation.16 | async-start | bytes 8515584 | tf_op jit(solution)/shard_map/reduce_scatter | solution.py:386
  (161 other events, 4327.7 us)
Sparse Core Ops, SparseCore 0:
  11.6 82.3 all-gather.2
  96.9 62.2 all-gather.4
  1362.1 109.7 reduce-scatter.6
  1477.6 130.0 reduce-scatter.4

commit v2 on v1

--- a/solution.py
+++ b/solution.py
@@ -1,6 +1,7 @@
 import jax
 import jax.numpy as jnp
 from jax import lax
+from jax.experimental import pallas as pl
 from jax.sharding import PartitionSpec as P
 
 H = 24
@@ -62,6 +63,112 @@
     peak = jnp.max(jnp.where(routed, logits, -jnp.inf), axis=-2, keepdims=True)
     shifted = jnp.where(routed, jnp.exp(jnp.minimum(logits - peak, 0.0)), 0.0)
     return shifted / jnp.sum(shifted, axis=-2, keepdims=True)
+
+
+def expert_kernel(
+    rows_ref,
+    blend_ref,
+    gates_ref,
+    gate_ref,
+    up_ref,
+    down_ref,
+    grads_ref,
+    scaled_ref,
+    pairs_ref,
+    gate_sum_ref,
+    up_sum_ref,
+    down_sum_ref,
+):
+    f32 = jnp.float32
+    bf16 = jnp.bfloat16
+
+    def product(left, right, left_axis, right_axis):
+        return lax.dot_general(
+            left, right, (((left_axis,), (right_axis,)), ((), ())), preferred_element_type=f32
+        )
+
+    @pl.when(pl.program_id(0) == 0)
+    def _():
+        gate_sum_ref[...] = jnp.zeros_like(gate_sum_ref)
+        up_sum_ref[...] = jnp.zeros_like(up_sum_ref)
+        down_sum_ref[...] = jnp.zeros_like(down_sum_ref)
+
+    rows = rows_ref[...]
+    gates = gates_ref[...]
+    blend = blend_ref[...].astype(f32)
+    gate_pre = product(rows, gate_ref[...], 1, 0)
+    up_pre = product(rows, up_ref[...], 1, 0)
+    logistic = 1.0 / (1.0 + jnp.exp(-gate_pre))
+    silu = gate_pre * logistic
+    hidden_act = (silu * up_pre).astype(bf16)
+    produced = product(hidden_act, down_ref[...], 1, 0)
+    pairs_ref[...] = jnp.sum(produced * blend, axis=1, keepdims=True)
+    scaled_ref[...] = (gates * produced).astype(bf16)
+    grad_produced = (gates * blend).astype(bf16)
+    grad_inner = product(grad_produced, down_ref[...], 1, 1)
+    grad_gate_pre = (
+        grad_inner * up_pre * (logistic * (1.0 + gate_pre * (1.0 - logistic)))
+    ).astype(bf16)
+    grad_up_pre = (grad_inner * silu).astype(bf16)
+    grads_ref[...] = (
+        product(grad_gate_pre, gate_ref[...], 1, 1) + product(grad_up_pre, up_ref[...], 1, 1)
+    ).astype(bf16)
+    down_sum_ref[...] += product(hidden_act, grad_produced, 0, 0)
+    gate_sum_ref[...] += product(rows, grad_gate_pre, 0, 0)
+    up_sum_ref[...] += product(rows, grad_up_pre, 0, 0)
+
+
+def run_experts(rows, blend, gates, gate_local, up_local, down_local):
+    count, width = rows.shape
+    ff_width = gate_local.shape[1]
+    block = next(b for b in (384, 256, 128, count) if count % b == 0)
+    f32 = jnp.float32
+    wide = pl.BlockSpec((block, width), lambda i: (i, 0))
+    thin = pl.BlockSpec((block, 1), lambda i: (i, 0))
+    inner = pl.BlockSpec((width, ff_width), lambda i: (0, 0))
+    outer = pl.BlockSpec((ff_width, width), lambda i: (0, 0))
+    return pl.pallas_call(
+        expert_kernel,
+        grid=(count // block,),
+        in_specs=[wide, wide, thin, inner, inner, outer],
+        out_specs=[wide, wide, thin, inner, inner, outer],
+        out_shape=[
+            jax.ShapeDtypeStruct((count, width), rows.dtype),
+            jax.ShapeDtypeStruct((count, width), rows.dtype),
+            jax.ShapeDtypeStruct((count, 1), f32),
+            jax.ShapeDtypeStruct((width, ff_width), f32),
+            jax.ShapeDtypeStruct((width, ff_width), f32),
+            jax.ShapeDtypeStruct((ff_width, width), f32),
+        ],
+        cost_estimate=pl.CostEstimate(flops=1000, bytes_accessed=1000, transcendentals=0),
+        name="experts",
+    )(rows, blend, gates, gate_local, up_local, down_local)
+
+
+def build_kernel(slots_ref, *refs):
+    out_ref = refs[-1]
+    plane, lines, capacity, width = out_ref.shape
+    for line in range(lines):
+        slots = slots_ref[line]
+        places = lax.broadcasted_iota(jnp.int32, (plane, capacity, slots.shape[1]), 1)
+        picks = jnp.where(slots[:, None, :] == places, 1.0, 0.0)
+        rows = jnp.dot(
+            picks.reshape(plane * capacity, slots.shape[1]).astype(jnp.bfloat16),
+            refs[line][...],
+            preferred_element_type=jnp.float32,
+        )
+        out_ref[:, line] = rows.reshape(plane, capacity, width).astype(jnp.bfloat16)
+
+
+def build_rows(slots, blocks, capacity):
+    lines, plane, unused = slots.shape
+    width = blocks[0].shape[1]
+    return pl.pallas_call(
+        build_kernel,
+        out_shape=jax.ShapeDtypeStruct((plane, lines, capacity, width), blocks[0].dtype),
+        cost_estimate=pl.CostEstimate(flops=1000, bytes_accessed=1000, transcendentals=0),
+        name="build_rows",
+    )(slots, *blocks)
 
 
 def on_device(
@@ -158,36 +265,35 @@
     cotan_seq = cotangent.reshape(micro_count, seq_len, model_width)
     hidden_seq = hidden.reshape(micro_count, seq_len, model_width)
 
-    def dispatch(micro, blocks):
-        rows = jnp.einsum(
-            "ject,jtd->ejcd", picks[micro], jnp.stack(blocks), preferred_element_type=f32
+    def hold(value, *after):
+        return lax.optimization_barrier((value, after))[0]
+
+    def build(micro, blocks):
+        if capacity % 8 == 0:
+            rows = build_rows(slots_here[:, micro], blocks, capacity)
+        else:
+            rows = jnp.einsum(
+                "ject,jtd->ejcd", picks[micro], jnp.stack(blocks), preferred_element_type=f32
+            ).astype(bf16)
+        return rows.reshape(plane, LINES * capacity, model_width)
+
+    def sums_of(micro, arrived):
+        sums = jnp.einsum(
+            "ject,ejcd->jtd",
+            picks[micro],
+            arrived.reshape(plane, LINES, capacity, model_width),
+            preferred_element_type=f32,
         ).astype(bf16)
-        return exchange(rows.reshape(plane, LINES * capacity, model_width)).reshape(
-            -1, model_width
-        )
-
-    def combine(micro, rows):
-        arrived = exchange(rows.reshape(plane, LINES * capacity, model_width)).reshape(
-            plane, LINES, capacity, model_width
-        )
-        sums = jnp.einsum(
-            "ject,ejcd->jtd", picks[micro], arrived, preferred_element_type=f32
-        ).astype(bf16)
-        back = give_back([sums[step] for step in range(LINES)])
-        total = back[0].astype(f32)
-        for part in back[1:]:
+        return give_back([sums[step] for step in range(LINES)])
+
+    def total_of(parts):
+        total = parts[0].astype(f32)
+        for part in parts[1:]:
             total = total + part.astype(f32)
         return total
 
-    grad_arrived = [
-        dispatch(micro, spread((res_scale * cotan_seq[micro]).astype(bf16)))
-        for micro in range(micro_count)
-    ]
-
-    kept = []
-    for micro in range(micro_count):
-        tokens_in = hidden_seq[micro]
-        blocks = block_ids[micro]
+    def attend(unused, inputs):
+        tokens_in, blocks = inputs
         recip_first = lax.rsqrt(jnp.mean(tokens_in * tokens_in, axis=1, keepdims=True) + norm_eps)
         normed_in = (tokens_in * recip_first * gain_first).astype(bf16)
         projected = jnp.dot(normed_in, qkv_proj, preferred_element_type=f32)
@@ -215,105 +321,76 @@
             .reshape(seq_len, H * HD)
             .astype(bf16)
         )
-        attn_out = jnp.dot(mixture, out_proj, preferred_element_type=f32)
+        return (
+            unused,
+            dict(
+                recip_first=recip_first,
+                normed_in=normed_in,
+                values=values,
+                query_rot=query_rot,
+                key_rot=key_rot,
+                log_total=log_total,
+                mixture=mixture,
+            ),
+        )
+
+    def after_attention(kept, tokens_in):
+        attn_out = jnp.dot(kept["mixture"], out_proj, preferred_element_type=f32)
         residual = tokens_in + res_scale * attn_out
         recip_second = lax.rsqrt(jnp.mean(residual * residual, axis=1, keepdims=True) + norm_eps)
         normed_mid = (residual * recip_second * gain_second).astype(bf16)
-        kept.append(
-            (
-                recip_first,
-                normed_in,
-                values,
-                query_rot,
-                key_rot,
-                visible,
-                log_total,
-                mixture,
-                residual,
-                recip_second,
-                normed_mid,
-            )
-        )
-
-    returned = []
-    grad_down_w = grad_gate_w = grad_up_w = 0.0
-    for micro in range(micro_count):
-        normed_mid = kept[micro][-1]
-        blocks = spread(normed_mid)
-        logits = jnp.einsum(
-            "de,jtd->jet", router, jnp.stack(blocks), preferred_element_type=f32
-        )
+        return dict(kept, residual=residual, recip_second=recip_second, normed_mid=normed_mid)
+
+    def gates_of(micro, blocks):
+        logits = jnp.einsum("de,jtd->jet", router, jnp.stack(blocks), preferred_element_type=f32)
         gates = masked_gates(logits, slot_blocks[:, micro] >= 0)
         gates_here = lax.dynamic_slice_in_dim(gates, here * plane, plane, axis=1)
         slot_gates = jnp.sum(
             jnp.where(picks[micro] > 0, gates_here[:, :, None, :], 0.0), axis=3
         ).transpose(1, 0, 2)
-        gate_rows = exchange(slot_gates.reshape(plane, LINES * capacity)).reshape(-1, 1)
-        arrived = dispatch(micro, blocks)
-        blend_rows = grad_arrived[micro]
-        gate_pre = jnp.dot(arrived, gate_local, preferred_element_type=f32)
-        up_pre = jnp.dot(arrived, up_local, preferred_element_type=f32)
-        logistic = jax.nn.sigmoid(gate_pre)
-        silu = gate_pre * logistic
-        hidden_act = (silu * up_pre).astype(bf16)
-        produced = jnp.dot(hidden_act, down_local, preferred_element_type=f32)
-        pair_grads = jnp.sum(produced * blend_rows.astype(f32), axis=1)
-        scaled = (gate_rows * produced).astype(bf16)
-        grad_produced = (gate_rows * blend_rows.astype(f32)).astype(bf16)
-        grad_inner = jnp.einsum(
-            "rd,fd->rf", grad_produced, down_local, preferred_element_type=f32
-        )
-        grad_gate_pre = (
-            grad_inner * up_pre * (logistic * (1.0 + gate_pre * (1.0 - logistic)))
-        ).astype(bf16)
-        grad_up_pre = (grad_inner * silu).astype(bf16)
-        grad_rows = jnp.einsum(
-            "rf,df->rd", grad_gate_pre, gate_local, preferred_element_type=f32
-        )
-        grad_rows = grad_rows + jnp.einsum(
-            "rf,df->rd", grad_up_pre, up_local, preferred_element_type=f32
-        )
-        pair_back = exchange(pair_grads.reshape(plane, LINES * capacity)).reshape(
-            plane, LINES, capacity
-        )
-        token_grads = jnp.sum(
-            jnp.where(picks[micro] > 0, pair_back.transpose(1, 0, 2)[:, :, :, None], 0.0), axis=2
-        )
-        pair_blocks = give_back([token_grads[step] for step in range(LINES)])
-        grad_mid_sum = combine(micro, grad_rows.astype(bf16))
-        blended = combine(micro, scaled)
-        returned.append((grad_mid_sum, blended, pair_blocks, gates[0]))
-        grad_down_w = grad_down_w + jnp.einsum(
-            "rf,rd->fd", hidden_act, grad_produced, preferred_element_type=f32
-        )
-        grad_gate_w = grad_gate_w + jnp.einsum(
-            "rd,rf->df", arrived, grad_gate_pre, preferred_element_type=f32
-        )
-        grad_up_w = grad_up_w + jnp.einsum(
-            "rd,rf->df", arrived, grad_up_pre, preferred_element_type=f32
-        )
-
-    outputs = []
-    token_grads_out = []
-    gain_first_w = gain_second_w = qkv_w = out_w = router_w = 0.0
-    for micro in range(micro_count):
-        (
-            recip_first,
-            normed_in,
-            values,
-            query_rot,
-            key_rot,
-            visible,
-            log_total,
-            mixture,
-            residual,
-            recip_second,
-            normed_mid,
-        ) = kept[micro]
-        grad_mid_sum, blended, pair_blocks, gates = returned[micro]
+        return gates[0], slot_gates.reshape(plane, LINES * capacity)
+
+    def run_expert(mid, blend, gate_rows):
+        grads, scaled, pair_grads, *weights = run_experts(
+            mid.reshape(-1, model_width),
+            blend.reshape(-1, model_width),
+            gate_rows.reshape(-1, 1),
+            gate_local,
+            up_local,
+            down_local,
+        )
+        return (
+            grads.reshape(mid.shape),
+            scaled.reshape(mid.shape),
+            pair_grads.reshape(mid.shape[:2]),
+            weights,
+        )
+
+    def pairs_home(pair_back):
+        token_grads = [
+            jnp.sum(
+                jnp.where(
+                    picks[m] > 0,
+                    pair_back[:, m]
+                    .reshape(plane, LINES, capacity)
+                    .transpose(1, 0, 2)[:, :, :, None],
+                    0.0,
+                ),
+                axis=2,
+            )
+            for m in range(micro_count)
+        ]
+        both = jnp.stack(token_grads, axis=1)
+        return give_back([both[step] for step in range(LINES)])
+
+    def attend_back(micro, grad_mid_sum, pair_blocks, gates, kept):
         tokens_in = hidden_seq[micro]
         cotan_in = cotan_seq[micro]
-        outputs.append(residual + blended * res_scale)
+        recip_first, normed_in, values = kept["recip_first"], kept["normed_in"], kept["values"]
+        query_rot, key_rot = kept["query_rot"], kept["key_rot"]
+        visible = block_ids[micro][None, :] <= block_ids[micro][:, None]
+        log_total, mixture, residual = kept["log_total"], kept["mixture"], kept["residual"]
+        recip_second, normed_mid = kept["recip_second"], kept["normed_mid"]
         pair_grads = jnp.zeros((experts, seq_len), f32)
         for step in range(LINES):
             pair_grads = lax.dynamic_update_slice_in_dim(
@@ -322,17 +399,17 @@
         grad_logits = (
             gates * (pair_grads - jnp.sum(gates * pair_grads, axis=0, keepdims=True))
         ).astype(bf16)
-        router_w = router_w + jnp.einsum(
+        router_w = jnp.einsum(
             "td,et->de", normed_mid, grad_logits, preferred_element_type=f32
         )
         grad_mid = grad_mid_sum + jnp.einsum(
             "et,de->td", grad_logits, router, preferred_element_type=f32
         )
         grad_residual, grad_gain = norm_backward(grad_mid, residual, recip_second, gain_second)
-        gain_second_w = gain_second_w + grad_gain
+        gain_second_w = grad_gain
         grad_residual = cotan_in + grad_residual
         grad_attn = (res_scale * grad_residual).astype(bf16)
-        out_w = out_w + jnp.einsum("tc,td->cd", mixture, grad_attn, preferred_element_type=f32)
+        out_w = jnp.einsum("tc,td->cd", mixture, grad_attn, preferred_element_type=f32)
         grad_mixture = (
             jnp.einsum("td,cd->tc", grad_attn, out_proj, preferred_element_type=f32)
             .astype(bf16)
@@ -369,11 +446,71 @@
             unrotate(grad_key_rot, cos_table, sin_table).astype(bf16).reshape(seq_len, KVH * HD)
         )
         grad_qkv = jnp.concatenate([grad_queries, grad_keys, grad_values], axis=1)
-        qkv_w = qkv_w + jnp.einsum("td,tc->dc", normed_in, grad_qkv, preferred_element_type=f32)
+        qkv_w = jnp.einsum("td,tc->dc", normed_in, grad_qkv, preferred_element_type=f32)
         grad_normed = jnp.einsum("tc,dc->td", grad_qkv, qkv_proj, preferred_element_type=f32)
         grad_source, grad_gain = norm_backward(grad_normed, tokens_in, recip_first, gain_first)
-        gain_first_w = gain_first_w + grad_gain
-        token_grads_out.append(grad_residual + grad_source)
+        return (
+            grad_residual + grad_source,
+            out_w,
+            qkv_w,
+            grad_gain,
+            gain_second_w,
+            router_w,
+        )
+
+    blend_blocks = [spread((res_scale * cotan_seq[m]).astype(bf16)) for m in range(2)]
+    blend0 = build(0, blend_blocks[0])
+    moved_blend0 = exchange(blend0)
+    unused, kept_both = lax.scan(
+        attend, jnp.zeros((), f32), (hold(hidden_seq, blend0), block_ids)
+    )
+    blend1 = build(1, hold(blend_blocks[1], kept_both["mixture"]))
+    moved_blend1 = exchange(hold(blend1, moved_blend0))
+    kept0, kept1 = (
+        after_attention({name: part[m] for name, part in kept_both.items()}, hidden_seq[m])
+        for m in range(2)
+    )
+    blocks0 = spread(kept0["normed_mid"])
+    blocks1 = spread(kept1["normed_mid"])
+    moved_mid0 = exchange(hold(build(0, blocks0), moved_blend1))
+    gates0, slot_gates0 = gates_of(0, blocks0)
+    gates1, slot_gates1 = gates_of(1, blocks1)
+    gate_rows = exchange(
+        hold(jnp.stack([slot_gates0, slot_gates1], axis=1), moved_mid0)
+    )
+    mid1 = build(1, blocks1)
+    moved_mid1 = exchange(hold(mid1, gate_rows))
+    grads0, scaled0, pairs0, weights0 = run_expert(
+        hold(moved_mid0, mid1), moved_blend0, gate_rows[:, 0]
+    )
+    moved_grads0 = exchange(hold(grads0, moved_mid1))
+    grads1, scaled1, pairs1, weights1 = run_expert(moved_mid1, moved_blend1, gate_rows[:, 1])
+    pair_back = exchange(hold(jnp.stack([pairs0, pairs1], axis=1), moved_grads0))
+    moved_grads1 = exchange(hold(grads1, pair_back))
+    pair_blocks = pairs_home(pair_back)
+    back0 = sums_of(0, moved_grads0)
+    moved_scaled0 = exchange(hold(scaled0, moved_grads1, back0))
+    back1 = sums_of(1, moved_grads1)
+    result0 = attend_back(
+        0, total_of(back0), [block[0] for block in pair_blocks], gates0, kept0
+    )
+    moved_scaled1 = exchange(hold(scaled1, moved_scaled0, back1, result0))
+    blend_back0 = sums_of(0, moved_scaled0)
+    result1 = attend_back(
+        1, hold(total_of(back1), result0), [block[1] for block in pair_blocks], gates1, kept1
+    )
+    blend_back1 = sums_of(1, moved_scaled1)
+    outputs = [
+        kept0["residual"] + res_scale * total_of(blend_back0),
+        kept1["residual"] + res_scale * total_of(blend_back1),
+    ]
+    token_grads_out = [result0[0], result1[0]]
+    out_w, qkv_w, gain_first_w, gain_second_w, router_w = (
+        a + b for a, b in zip(result0[1:], result1[1:], strict=True)
+    )
+    grad_gate_w, grad_up_w, grad_down_w = (
+        a + b for a, b in zip(weights0, weights1, strict=True)
+    )
 
     small_w = jnp.concatenate([gain_second_w[:, None], router_w], axis=1)
     small_w = jnp.pad(small_w, ((0, 0), (0, -small_w.shape[1] % 128)))

time: 1630 us -> 1370 us (0.84)
  waiting for transfers between devices: 1010 us -> 786 us
  matrix products: 283 us -> 141 us
  Pallas kernels: 0 us -> 120 us
  starting transfers between devices: 96.5 us -> 149 us
  other arithmetic: 104 us -> 79.1 us
  local copies, waits for them, and re-layouts: 90.6 us -> 69.3 us
    dot_general x56 -> x36, matrix products: 283 us -> 141 us  [the longest x4 22.8 us: sums_of(): jnp.einsum('ject,ejcd->jtd', picks[micro], arrived.reshape(plane, LINES,...]
    all_to_all x10 -> x9, waiting for transfers between devices: 346 us -> 214 us  [exchange(): lax.all_to_all(block, 'dp', split_axis=0, concat_axis=0, tiled=True, axis...]
    pallas_call x0 -> x6, Pallas kernels: none -> 120 us  [the longest x2 93.2 us: run_experts(): pl.pallas_call(expert_kernel, grid=(count // block,), in_specs=[wide, wid...]
    ppermute x15, waiting for transfers between devices: 264 us -> 196 us  [spread(): lax.ppermute(block, 'dp', line_shift(step))]
    all_gather x1, waiting for transfers between devices: 65.7 us -> 7.39 us  [on_device(): lax.all_gather(jnp.concatenate([w_query, w_key, w_value, jnp.pad(small, (...]
    ppermute x18 -> x15, starting transfers between devices: 28.4 us -> 65.6 us  [give_back(): lax.ppermute(blocks[step], 'dp', line_shift(-step))]
    convert_element_type x10 -> x6, other arithmetic: 49 us -> 14.6 us  [the longest x2 9.55 us: attend_back(): grad_scores = (probs_again * (grad_probs - jnp.sum(probs_again * grad_pro...]
    ppermute x18 -> x15, waiting for transfers between devices: 159 us -> 190 us  [give_back(): lax.ppermute(blocks[step], 'dp', line_shift(-step))]
  transfers between devices with their start and end apart: 47 -> 43, of which waited for: 30 -> 27; matrix products, arithmetic and copies ran while one was open for 18% -> 17% of each run, Pallas kernels for 0% -> 9%
where the time goes in v2:
time: 1370 us
  waiting for transfers between devices  786 us (57%)
  starting transfers between devices  149 us (11%)
  matrix products  141 us (10%)
  Pallas kernels  120 us (9%)
  other arithmetic  79.1 us (6%)
  local copies, waits for them, and re-layouts  69.3 us (5%)
  between operations  15.6 us (1%)
    all_to_all x9, waiting for transfers between devices, exchange(): lax.all_to_all(block, 'dp', split_axis=0, concat_axis=0, tiled=True, axis...  214 us
    ppermute x15, waiting for transfers between devices, spread(): lax.ppermute(block, 'dp', line_shift(step))  196 us
    ppermute x15, waiting for transfers between devices, give_back(): lax.ppermute(blocks[step], 'dp', line_shift(-step))  190 us
    reduce_scatter x1, waiting for transfers between devices, on_device(): lax.psum_scatter(jnp.concatenate([qkv_w, jnp.pad(gain_first_w[:, None], (...  133 us
    pallas_call x2, Pallas kernels, run_experts(): pl.pallas_call(expert_kernel, grid=(count // block,), in_specs=[wide, wid...  93.2 us
    ppermute x15, starting transfers between devices, give_back(): lax.ppermute(blocks[step], 'dp', line_shift(-step))  65.6 us
    all_to_all x9, starting transfers between devices, exchange(): lax.all_to_all(block, 'dp', split_axis=0, concat_axis=0, tiled=True, axis...  43.4 us
    ppermute x15, starting transfers between devices, spread(): lax.ppermute(block, 'dp', line_shift(step))  40 us
  transfers between devices with their start and end apart: 43, of which 27 were waited for; matrix products, arithmetic and copies ran while one was open for 17% of the time, Pallas kernels for 9%

profile of v2, /device:TPU:0, one launch (start us, length us, event | category | flops | bytes accessed | tf_op | source)
XLA Modules:
  0.0 1368.5 jit_solution(4766713671626713987)
XLA Ops:
  26.2 58.5 %collective-permute-done = s32[2,32,256]{2,1,0:T(8,128)S(1)} collective-permute-done((s32[2,32,256]{2,1,0:T(8,128)S(1)}, s32[2,32,256]{2,1,0:T(8,128)S(1)}, u32[]{:S(2)}, u32[]{:S(2)}) %collective-permute-start) | collective-permute-done | bytes 65568 | tf_op jit(solution)/shard_map/ppermute | solution.py:218
  84.7 36.2 %collective-permute-done.1 = s32[2,32,256]{2,1,0:T(8,128)S(1)} collective-permute-done((s32[2,32,256]{2,1,0:T(8,128)S(1)}, s32[2,32,256]{2,1,0:T(8,128)S(1)}, u32[]{:S(2)}, u32[]{:S(2)}) %collective-permute-start.1) | collective-permute-done | bytes 65568 | tf_op jit(solution)/shard_map/ppermute | solution.py:218
  164.0 51.0 %while.25 = (s32[]{:T(128)}, bf16[2,256,8,64]{1,3,2,0:T(8,128)(2,1)}, f32[2,8,3,256,1]{3,2,1,4,0:T(4,128)}, bf16[2,256,1536]{1,2,0:T(8,128)(2,1)}, bf16[2,256,15...) while((s32[]{:T(128)}, ...), condition=%wide.region_7.8_spmd.clone.clone.clone, body=%wide.region_3.7_spmd.clone.clone.clone.sunk | while | flops 2444691712 | bytes 154750128 | solution.py:464
  221.7 15.8 %all-to-all-done = bf16[8,288,1536]{2,1,0:T(8,128)(2,1)} async-done(((bf16[8,288,1536]{2,1,0:T(8,128)(2,1)}), bf16[8,288,1536]{2,1,0:T(8,128)(2,1)}, u32[]{:S(2)}, u32[]{:S(2)}) %all-to-all-start) | async-done | bytes 7077920 | tf_op jit(solution)/shard_map/all_to_all | solution.py:227
  262.6 17.8 %collective-permute-done.6.refs_1_ = bf16[256,1536]{1,0:T(8,128)(2,1)S(1)} collective-permute-done((bf16[256,1536]{1,0:T(8,128)(2,1)S(1)}, bf16[256,1536]{1,0:T(8,128)(2,1)S(1)}, u32[]{:S(2)}, u32[]{:S(2)}) %collective-permute-start.6) | collective-permute-done | bytes 786464 | tf_op jit(solution)/shard_map/ppermute | solution.py:218
  280.5 33.0 %collective-permute-done.7.refs_2_ = bf16[256,1536]{1,0:T(8,128)(2,1)S(1)} collective-permute-done((bf16[256,1536]{1,0:T(8,128)(2,1)S(1)}, bf16[256,1536]{1,0:T(8,128)(2,1)S(1)}, u32[]{:S(2)}, u32[]{:S(2)}) %collective-permute-start.7) | collective-permute-done | bytes 786464 | tf_op jit(solution)/shard_map/ppermute | solution.py:218
  327.6 15.1 %collective-permute-start.12 = (bf16[256,1536]{1,0:T(8,128)(2,1)}, bf16[256,1536]{1,0:T(8,128)(2,1)S(1)}, u32[]{:S(2)}, u32[]{:S(2)}) collective-permute-start(bf16[256,1536]{1,0:T(8,128)(2,1)} %get-tuple-element.492.refs_0_), channel_id=1, source_target_pairs={{0,8},{1,9},{2,10},{3,11},{4,12},{5,13},{6,14},{7,15},{8,16},{9,17... | collective-permute-start | bytes 2359304 | tf_op jit(solution)/shard_map/ppermute | solution.py:218
  348.6 13.7 collective-permute-done.12.refs_1_
  362.3 33.4 %collective-permute-done.13.refs_2_ = bf16[256,1536]{1,0:T(8,128)(2,1)S(1)} collective-permute-done((bf16[256,1536]{1,0:T(8,128)(2,1)}, bf16[256,1536]{1,0:T(8,128)(2,1)S(1)}, u32[]{:S(2)}, u32[]{:S(2)}) %collective-permute-start.13) | collective-permute-done | bytes 786464 | tf_op jit(solution)/shard_map/ppermute | solution.py:218
  425.6 46.6 %experts.2 = (bf16[2304,1536]{1,0:T(8,128)(2,1)}, bf16[2304,1536]{1,0:T(8,128)(2,1)}, f32[2304,1]{1,0:T(8,128)}, f32[1536,512]{1,0:T(8,128)}, f32[1536,512]{1,0:T(8,128)}, /*index=5*/f32[512,1536]{1,0:T(8,128)}) custom-call(bf16[2304,1536]{1,0:T(8,128)(2,1)} %bitcast.19.rows_ref, bf16[2304,1536]{1,0:T(8,128)(2,1)} %bitcast.20.blend_ref, ...), custom_call_target="tpu_custom_call" | custom-call | flops 1000 | bytes 1000 | tf_op jit(solution)/shard_map/experts/pallas_call | solution.py:130
  472.2 31.3 %all-to-all-done.4 = bf16[8,288,1536]{2,1,0:T(8,128)(2,1)} async-done(((bf16[8,288,1536]{2,1,0:T(8,128)(2,1)}), bf16[8,288,1536]{2,1,0:T(8,128)(2,1)}, u32[]{:S(2)}, u32[]{:S(2)}) %all-to-all-start.4) | async-done | bytes 7077920 | tf_op jit(solution)/shard_map/all_to_all | solution.py:227
  512.3 46.6 %experts.3 = (bf16[2304,1536]{1,0:T(8,128)(2,1)}, bf16[2304,1536]{1,0:T(8,128)(2,1)}, f32[2304,1]{1,0:T(8,128)}, f32[1536,512]{1,0:T(8,128)}, f32[1536,512]{1,0:T(8,128)}, /*index=5*/f32[512,1536]{1,0:T(8,128)}) custom-call(bf16[2304,1536]{1,0:T(8,128)(2,1)} %bitcast.40.rows_ref, bf16[2304,1536]{1,0:T(8,128)(2,1)} %bitcast.41.blend_ref, ...), custom_call_target="tpu_custom_call" | custom-call | flops 1000 | bytes 1000 | tf_op jit(solution)/shard_map/experts/pallas_call | solution.py:130
  560.7 27.9 %all-to-all-done.5 = bf16[8,288,1536]{2,1,0:T(8,128)(2,1)} async-done(((bf16[8,288,1536]{2,1,0:T(8,128)(2,1)}), bf16[8,288,1536]{2,1,0:T(8,128)(2,1)}, u32[]{:S(2)}, u32[]{:S(2)}) %all-to-all-start.5) | async-done | bytes 7077920 | tf_op jit(solution)/shard_map/all_to_all | solution.py:227
  607.9 15.9 %collective-permute-start.15 = (bf16[256,1536]{1,0:T(8,128)(2,1)S(1)}, bf16[256,1536]{1,0:T(8,128)(2,1)}, u32[]{:S(2)}, u32[]{:S(2)}) collective-permute-start(bf16[256,1536]{1,0:T(8,128)(2,1)S(1)} %get-tuple-element.460), channel_id=1, source_target_pairs={{0,24},{1,25},{2,26},{3,27},{4,28},{5,29},{6,30},{7,31},{8,0},{9,1... | collective-permute-start | bytes 2359304 | tf_op jit(solution)/shard_map/ppermute | solution.py:223
  624.4 17.4 %collective-permute-done.15 = bf16[256,1536]{1,0:T(8,128)(2,1)} collective-permute-done((bf16[256,1536]{1,0:T(8,128)(2,1)S(1)}, bf16[256,1536]{1,0:T(8,128)(2,1)}, u32[]{:S(2)}, u32[]{:S(2)}) %collective-permute-start.15) | collective-permute-done | bytes 786464 | tf_op jit(solution)/shard_map/ppermute | solution.py:223
  641.9 51.0 %collective-permute-done.16 = bf16[256,1536]{1,0:T(8,128)(2,1)} collective-permute-done((bf16[256,1536]{1,0:T(8,128)(2,1)S(1)}, bf16[256,1536]{1,0:T(8,128)(2,1)}, u32[]{:S(2)}, u32[]{:S(2)}) %collective-permute-start.16) | collective-permute-done | bytes 786464 | tf_op jit(solution)/shard_map/ppermute | solution.py:223
  719.9 58.2 %all-to-all-done.8 = bf16[8,288,1536]{2,1,0:T(8,128)(2,1)} async-done(((bf16[8,288,1536]{2,1,0:T(8,128)(2,1)}), bf16[8,288,1536]{2,1,0:T(8,128)(2,1)}, u32[]{:S(2)}, u32[]{:S(2)}) %all-to-all-start.8) | async-done | bytes 7077920 | tf_op jit(solution)/shard_map/all_to_all | solution.py:227
  807.0 34.2 %collective-permute-start.23 = (bf16[256,1536]{1,0:T(8,128)(2,1)}, bf16[256,1536]{1,0:T(8,128)(2,1)}, u32[]{:S(2)}, u32[]{:S(2)}) collective-permute-start(bf16[256,1536]{1,0:T(8,128)(2,1)} %get-tuple-element.455), channel_id=1, source_target_pairs={{0,8},{1,9},{2,10},{3,11},{4,12},{5,13},{6,14},{7,15},{8,16},{9,17... | collective-permute-start | bytes 2359304 | tf_op jit(solution)/shard_map/ppermute | solution.py:223
  841.2 49.6 %collective-permute-done.19 = bf16[256,1536]{1,0:T(8,128)(2,1)S(1)} collective-permute-done((bf16[256,1536]{1,0:T(8,128)(2,1)S(1)}, bf16[256,1536]{1,0:T(8,128)(2,1)S(1)}, u32[]{:S(2)}, u32[]{:S(2)}) %collective-permute-start.19) | collective-permute-done | bytes 786464 | tf_op jit(solution)/shard_map/ppermute | solution.py:223
  951.0 72.3 %all-to-all-done.9 = bf16[8,288,1536]{2,1,0:T(8,128)(2,1)} async-done(((bf16[8,288,1536]{2,1,0:T(8,128)(2,1)}), bf16[8,288,1536]{2,1,0:T(8,128)(2,1)}, u32[]{:S(2)}, u32[]{:S(2)}) %all-to-all-start.9) | async-done | bytes 7077920 | tf_op jit(solution)/shard_map/all_to_all | solution.py:227
  1034.1 13.8 %collective-permute-done.27 = bf16[256,1536]{1,0:T(8,128)(2,1)S(1)} collective-permute-done((bf16[256,1536]{1,0:T(8,128)(2,1)S(1)}, bf16[256,1536]{1,0:T(8,128)(2,1)S(1)}, u32[]{:S(2)}, u32[]{:S(2)}) %collective-permute-start.27) | collective-permute-done | bytes 786464 | tf_op jit(solution)/shard_map/ppermute | solution.py:223
  1048.0 46.1 %collective-permute-done.28 = bf16[256,1536]{1,0:T(8,128)(2,1)S(1)} collective-permute-done((bf16[256,1536]{1,0:T(8,128)(2,1)S(1)}, bf16[256,1536]{1,0:T(8,128)(2,1)S(1)}, u32[]{:S(2)}, u32[]{:S(2)}) %collective-permute-start.28) | collective-permute-done | bytes 786464 | tf_op jit(solution)/shard_map/ppermute | solution.py:223
  1182.3 38.6 %reduce-scatter.7.cloned.1.call-done = bf16[48,1664]{1,0:T(8,128)(2,1)} async-done(((bf16[1536,1664]{1,0:T(8,128)(2,1)}), bf16[48,1664]{1,0:T(8,128)(2,1)}) %reduce-scatter.7.cloned.1.call-update) | async-done | bytes 159760
  1224.4 132.5 %reduce-scatter.5.cloned.1.call-done = bf16[48,2688]{1,0:T(8,128)(2,1)} async-done(((bf16[1536,2688]{1,0:T(8,128)(2,1)}), bf16[48,2688]{1,0:T(8,128)(2,1)}) %reduce-scatter.5.cloned.1.call-update) | async-done | bytes 258064 | tf_op jit(solution)/shard_map/reduce_scatter | solution.py:523
  (596 shorter events, 446.6 us)
Async XLA Ops:
  7.2 147.4 %all-gather.3.cloned.1.call-start = ((), (), s32[]{:S(2)}) async-start(), calls=%async_computation.12 | async-start | bytes 8515584 | tf_op jit(solution)/shard_map/all_gather | solution.py:233
  11.3 238.6 %all-gather.5.cloned.1.call-start = ((), (), s32[]{:S(2)}) async-start(), calls=%async_computation.13 | async-start | bytes 4866048 | tf_op jit(solution)/shard_map/all_gather | solution.py:241
  14.5 119.1 %collective-permute-start.3 = (bf16[256,1536]{1,0:T(8,128)(2,1)S(1)}, bf16[256,1536]{1,0:T(8,128)(2,1)S(1)}, u32[]{:S(2)}, u32[]{:S(2)}) collective-permute-start(bf16[256,1536]{1,0:T(8,128)(2,1)S(1)} %get-tuple-element.462.refs_0_), channel_id=1, source_target_pairs={{0,8},{1,9},{2,10},{3,11},{4,12},{5,13},{6,14},{7,15},{8,16},{9,17... | collective-permute-start | bytes 2359304 | tf_op jit(solution)/shard_map/ppermute | solution.py:218
  17.6 117.0 %collective-permute-start.4 = (bf16[256,1536]{1,0:T(8,128)(2,1)S(1)}, bf16[256,1536]{1,0:T(8,128)(2,1)S(1)}, u32[]{:S(2)}, u32[]{:S(2)}) collective-permute-start(bf16[256,1536]{1,0:T(8,128)(2,1)S(1)} %get-tuple-element.462.refs_0_), channel_id=1, source_target_pairs={{0,16},{1,17},{2,18},{3,19},{4,20},{5,21},{6,22},{7,23},{8,24},{9,... | collective-permute-start | bytes 2359304 | tf_op jit(solution)/shard_map/ppermute | solution.py:218
  20.2 114.5 %collective-permute-start.5 = (bf16[256,1536]{1,0:T(8,128)(2,1)S(1)}, bf16[256,1536]{1,0:T(8,128)(2,1)}, u32[]{:S(2)}, u32[]{:S(2)}) collective-permute-start(bf16[256,1536]{1,0:T(8,128)(2,1)S(1)} %get-tuple-element.462.refs_0_), channel_id=1, source_target_pairs={{0,24},{1,25},{2,26},{3,27},{4,28},{5,29},{6,30},{7,31},{8,0},{9,1... | collective-permute-start | bytes 2359304 | tf_op jit(solution)/shard_map/ppermute | solution.py:218
  25.7 95.2 %collective-permute-start.1 = (s32[2,32,256]{2,1,0:T(8,128)S(1)}, s32[2,32,256]{2,1,0:T(8,128)S(1)}, u32[]{:S(2)}, u32[]{:S(2)}) collective-permute-start(s32[2,32,256]{2,1,0:T(8,128)S(1)} %broadcast_select_fusion), channel_id=1, source_target_pairs={{0,16},{1,17},{2,18},{3,19},{4,20},{5,21},{6,22},{7,23},{8,24},{9,... | collective-permute-start | bytes 196616 | tf_op jit(solution)/shard_map/ppermute | solution.py:218
  120.9 94.1 %collective-permute-start.10 = (bf16[256,1536]{1,0:T(8,128)(2,1)}, bf16[256,1536]{1,0:T(8,128)(2,1)}, u32[]{:S(2)}, u32[]{:S(2)}) collective-permute-start(bf16[256,1536]{1,0:T(8,128)(2,1)} %get-tuple-element.138.refs_0_), channel_id=1, source_target_pairs={{0,16},{1,17},{2,18},{3,19},{4,20},{5,21},{6,22},{7,23},{8,24},{9,... | collective-permute-start | bytes 2359304 | tf_op jit(solution)/shard_map/ppermute | solution.py:218
  127.6 87.4 %collective-permute-start.11 = (bf16[256,1536]{1,0:T(8,128)(2,1)}, bf16[256,1536]{1,0:T(8,128)(2,1)}, u32[]{:S(2)}, u32[]{:S(2)}) collective-permute-start(bf16[256,1536]{1,0:T(8,128)(2,1)} %get-tuple-element.138.refs_0_), channel_id=1, source_target_pairs={{0,24},{1,25},{2,26},{3,27},{4,28},{5,29},{6,30},{7,31},{8,0},{9,1... | collective-permute-start | bytes 2359304 | tf_op jit(solution)/shard_map/ppermute | solution.py:218
  133.6 81.4 %collective-permute-start.9 = (bf16[256,1536]{1,0:T(8,128)(2,1)}, bf16[256,1536]{1,0:T(8,128)(2,1)}, u32[]{:S(2)}, u32[]{:S(2)}) collective-permute-start(bf16[256,1536]{1,0:T(8,128)(2,1)} %get-tuple-element.138.refs_0_), channel_id=1, source_target_pairs={{0,8},{1,9},{2,10},{3,11},{4,12},{5,13},{6,14},{7,15},{8,16},{9,17... | collective-permute-start | bytes 2359304 | tf_op jit(solution)/shard_map/ppermute | solution.py:218
  142.2 95.3 %all-to-all-start = ((bf16[8,288,1536]{2,1,0:T(8,128)(2,1)}), bf16[8,288,1536]{2,1,0:T(8,128)(2,1)}, u32[]{:S(2)}, u32[]{:S(2)}) async-start(bf16[8,288,1536]{2,1,0:T(8,128)(2,1)} %bitcast.487), calls=%async_computation | async-start | bytes 14155776 | tf_op jit(solution)/shard_map/all_to_all | solution.py:227
  237.5 85.0 %all-to-all-start.1 = ((bf16[8,288,1536]{2,1,0:T(8,128)(2,1)}), bf16[8,288,1536]{2,1,0:T(8,128)(2,1)}, u32[]{:S(2)}, u32[]{:S(2)}) async-start(bf16[8,288,1536]{2,1,0:T(8,128)(2,1)} %bitcast.489), calls=%async_computation.1 | async-start | bytes 14155776 | tf_op jit(solution)/shard_map/all_to_all | solution.py:227
  322.6 84.9 %all-to-all-start.2 = ((bf16[8,288,1536]{2,1,0:T(8,128)(2,1)}), bf16[8,288,1536]{2,1,0:T(8,128)(2,1)}, u32[]{:S(2)}, u32[]{:S(2)}) async-start(bf16[8,288,1536]{2,1,0:T(8,128)(2,1)} %bitcast.488), calls=%async_computation.2 | async-start | bytes 14155776 | tf_op jit(solution)/shard_map/all_to_all | solution.py:227
  418.3 85.2 %all-to-all-start.4 = ((bf16[8,288,1536]{2,1,0:T(8,128)(2,1)}), bf16[8,288,1536]{2,1,0:T(8,128)(2,1)}, u32[]{:S(2)}, u32[]{:S(2)}) async-start(bf16[8,288,1536]{2,1,0:T(8,128)(2,1)} %bitcast.490), calls=%async_computation.4 | async-start | bytes 14155776 | tf_op jit(solution)/shard_map/all_to_all | solution.py:227
  503.5 85.0 %all-to-all-start.5 = ((bf16[8,288,1536]{2,1,0:T(8,128)(2,1)}), bf16[8,288,1536]{2,1,0:T(8,128)(2,1)}, u32[]{:S(2)}, u32[]{:S(2)}) async-start(bf16[8,288,1536]{2,1,0:T(8,128)(2,1)} %bitcast.503), calls=%async_computation.5 | async-start | bytes 14155776 | tf_op jit(solution)/shard_map/all_to_all | solution.py:227
  595.8 97.1 %all-to-all-start.7 = ((bf16[8,288,1536]{2,1,0:T(8,128)(2,1)}), bf16[8,288,1536]{2,1,0:T(8,128)(2,1)}, u32[]{:S(2)}, u32[]{:S(2)}) async-start(bf16[8,288,1536]{2,1,0:T(8,128)(2,1)} %bitcast.502), calls=%async_computation.7 | async-start | bytes 14155776 | tf_op jit(solution)/shard_map/all_to_all | solution.py:227
  692.9 85.2 %all-to-all-start.8 = ((bf16[8,288,1536]{2,1,0:T(8,128)(2,1)}), bf16[8,288,1536]{2,1,0:T(8,128)(2,1)}, u32[]{:S(2)}, u32[]{:S(2)}) async-start(bf16[8,288,1536]{2,1,0:T(8,128)(2,1)} %bitcast.501), calls=%async_computation.8 | async-start | bytes 14155776 | tf_op jit(solution)/shard_map/all_to_all | solution.py:227
  787.5 103.3 %collective-permute-start.19 = (bf16[256,1536]{1,0:T(8,128)(2,1)S(1)}, bf16[256,1536]{1,0:T(8,128)(2,1)S(1)}, u32[]{:S(2)}, u32[]{:S(2)}) collective-permute-start(bf16[256,1536]{1,0:T(8,128)(2,1)S(1)} %get-tuple-element.451), channel_id=1, source_target_pairs={{0,16},{1,17},{2,18},{3,19},{4,20},{5,21},{6,22},{7,23},{8,24},{9,... | collective-permute-start | bytes 2359304 | tf_op jit(solution)/shard_map/ppermute | solution.py:223
  788.1 102.7 %collective-permute-start.20 = (bf16[256,1536]{1,0:T(8,128)(2,1)S(1)}, bf16[256,1536]{1,0:T(8,128)(2,1)S(1)}, u32[]{:S(2)}, u32[]{:S(2)}) collective-permute-start(bf16[256,1536]{1,0:T(8,128)(2,1)S(1)} %get-tuple-element.450), channel_id=1, source_target_pairs={{0,8},{1,9},{2,10},{3,11},{4,12},{5,13},{6,14},{7,15},{8,16},{9,17... | collective-permute-start | bytes 2359304 | tf_op jit(solution)/shard_map/ppermute | solution.py:223
  796.6 141.8 %collective-permute-start.21 = (bf16[256,1536]{1,0:T(8,128)(2,1)}, bf16[256,1536]{1,0:T(8,128)(2,1)}, u32[]{:S(2)}, u32[]{:S(2)}) collective-permute-start(bf16[256,1536]{1,0:T(8,128)(2,1)} %get-tuple-element.457), channel_id=1, source_target_pairs={{0,24},{1,25},{2,26},{3,27},{4,28},{5,29},{6,30},{7,31},{8,0},{9,1... | collective-permute-start | bytes 2359304 | tf_op jit(solution)/shard_map/ppermute | solution.py:223
  800.4 138.0 %collective-permute-start.22 = (bf16[256,1536]{1,0:T(8,128)(2,1)}, bf16[256,1536]{1,0:T(8,128)(2,1)}, u32[]{:S(2)}, u32[]{:S(2)}) collective-permute-start(bf16[256,1536]{1,0:T(8,128)(2,1)} %get-tuple-element.456), channel_id=1, source_target_pairs={{0,16},{1,17},{2,18},{3,19},{4,20},{5,21},{6,22},{7,23},{8,24},{9,... | collective-permute-start | bytes 2359304 | tf_op jit(solution)/shard_map/ppermute | solution.py:223
  807.0 131.4 %collective-permute-start.23 = (bf16[256,1536]{1,0:T(8,128)(2,1)}, bf16[256,1536]{1,0:T(8,128)(2,1)}, u32[]{:S(2)}, u32[]{:S(2)}) collective-permute-start(bf16[256,1536]{1,0:T(8,128)(2,1)} %get-tuple-element.455), channel_id=1, source_target_pairs={{0,8},{1,9},{2,10},{3,11},{4,12},{5,13},{6,14},{7,15},{8,16},{9,17... | collective-permute-start | bytes 2359304 | tf_op jit(solution)/shard_map/ppermute | solution.py:223
  938.4 84.8 %all-to-all-start.9 = ((bf16[8,288,1536]{2,1,0:T(8,128)(2,1)}), bf16[8,288,1536]{2,1,0:T(8,128)(2,1)}, u32[]{:S(2)}, u32[]{:S(2)}) async-start(bf16[8,288,1536]{2,1,0:T(8,128)(2,1)} %bitcast.500), calls=%async_computation.9 | async-start | bytes 14155776 | tf_op jit(solution)/shard_map/all_to_all | solution.py:227
  943.3 277.7 %reduce-scatter.7.cloned.1.call-start = ((), (), s32[]{:S(2)}) async-start(), calls=%async_computation.15 | async-start | bytes 5271552
  1109.1 247.8 %reduce-scatter.5.cloned.1.call-start = ((), (), s32[]{:S(2)}) async-start(), calls=%async_computation.14 | async-start | bytes 8515584 | tf_op jit(solution)/shard_map/reduce_scatter | solution.py:523
  (177 other events, 2616.6 us)
Sparse Core Ops, SparseCore 0:
  11.5 143.1 all-gather.2
  157.5 92.3 all-gather.4
  1109.2 111.7 reduce-scatter.6
  1226.7 130.1 reduce-scatter.4

commit v3 on v2

--- a/solution.py
+++ b/solution.py
@@ -2,6 +2,7 @@
 import jax.numpy as jnp
 from jax import lax
 from jax.experimental import pallas as pl
+from jax.experimental.pallas import tpu as pltpu
 from jax.sharding import PartitionSpec as P
 
 H = 24
@@ -20,32 +21,6 @@
     frequency = rope_base ** (-(jnp.arange(half_size, dtype=jnp.float32) * 2.0) / head_size)
     angles = jnp.arange(length, dtype=jnp.float32)[:, None] * frequency[None, :]
     return (jnp.cos(angles)[:, None, :], jnp.sin(angles)[:, None, :])
-
-
-def rotate(operand, cos_table, sin_table):
-    half_size = operand.shape[-1] // 2
-    lower_half = operand[..., :half_size]
-    upper_half = operand[..., half_size:]
-    return jnp.concatenate(
-        [
-            lower_half * cos_table - upper_half * sin_table,
-            upper_half * cos_table + lower_half * sin_table,
-        ],
-        axis=-1,
-    )
-
-
-def unrotate(operand, cos_table, sin_table):
-    half_size = operand.shape[-1] // 2
-    lower_half = operand[..., :half_size]
-    upper_half = operand[..., half_size:]
-    return jnp.concatenate(
-        [
-            lower_half * cos_table + upper_half * sin_table,
-            upper_half * cos_table - lower_half * sin_table,
-        ],
-        axis=-1,
-    )
 
 
 LINES = 4
@@ -171,6 +146,214 @@
     )(slots, *blocks)
 
 
+def swap_halves(value):
+    width = value.shape[1]
+    half = HD // 2
+    lanes = lax.broadcasted_iota(jnp.int32, value.shape, 1)
+    return jnp.where(
+        lanes % HD < half, pltpu.roll(value, width - half, 1), pltpu.roll(value, half, 1)
+    )
+
+
+def head_of(value, head):
+    return value[:, head * HD : (head + 1) * HD]
+
+
+def head_product(left, right, left_axis, right_axis):
+    return lax.dot_general(
+        left,
+        right,
+        (((left_axis,), (right_axis,)), ((), ())),
+        preferred_element_type=jnp.float32,
+    )
+
+
+def probabilities(query, key, visible):
+    scores = jnp.where(visible, attn_scale * head_product(query, key, 1, 1), -1e30)
+    shifted = jnp.exp(scores - jnp.max(scores, axis=1, keepdims=True))
+    return shifted / jnp.sum(shifted, axis=1, keepdims=True)
+
+
+def attend_kernel(
+    query_ref,
+    key_ref,
+    value_ref,
+    cos_ref,
+    sin_ref,
+    own_ref,
+    other_ref,
+    query_out,
+    key_out,
+    value_out,
+    mixture_out,
+):
+    bf16 = jnp.bfloat16
+    key_width = key_ref.shape[1]
+    queries = query_ref[...]
+    keys = key_ref[...]
+    cos_table = cos_ref[...]
+    sin_table = sin_ref[...]
+    queries = (queries * cos_table + swap_halves(queries) * sin_table).astype(bf16)
+    keys = (
+        keys * cos_table[:, :key_width] + swap_halves(keys) * sin_table[:, :key_width]
+    ).astype(bf16)
+    values = value_ref[...].astype(bf16)
+    query_out[...] = queries
+    key_out[...] = keys
+    value_out[...] = values
+    visible = other_ref[0] <= own_ref[...]
+    mixed = []
+    for head in range(queries.shape[1] // HD):
+        shared = head // (H // KVH)
+        probs = probabilities(head_of(queries, head), head_of(keys, shared), visible)
+        mixed.append(head_product(probs.astype(bf16), head_of(values, shared), 1, 0))
+    mixture_out[...] = jnp.concatenate(mixed, axis=1).astype(bf16)
+
+
+def attend_back_kernel(
+    query_ref,
+    key_ref,
+    value_ref,
+    mixture_ref,
+    cos_ref,
+    sin_ref,
+    own_ref,
+    other_ref,
+    query_out,
+    key_out,
+    value_out,
+):
+    bf16 = jnp.bfloat16
+    key_width = key_ref.shape[1]
+    queries = query_ref[...]
+    keys = key_ref[...]
+    values = value_ref[...]
+    grad_mixture = mixture_ref[...]
+    cos_table = cos_ref[...]
+    sin_table = sin_ref[...]
+    visible = other_ref[0] <= own_ref[...]
+    grad_queries = []
+    grad_keys = [0.0] * (key_width // HD)
+    grad_values = [0.0] * (key_width // HD)
+    for head in range(queries.shape[1] // HD):
+        shared = head // (H // KVH)
+        query, key = head_of(queries, head), head_of(keys, shared)
+        grad_mix = head_of(grad_mixture, head)
+        probs = probabilities(query, key, visible)
+        grad_probs = head_product(grad_mix, head_of(values, shared), 1, 1)
+        inner = jnp.sum(probs * grad_probs, axis=1, keepdims=True)
+        grad_scores = (probs * (grad_probs - inner)).astype(bf16)
+        grad_values[shared] += head_product(probs.astype(bf16), grad_mix, 0, 0)
+        grad_keys[shared] += head_product(grad_scores, query, 0, 0)
+        grad_queries.append(head_product(grad_scores, key, 1, 0))
+    grad_query = attn_scale * jnp.concatenate(grad_queries, axis=1)
+    grad_key = attn_scale * jnp.concatenate(grad_keys, axis=1)
+    query_out[...] = (grad_query * cos_table - swap_halves(grad_query) * sin_table).astype(bf16)
+    key_out[...] = (
+        grad_key * cos_table[:, :key_width] - swap_halves(grad_key) * sin_table[:, :key_width]
+    ).astype(bf16)
+    value_out[...] = jnp.concatenate(grad_values, axis=1).astype(bf16)
+
+
+def attention_specs(seq_len):
+    query_block = 2 * (H // KVH) * HD
+    key_block = 2 * HD
+    wide = pl.BlockSpec((seq_len, query_block), lambda m, i: (m, i))
+    thin = pl.BlockSpec((seq_len, key_block), lambda m, i: (m, i))
+    table = pl.BlockSpec((seq_len, query_block), lambda m, i: (0, 0))
+    own = pl.BlockSpec((seq_len, 1), lambda m, i: (m, 0))
+    other = pl.BlockSpec((1, 1, seq_len), lambda m, i: (m, 0, 0))
+    return wide, thin, table, own, other
+
+
+def wide_tables(seq_len):
+    cos_table, sin_table = rotary_tables(seq_len, HD)
+    cos_table, sin_table = cos_table[:, 0], sin_table[:, 0]
+    count = 2 * (H // KVH)
+    return (
+        jnp.tile(jnp.concatenate([cos_table, cos_table], axis=1), (1, count)),
+        jnp.tile(jnp.concatenate([-sin_table, sin_table], axis=1), (1, count)),
+    )
+
+
+def run_attention(projected, tables, block_ids):
+    micro_count, seq_len = block_ids.shape
+    wide, thin, table, own, other = attention_specs(seq_len)
+    rows = projected.shape[0]
+    bf16 = jnp.bfloat16
+    first_key = H * HD // (2 * HD)
+    first_value = first_key + KVH // 2
+    return pl.pallas_call(
+        attend_kernel,
+        grid=(micro_count, KVH // 2),
+        in_specs=[
+            wide,
+            pl.BlockSpec((seq_len, 2 * HD), lambda m, i: (m, first_key + i)),
+            pl.BlockSpec((seq_len, 2 * HD), lambda m, i: (m, first_value + i)),
+            table,
+            table,
+            own,
+            other,
+        ],
+        out_specs=[wide, thin, thin, wide],
+        out_shape=[
+            jax.ShapeDtypeStruct((rows, H * HD), bf16),
+            jax.ShapeDtypeStruct((rows, KVH * HD), bf16),
+            jax.ShapeDtypeStruct((rows, KVH * HD), bf16),
+            jax.ShapeDtypeStruct((rows, H * HD), bf16),
+        ],
+        cost_estimate=pl.CostEstimate(flops=1000, bytes_accessed=1000, transcendentals=0),
+        name="attention",
+    )(
+        projected,
+        projected,
+        projected,
+        *tables,
+        block_ids.reshape(-1, 1),
+        block_ids.reshape(micro_count, 1, seq_len),
+    )
+
+
+def run_attention_back(queries, keys, values, grad_mixture, tables, block_ids, micro):
+    micro_count, seq_len = block_ids.shape
+    wide, thin, table, own, other = attention_specs(seq_len)
+    bf16 = jnp.bfloat16
+
+    def at(spec, index):
+        return pl.BlockSpec(spec.block_shape, index)
+
+    return pl.pallas_call(
+        attend_back_kernel,
+        grid=(1, KVH // 2),
+        in_specs=[
+            at(wide, lambda m, i: (micro, i)),
+            at(thin, lambda m, i: (micro, i)),
+            at(thin, lambda m, i: (micro, i)),
+            wide,
+            table,
+            table,
+            at(own, lambda m, i: (micro, 0)),
+            at(other, lambda m, i: (micro, 0, 0)),
+        ],
+        out_specs=[wide, thin, thin],
+        out_shape=[
+            jax.ShapeDtypeStruct((seq_len, H * HD), bf16),
+            jax.ShapeDtypeStruct((seq_len, KVH * HD), bf16),
+            jax.ShapeDtypeStruct((seq_len, KVH * HD), bf16),
+        ],
+        cost_estimate=pl.CostEstimate(flops=1000, bytes_accessed=1000, transcendentals=0),
+        name="attention_back",
+    )(
+        queries,
+        keys,
+        values,
+        grad_mixture,
+        *tables,
+        block_ids.reshape(-1, 1),
+        block_ids.reshape(micro_count, 1, seq_len),
+    )
+
+
 def on_device(
     hidden,
     cotangent,
@@ -195,11 +378,10 @@
     experts = w_router.shape[1]
     plane = devices // LINES
     capacity = (9 * seq_len * top_count + 8 * experts - 1) // (8 * experts)
-    groups = H // KVH
     query_width = w_query.shape[1]
     kv_width = w_key.shape[1]
     qkv_width = query_width + 2 * kv_width
-    cos_table, sin_table = rotary_tables(seq_len, HD)
+    tables = wide_tables(seq_len)
     gate_local = w_gate[0]
     up_local = w_up[0]
     down_local = w_down[0]
@@ -292,54 +474,19 @@
             total = total + part.astype(f32)
         return total
 
-    def attend(unused, inputs):
-        tokens_in, blocks = inputs
+    def attend(tokens_in):
         recip_first = lax.rsqrt(jnp.mean(tokens_in * tokens_in, axis=1, keepdims=True) + norm_eps)
         normed_in = (tokens_in * recip_first * gain_first).astype(bf16)
         projected = jnp.dot(normed_in, qkv_proj, preferred_element_type=f32)
-        queries = projected[:, :query_width].reshape(seq_len, H, HD)
-        keys_raw = projected[:, query_width : query_width + kv_width].reshape(seq_len, KVH, HD)
-        values = projected[:, query_width + kv_width :].astype(bf16).reshape(seq_len, KVH, HD)
-        query_rot = (
-            rotate(queries, cos_table, sin_table).astype(bf16).reshape(seq_len, KVH, groups, HD)
-        )
-        key_rot = rotate(keys_raw, cos_table, sin_table).astype(bf16)
-        visible = blocks[None, :] <= blocks[:, None]
-        scores = attn_scale * jnp.einsum(
-            "qhgd,khd->hgqk", query_rot, key_rot, preferred_element_type=f32
-        )
-        scores = jnp.where(visible, scores, -1e30)
-        row_peak = jnp.max(scores, axis=3, keepdims=True)
-        shifted_exp = jnp.exp(scores - row_peak)
-        row_total = jnp.sum(shifted_exp, axis=3, keepdims=True)
-        attn_probs = shifted_exp / row_total
-        log_total = row_peak + jnp.log(row_total)
-        mixture = (
-            jnp.einsum(
-                "hgqk,khd->qhgd", attn_probs.astype(bf16), values, preferred_element_type=f32
-            )
-            .reshape(seq_len, H * HD)
-            .astype(bf16)
-        )
-        return (
-            unused,
-            dict(
-                recip_first=recip_first,
-                normed_in=normed_in,
-                values=values,
-                query_rot=query_rot,
-                key_rot=key_rot,
-                log_total=log_total,
-                mixture=mixture,
-            ),
-        )
-
-    def after_attention(kept, tokens_in):
-        attn_out = jnp.dot(kept["mixture"], out_proj, preferred_element_type=f32)
+        queries, keys, values, mixture = run_attention(projected, tables, block_ids)
+        return recip_first, normed_in, queries, keys, values, mixture
+
+    def after_attention(mixture, tokens_in):
+        attn_out = jnp.dot(mixture, out_proj, preferred_element_type=f32)
         residual = tokens_in + res_scale * attn_out
         recip_second = lax.rsqrt(jnp.mean(residual * residual, axis=1, keepdims=True) + norm_eps)
         normed_mid = (residual * recip_second * gain_second).astype(bf16)
-        return dict(kept, residual=residual, recip_second=recip_second, normed_mid=normed_mid)
+        return residual, recip_second, normed_mid
 
     def gates_of(micro, blocks):
         logits = jnp.einsum("de,jtd->jet", router, jnp.stack(blocks), preferred_element_type=f32)
@@ -383,14 +530,13 @@
         both = jnp.stack(token_grads, axis=1)
         return give_back([both[step] for step in range(LINES)])
 
-    def attend_back(micro, grad_mid_sum, pair_blocks, gates, kept):
+    def attend_back(micro, grad_mid_sum, pair_blocks, gates):
         tokens_in = hidden_seq[micro]
         cotan_in = cotan_seq[micro]
-        recip_first, normed_in, values = kept["recip_first"], kept["normed_in"], kept["values"]
-        query_rot, key_rot = kept["query_rot"], kept["key_rot"]
-        visible = block_ids[micro][None, :] <= block_ids[micro][:, None]
-        log_total, mixture, residual = kept["log_total"], kept["mixture"], kept["residual"]
-        recip_second, normed_mid = kept["recip_second"], kept["normed_mid"]
+        residual, recip_second, normed_mid = after[micro]
+        first_recip, first_normed, mixed = (
+            rows_of(part, micro) for part in (recip_first, normed_in, mixture)
+        )
         pair_grads = jnp.zeros((experts, seq_len), f32)
         for step in range(LINES):
             pair_grads = lax.dynamic_update_slice_in_dim(
@@ -409,46 +555,17 @@
         gain_second_w = grad_gain
         grad_residual = cotan_in + grad_residual
         grad_attn = (res_scale * grad_residual).astype(bf16)
-        out_w = jnp.einsum("tc,td->cd", mixture, grad_attn, preferred_element_type=f32)
-        grad_mixture = (
-            jnp.einsum("td,cd->tc", grad_attn, out_proj, preferred_element_type=f32)
-            .astype(bf16)
-            .reshape(seq_len, KVH, groups, HD)
-        )
-        scores_again = attn_scale * jnp.einsum(
-            "qhgd,khd->hgqk", query_rot, key_rot, preferred_element_type=f32
-        )
-        scores_again = jnp.where(visible, scores_again, -1e30)
-        probs_again = jnp.exp(scores_again - log_total)
-        grad_probs = jnp.einsum("qhgd,khd->hgqk", grad_mixture, values, preferred_element_type=f32)
-        grad_values = (
-            jnp.einsum(
-                "hgqk,qhgd->khd", probs_again.astype(bf16), grad_mixture, preferred_element_type=f32
-            )
-            .astype(bf16)
-            .reshape(seq_len, KVH * HD)
-        )
-        grad_scores = (
-            probs_again * (grad_probs - jnp.sum(probs_again * grad_probs, axis=3, keepdims=True))
+        out_w = jnp.einsum("tc,td->cd", mixed, grad_attn, preferred_element_type=f32)
+        grad_mixture = jnp.einsum(
+            "td,cd->tc", grad_attn, out_proj, preferred_element_type=f32
         ).astype(bf16)
-        grad_query_rot = attn_scale * jnp.einsum(
-            "hgqk,khd->qhgd", grad_scores, key_rot, preferred_element_type=f32
-        )
-        grad_key_rot = attn_scale * jnp.einsum(
-            "hgqk,qhgd->khd", grad_scores, query_rot, preferred_element_type=f32
-        )
-        grad_queries = (
-            unrotate(grad_query_rot.reshape(seq_len, H, HD), cos_table, sin_table)
-            .astype(bf16)
-            .reshape(seq_len, H * HD)
-        )
-        grad_keys = (
-            unrotate(grad_key_rot, cos_table, sin_table).astype(bf16).reshape(seq_len, KVH * HD)
+        grad_queries, grad_keys, grad_values = run_attention_back(
+            queries, keys, values, grad_mixture, tables, block_ids, micro
         )
         grad_qkv = jnp.concatenate([grad_queries, grad_keys, grad_values], axis=1)
-        qkv_w = jnp.einsum("td,tc->dc", normed_in, grad_qkv, preferred_element_type=f32)
+        qkv_w = jnp.einsum("td,tc->dc", first_normed, grad_qkv, preferred_element_type=f32)
         grad_normed = jnp.einsum("tc,dc->td", grad_qkv, qkv_proj, preferred_element_type=f32)
-        grad_source, grad_gain = norm_backward(grad_normed, tokens_in, recip_first, gain_first)
+        grad_source, grad_gain = norm_backward(grad_normed, tokens_in, first_recip, gain_first)
         return (
             grad_residual + grad_source,
             out_w,
@@ -458,27 +575,30 @@
             router_w,
         )
 
-    blend_blocks = [spread((res_scale * cotan_seq[m]).astype(bf16)) for m in range(2)]
+    blend_rows = [(res_scale * cotan_seq[m]).astype(bf16) for m in range(2)]
+    blend_blocks = [
+        spread(hold(blend_rows[0], slot_blocks)),
+        spread(hold(blend_rows[1], first)),
+    ]
     blend0 = build(0, blend_blocks[0])
     moved_blend0 = exchange(blend0)
-    unused, kept_both = lax.scan(
-        attend, jnp.zeros((), f32), (hold(hidden_seq, blend0), block_ids)
-    )
-    blend1 = build(1, hold(blend_blocks[1], kept_both["mixture"]))
+    recip_first, normed_in, queries, keys, values, mixture = attend(hold(hidden, blend0))
+
+    def rows_of(value, micro):
+        return value[micro * seq_len : (micro + 1) * seq_len]
+
+    blend1 = build(1, hold(blend_blocks[1], mixture))
     moved_blend1 = exchange(hold(blend1, moved_blend0))
-    kept0, kept1 = (
-        after_attention({name: part[m] for name, part in kept_both.items()}, hidden_seq[m])
-        for m in range(2)
-    )
-    blocks0 = spread(kept0["normed_mid"])
-    blocks1 = spread(kept1["normed_mid"])
+    after = [after_attention(rows_of(mixture, m), hidden_seq[m]) for m in range(2)]
+    blocks0 = spread(after[0][2])
+    blocks1 = spread(after[1][2])
     moved_mid0 = exchange(hold(build(0, blocks0), moved_blend1))
     gates0, slot_gates0 = gates_of(0, blocks0)
     gates1, slot_gates1 = gates_of(1, blocks1)
+    mid1 = build(1, blocks1)
     gate_rows = exchange(
-        hold(jnp.stack([slot_gates0, slot_gates1], axis=1), moved_mid0)
-    )
-    mid1 = build(1, blocks1)
+        hold(jnp.stack([slot_gates0, slot_gates1], axis=1), moved_mid0, mid1)
+    )
     moved_mid1 = exchange(hold(mid1, gate_rows))
     grads0, scaled0, pairs0, weights0 = run_expert(
         hold(moved_mid0, mid1), moved_blend0, gate_rows[:, 0]
@@ -492,17 +612,20 @@
     moved_scaled0 = exchange(hold(scaled0, moved_grads1, back0))
     back1 = sums_of(1, moved_grads1)
     result0 = attend_back(
-        0, total_of(back0), [block[0] for block in pair_blocks], gates0, kept0
-    )
-    moved_scaled1 = exchange(hold(scaled1, moved_scaled0, back1, result0))
-    blend_back0 = sums_of(0, moved_scaled0)
+        0, hold(total_of(back0), back1[0]), [block[0] for block in pair_blocks], gates0
+    )
+    moved_scaled1 = exchange(hold(scaled1, moved_scaled0, back1[1], result0))
+    blend_back0 = sums_of(0, hold(moved_scaled0, result0))
     result1 = attend_back(
-        1, hold(total_of(back1), result0), [block[1] for block in pair_blocks], gates1, kept1
-    )
-    blend_back1 = sums_of(1, moved_scaled1)
+        1,
+        hold(total_of(back1), result0, blend_back0[0]),
+        [block[1] for block in pair_blocks],
+        gates1,
+    )
+    blend_back1 = sums_of(1, hold(moved_scaled1, result1))
     outputs = [
-        kept0["residual"] + res_scale * total_of(blend_back0),
-        kept1["residual"] + res_scale * total_of(blend_back1),
+        after[0][0] + res_scale * total_of(blend_back0),
+        after[1][0] + res_scale * total_of(blend_back1),
     ]
     token_grads_out = [result0[0], result1[0]]
     out_w, qkv_w, gain_first_w, gain_second_w, router_w = (

time: 1370 us -> 1230 us (0.90)
  waiting for transfers between devices: 786 us -> 633 us
  Pallas kernels: 120 us -> 173 us
  matrix products: 141 us -> 93.5 us
  starting transfers between devices: 149 us -> 187 us
  other arithmetic: 79.1 us -> 59.5 us
  local copies, waits for them, and re-layouts: 69.3 us -> 51.9 us
    ppermute x15, waiting for transfers between devices: 190 us -> 81.7 us  [give_back(): lax.ppermute(blocks[step], 'dp', line_shift(-step))]
    all_to_all x9, waiting for transfers between devices: 214 us -> 140 us  [exchange(): lax.all_to_all(block, 'dp', split_axis=0, concat_axis=0, tiled=True, axis...]
    ppermute x15, waiting for transfers between devices: 196 us -> 265 us  [spread(): lax.ppermute(block, 'dp', line_shift(step))]
    pallas_call x0 -> x3, Pallas kernels: none -> 52.4 us  [the longest x2 33.7 us: run_attention_back(): pl.pallas_call(attend_back_kernel, grid=(1, KVH // 2), in_specs=[at(wide,...]
    dot_general x20 -> x6, matrix products: 77.2 us -> 27.6 us  [the longest x2 18.9 us: attend_back(): jnp.einsum('td,tc->dc', first_normed, grad_qkv, preferred_element_type=f32)]
    unnamed x5, waiting for transfers between devices: 38.7 us -> 0.75 us
    all_to_all x9, starting transfers between devices: 43.4 us -> 67 us  [exchange(): lax.all_to_all(block, 'dp', split_axis=0, concat_axis=0, tiled=True, axis...]
  transfers between devices with their start and end apart: 43 -> 43, of which waited for: 27 -> 19; matrix products, arithmetic and copies ran while one was open for 17% -> 13% of each run, Pallas kernels for 9% -> 14%
where the time goes in v3:
time: 1230 us; the launch traced here: 1220 us
  waiting for transfers between devices  633 us (51%)
  starting transfers between devices  187 us (15%)
  Pallas kernels  173 us (14%)
  matrix products  93.5 us (8%)
  other arithmetic  59.5 us (5%)
  local copies, waits for them, and re-layouts  51.9 us (4%)
  between operations  15.4 us (1%)
    ppermute x15, waiting for transfers between devices, spread(): lax.ppermute(block, 'dp', line_shift(step))  265 us
    all_to_all x9, waiting for transfers between devices, exchange(): lax.all_to_all(block, 'dp', split_axis=0, concat_axis=0, tiled=True, axis...  140 us
    reduce_scatter x1, waiting for transfers between devices, on_device(): lax.psum_scatter(jnp.concatenate([qkv_w, jnp.pad(gain_first_w[:, None], (...  126 us
    pallas_call x2, Pallas kernels, run_experts(): pl.pallas_call(expert_kernel, grid=(count // block,), in_specs=[wide, wid...  93.2 us
    ppermute x15, waiting for transfers between devices, give_back(): lax.ppermute(blocks[step], 'dp', line_shift(-step))  81.7 us
    ppermute x15, starting transfers between devices, give_back(): lax.ppermute(blocks[step], 'dp', line_shift(-step))  70.8 us
    all_to_all x9, starting transfers between devices, exchange(): lax.all_to_all(block, 'dp', split_axis=0, concat_axis=0, tiled=True, axis...  67 us
    ppermute x15, starting transfers between devices, spread(): lax.ppermute(block, 'dp', line_shift(step))  48.2 us
  transfers between devices with their start and end apart: 43, of which 19 were waited for; matrix products, arithmetic and copies ran while one was open for 13% of the time, Pallas kernels for 14%

profile of v3, /device:TPU:0, one launch (start us, length us, event | category | flops | bytes accessed | tf_op | source)
XLA Modules:
  0.0 1220.8 jit_solution(1771206926824093319)
XLA Ops:
  36.1 15.5 %collective-permute-done.5.refs_3_ = bf16[256,1536]{1,0:T(8,128)(2,1)S(1)} collective-permute-done((bf16[256,1536]{1,0:T(8,128)(2,1)S(1)}, bf16[256,1536]{1,0:T(8,128)(2,1)S(1)}, u32[]{:S(2)}, u32[]{:S(2)}) %collective-permute-start.5) | collective-permute-done | bytes 786464 | tf_op jit(solution)/shard_map/ppermute | solution.py:400
  51.7 71.5 %collective-permute-done.4.refs_2_ = bf16[256,1536]{1,0:T(8,128)(2,1)S(1)} collective-permute-done((bf16[256,1536]{1,0:T(8,128)(2,1)S(1)}, bf16[256,1536]{1,0:T(8,128)(2,1)S(1)}, u32[]{:S(2)}, u32[]{:S(2)}) %collective-permute-start.4) | collective-permute-done | bytes 786464 | tf_op jit(solution)/shard_map/ppermute | solution.py:400
  166.6 18.7 %attention.1 = (bf16[512,1536]{1,0:T(8,128)(2,1)}, bf16[512,512]{1,0:T(8,128)(2,1)}, bf16[512,512]{1,0:T(8,128)(2,1)}, bf16[512,1536]{1,0:T(8,128)(2,1)}) custom-call(f32[512,2560]{1,0:T(8,128)} %fusion.16.query_ref.key_ref.value_ref, f32[512,2560]{1,0:T(8,128)} %fusion.16.query_ref.key_ref.value_ref, f32[512,2560]{1,0:T(8,128)} %fusion.16.query_ref.key_ref.value_ref, ...), custom_call_target="tpu_custom_call" | custom-call | flops 1000 | bytes 1000 | tf_op jit(solution)/shard_map/attention/pallas_call | solution.py:286
  185.3 40.4 %collective-permute-done.10.refs_2_ = bf16[256,1536]{1,0:T(8,128)(2,1)} collective-permute-done((bf16[256,1536]{1,0:T(8,128)(2,1)}, bf16[256,1536]{1,0:T(8,128)(2,1)}, u32[]{:S(2)}, u32[]{:S(2)}) %collective-permute-start.10) | collective-permute-done | bytes 786464 | tf_op jit(solution)/shard_map/ppermute | solution.py:400
  232.6 28.8 %all-to-all-start.1 = ((bf16[8,288,1536]{2,1,0:T(8,128)(2,1)}), bf16[8,288,1536]{2,1,0:T(8,128)(2,1)}, u32[]{:S(2)}, u32[]{:S(2)}) async-start(bf16[8,288,1536]{2,1,0:T(8,128)(2,1)} %bitcast.205), calls=%async_computation.1 | async-start | bytes 14155776 | tf_op jit(solution)/shard_map/all_to_all | solution.py:409
  261.4 18.0 %all-gather.5.cloned.1.call-done = bf16[1536,1536]{1,0:T(8,128)(2,1)} async-done(((bf16[48,1536]{1,0:T(8,128)(2,1)}), bf16[1536,1536]{1,0:T(8,128)(2,1)}) %all-gather.5.cloned.1.call-update) | async-done | bytes 4718608 | tf_op jit(solution)/shard_map/all_gather | solution.py:423
  287.6 18.0 %collective-permute-start.8 = (bf16[256,1536]{1,0:T(8,128)(2,1)S(1)}, bf16[256,1536]{1,0:T(8,128)(2,1)S(1)}, u32[]{:S(2)}, u32[]{:S(2)}) collective-permute-start(bf16[256,1536]{1,0:T(8,128)(2,1)S(1)} %get-tuple-element.201.refs_0_), channel_id=1, source_target_pairs={{0,24},{1,25},{2,26},{3,27},{4,28},{5,29},{6,30},{7,31},{8,0},{9,1... | collective-permute-start | bytes 2359304 | tf_op jit(solution)/shard_map/ppermute | solution.py:400
  310.3 15.7 %collective-permute-done.8.refs_3_ = bf16[256,1536]{1,0:T(8,128)(2,1)S(1)} collective-permute-done((bf16[256,1536]{1,0:T(8,128)(2,1)S(1)}, bf16[256,1536]{1,0:T(8,128)(2,1)S(1)}, u32[]{:S(2)}, u32[]{:S(2)}) %collective-permute-start.8) | collective-permute-done | bytes 786464 | tf_op jit(solution)/shard_map/ppermute | solution.py:400
  326.0 51.7 %collective-permute-done.7.refs_2_ = bf16[256,1536]{1,0:T(8,128)(2,1)S(1)} collective-permute-done((bf16[256,1536]{1,0:T(8,128)(2,1)S(1)}, bf16[256,1536]{1,0:T(8,128)(2,1)S(1)}, u32[]{:S(2)}, u32[]{:S(2)}) %collective-permute-start.7) | collective-permute-done | bytes 786464 | tf_op jit(solution)/shard_map/ppermute | solution.py:400
  393.0 18.7 %collective-permute-done.14.refs_3_ = bf16[256,1536]{1,0:T(8,128)(2,1)} collective-permute-done((bf16[256,1536]{1,0:T(8,128)(2,1)}, bf16[256,1536]{1,0:T(8,128)(2,1)}, u32[]{:S(2)}, u32[]{:S(2)}) %collective-permute-start.14) | collective-permute-done | bytes 786464 | tf_op jit(solution)/shard_map/ppermute | solution.py:400
  411.7 47.1 %collective-permute-done.13.refs_2_ = bf16[256,1536]{1,0:T(8,128)(2,1)} collective-permute-done((bf16[256,1536]{1,0:T(8,128)(2,1)}, bf16[256,1536]{1,0:T(8,128)(2,1)}, u32[]{:S(2)}, u32[]{:S(2)}) %collective-permute-start.13) | collective-permute-done | bytes 786464 | tf_op jit(solution)/shard_map/ppermute | solution.py:400
  492.2 46.6 %experts.2 = (bf16[2304,1536]{1,0:T(8,128)(2,1)}, bf16[2304,1536]{1,0:T(8,128)(2,1)}, f32[2304,1]{1,0:T(8,128)}, f32[1536,512]{1,0:T(8,128)}, f32[1536,512]{1,0:T(8,128)}, /*index=5*/f32[512,1536]{1,0:T(8,128)}) custom-call(bf16[2304,1536]{1,0:T(8,128)(2,1)} %bitcast.18.rows_ref, bf16[2304,1536]{1,0:T(8,128)(2,1)} %bitcast.19.blend_ref, ...), custom_call_target="tpu_custom_call" | custom-call | flops 1000 | bytes 1000 | tf_op jit(solution)/shard_map/experts/pallas_call | solution.py:105
  538.8 31.3 %all-to-all-done.4 = bf16[8,288,1536]{2,1,0:T(8,128)(2,1)} async-done(((bf16[8,288,1536]{2,1,0:T(8,128)(2,1)}), bf16[8,288,1536]{2,1,0:T(8,128)(2,1)}, u32[]{:S(2)}, u32[]{:S(2)}) %all-to-all-start.4) | async-done | bytes 7077920 | tf_op jit(solution)/shard_map/all_to_all | solution.py:409
  579.0 46.6 %experts.3 = (bf16[2304,1536]{1,0:T(8,128)(2,1)}, bf16[2304,1536]{1,0:T(8,128)(2,1)}, f32[2304,1]{1,0:T(8,128)}, f32[1536,512]{1,0:T(8,128)}, f32[1536,512]{1,0:T(8,128)}, /*index=5*/f32[512,1536]{1,0:T(8,128)}) custom-call(bf16[2304,1536]{1,0:T(8,128)(2,1)} %bitcast.39.rows_ref, bf16[2304,1536]{1,0:T(8,128)(2,1)} %bitcast.40.blend_ref, ...), custom_call_target="tpu_custom_call" | custom-call | flops 1000 | bytes 1000 | tf_op jit(solution)/shard_map/experts/pallas_call | solution.py:105
  627.3 27.7 %all-to-all-done.5 = bf16[8,288,1536]{2,1,0:T(8,128)(2,1)} async-done(((bf16[8,288,1536]{2,1,0:T(8,128)(2,1)}), bf16[8,288,1536]{2,1,0:T(8,128)(2,1)}, u32[]{:S(2)}, u32[]{:S(2)}) %all-to-all-start.5) | async-done | bytes 7077920 | tf_op jit(solution)/shard_map/all_to_all | solution.py:409
  687.6 37.9 %collective-permute-done.18 = f32[2,8,256]{2,1,0:T(8,128)S(1)} collective-permute-done((f32[2,8,256]{2,1,0:T(8,128)S(1)}, f32[2,8,256]{2,1,0:T(8,128)S(1)}, u32[]{:S(2)}, u32[]{:S(2)}) %collective-permute-start.18) | collective-permute-done | bytes 16416 | tf_op jit(solution)/shard_map/ppermute | solution.py:405
  725.5 16.7 %collective-permute-start.19 = (f32[2,8,256]{2,1,0:T(8,128)S(1)}, f32[2,8,256]{2,1,0:T(8,128)S(1)}, u32[]{:S(2)}, u32[]{:S(2)}) collective-permute-start(f32[2,8,256]{2,1,0:T(8,128)S(1)} %get-tuple-element.193), channel_id=1, source_target_pairs={{0,16},{1,17},{2,18},{3,19},{4,20},{5,21},{6,22},{7,23},{8,24},{9,... | collective-permute-start | bytes 49160 | tf_op jit(solution)/shard_map/ppermute | solution.py:405
  753.8 16.9 %attention_back.2 = (bf16[256,1536]{1,0:T(8,128)(2,1)}, bf16[256,512]{1,0:T(8,128)(2,1)}, bf16[256,512]{1,0:T(8,128)(2,1)}) custom-call(bf16[512,1536]{1,0:T(8,128)(2,1)} %get-tuple-element.78.query_ref, bf16[512,512]{1,0:T(8,128)(2,1)} %get-tuple-element.79.key_ref, bf16[512,512]{1,0:T(8,128)(2,1)} %get-tuple-element.80.value_ref, ...), custom_call_target="tpu_custom_call" | custom-call | flops 1000 | bytes 1000 | tf_op jit(solution)/shard_map/attention_back/pallas_call | solution.py:325
  801.0 38.9 %collective-permute-done.25 = bf16[256,1536]{1,0:T(8,128)(2,1)S(1)} collective-permute-done((bf16[256,1536]{1,0:T(8,128)(2,1)S(1)}, bf16[256,1536]{1,0:T(8,128)(2,1)S(1)}, u32[]{:S(2)}, u32[]{:S(2)}) %collective-permute-start.25) | collective-permute-done | bytes 786464 | tf_op jit(solution)/shard_map/ppermute | solution.py:405
  864.8 16.9 %attention_back.3 = (bf16[256,1536]{1,0:T(8,128)(2,1)}, bf16[256,512]{1,0:T(8,128)(2,1)}, bf16[256,512]{1,0:T(8,128)(2,1)}) custom-call(bf16[512,1536]{1,0:T(8,128)(2,1)} %get-tuple-element.78.query_ref, bf16[512,512]{1,0:T(8,128)(2,1)} %get-tuple-element.79.key_ref, bf16[512,512]{1,0:T(8,128)(2,1)} %get-tuple-element.80.value_ref, ...), custom_call_target="tpu_custom_call" | custom-call | flops 1000 | bytes 1000 | tf_op jit(solution)/shard_map/attention_back/pallas_call | solution.py:325
  909.4 39.2 %all-to-all-done.8 = bf16[8,288,1536]{2,1,0:T(8,128)(2,1)} async-done(((bf16[8,288,1536]{2,1,0:T(8,128)(2,1)}), bf16[8,288,1536]{2,1,0:T(8,128)(2,1)}, u32[]{:S(2)}, u32[]{:S(2)}) %all-to-all-start.8) | async-done | bytes 7077920 | tf_op jit(solution)/shard_map/all_to_all | solution.py:409
  979.7 12.9 %collective-permute-start.23 = (bf16[256,1536]{1,0:T(8,128)(2,1)S(1)}, bf16[256,1536]{1,0:T(8,128)(2,1)S(1)}, u32[]{:S(2)}, u32[]{:S(2)}) collective-permute-start(bf16[256,1536]{1,0:T(8,128)(2,1)S(1)} %get-tuple-element.173), channel_id=1, source_target_pairs={{0,8},{1,9},{2,10},{3,11},{4,12},{5,13},{6,14},{7,15},{8,16},{9,17... | collective-permute-start | bytes 2359304 | tf_op jit(solution)/shard_map/ppermute | solution.py:405
  996.4 42.0 %all-to-all-done.9 = bf16[8,288,1536]{2,1,0:T(8,128)(2,1)} async-done(((bf16[8,288,1536]{2,1,0:T(8,128)(2,1)}), bf16[8,288,1536]{2,1,0:T(8,128)(2,1)}, u32[]{:S(2)}, u32[]{:S(2)}) %all-to-all-start.9) | async-done | bytes 7077920 | tf_op jit(solution)/shard_map/all_to_all | solution.py:409
  1078.3 126.4 %reduce-scatter.5.cloned.1.call-done = bf16[48,2688]{1,0:T(8,128)(2,1)} async-done(((bf16[1536,2688]{1,0:T(8,128)(2,1)}), bf16[48,2688]{1,0:T(8,128)(2,1)}) %reduce-scatter.5.cloned.1.call-update) | async-done | bytes 258064 | tf_op jit(solution)/shard_map/reduce_scatter | solution.py:646
  (339 shorter events, 361.2 us)
Async XLA Ops:
  7.2 135.3 %all-gather.3.cloned.1.call-start = ((), (), s32[]{:S(2)}) async-start(), calls=%async_computation.12 | async-start | bytes 8515584 | tf_op jit(solution)/shard_map/all_gather | solution.py:415
  32.7 90.5 %collective-permute-start.4 = (bf16[256,1536]{1,0:T(8,128)(2,1)S(1)}, bf16[256,1536]{1,0:T(8,128)(2,1)S(1)}, u32[]{:S(2)}, u32[]{:S(2)}) collective-permute-start(bf16[256,1536]{1,0:T(8,128)(2,1)S(1)} %get-tuple-element.55.refs_0_), channel_id=1, source_target_pairs={{0,16},{1,17},{2,18},{3,19},{4,20},{5,21},{6,22},{7,23},{8,24},{9,... | collective-permute-start | bytes 2359304 | tf_op jit(solution)/shard_map/ppermute | solution.py:400
  33.6 89.6 %collective-permute-start.3 = (bf16[256,1536]{1,0:T(8,128)(2,1)S(1)}, bf16[256,1536]{1,0:T(8,128)(2,1)S(1)}, u32[]{:S(2)}, u32[]{:S(2)}) collective-permute-start(bf16[256,1536]{1,0:T(8,128)(2,1)S(1)} %get-tuple-element.55.refs_0_), channel_id=1, source_target_pairs={{0,8},{1,9},{2,10},{3,11},{4,12},{5,13},{6,14},{7,15},{8,16},{9,17... | collective-permute-start | bytes 2359304 | tf_op jit(solution)/shard_map/ppermute | solution.py:400
  131.1 101.5 %all-to-all-start = ((bf16[8,288,1536]{2,1,0:T(8,128)(2,1)}), bf16[8,288,1536]{2,1,0:T(8,128)(2,1)}, u32[]{:S(2)}, u32[]{:S(2)}) async-start(bf16[8,288,1536]{2,1,0:T(8,128)(2,1)} %bitcast.202), calls=%async_computation | async-start | bytes 14155776 | tf_op jit(solution)/shard_map/all_to_all | solution.py:409
  136.2 143.3 %all-gather.5.cloned.1.call-start = ((), (), s32[]{:S(2)}) async-start(), calls=%async_computation.13 | async-start | bytes 4866048 | tf_op jit(solution)/shard_map/all_gather | solution.py:423
  150.1 75.6 %collective-permute-start.10 = (bf16[256,1536]{1,0:T(8,128)(2,1)}, bf16[256,1536]{1,0:T(8,128)(2,1)}, u32[]{:S(2)}, u32[]{:S(2)}) collective-permute-start(bf16[256,1536]{1,0:T(8,128)(2,1)} %get-tuple-element.59.refs_0_), channel_id=1, source_target_pairs={{0,16},{1,17},{2,18},{3,19},{4,20},{5,21},{6,22},{7,23},{8,24},{9,... | collective-permute-start | bytes 2359304 | tf_op jit(solution)/shard_map/ppermute | solution.py:400
  232.6 152.7 %all-to-all-start.1 = ((bf16[8,288,1536]{2,1,0:T(8,128)(2,1)}), bf16[8,288,1536]{2,1,0:T(8,128)(2,1)}, u32[]{:S(2)}, u32[]{:S(2)}) async-start(bf16[8,288,1536]{2,1,0:T(8,128)(2,1)} %bitcast.205), calls=%async_computation.1 | async-start | bytes 14155776 | tf_op jit(solution)/shard_map/all_to_all | solution.py:409
  385.3 91.3 %all-to-all-start.2 = ((bf16[8,288,1536]{2,1,0:T(8,128)(2,1)}), bf16[8,288,1536]{2,1,0:T(8,128)(2,1)}, u32[]{:S(2)}, u32[]{:S(2)}) async-start(bf16[8,288,1536]{2,1,0:T(8,128)(2,1)} %bitcast.203), calls=%async_computation.2 | async-start | bytes 14155776 | tf_op jit(solution)/shard_map/all_to_all | solution.py:409
  485.0 85.0 %all-to-all-start.4 = ((bf16[8,288,1536]{2,1,0:T(8,128)(2,1)}), bf16[8,288,1536]{2,1,0:T(8,128)(2,1)}, u32[]{:S(2)}, u32[]{:S(2)}) async-start(bf16[8,288,1536]{2,1,0:T(8,128)(2,1)} %bitcast.204), calls=%async_computation.4 | async-start | bytes 14155776 | tf_op jit(solution)/shard_map/all_to_all | solution.py:409
  570.1 85.0 %all-to-all-start.5 = ((bf16[8,288,1536]{2,1,0:T(8,128)(2,1)}), bf16[8,288,1536]{2,1,0:T(8,128)(2,1)}, u32[]{:S(2)}, u32[]{:S(2)}) async-start(bf16[8,288,1536]{2,1,0:T(8,128)(2,1)} %bitcast.209), calls=%async_computation.5 | async-start | bytes 14155776 | tf_op jit(solution)/shard_map/all_to_all | solution.py:409
  669.4 76.2 %collective-permute-start.17 = (bf16[256,1536]{1,0:T(8,128)(2,1)}, bf16[256,1536]{1,0:T(8,128)(2,1)}, u32[]{:S(2)}, u32[]{:S(2)}) collective-permute-start(bf16[256,1536]{1,0:T(8,128)(2,1)} %get-tuple-element.181), channel_id=1, source_target_pairs={{0,8},{1,9},{2,10},{3,11},{4,12},{5,13},{6,14},{7,15},{8,16},{9,17... | collective-permute-start | bytes 2359304 | tf_op jit(solution)/shard_map/ppermute | solution.py:405
  670.9 74.7 %collective-permute-start.16 = (bf16[256,1536]{1,0:T(8,128)(2,1)}, bf16[256,1536]{1,0:T(8,128)(2,1)}, u32[]{:S(2)}, u32[]{:S(2)}) collective-permute-start(bf16[256,1536]{1,0:T(8,128)(2,1)} %get-tuple-element.182), channel_id=1, source_target_pairs={{0,16},{1,17},{2,18},{3,19},{4,20},{5,21},{6,22},{7,23},{8,24},{9,... | collective-permute-start | bytes 2359304 | tf_op jit(solution)/shard_map/ppermute | solution.py:405
  672.8 72.8 %collective-permute-start.15 = (bf16[256,1536]{1,0:T(8,128)(2,1)}, bf16[256,1536]{1,0:T(8,128)(2,1)}, u32[]{:S(2)}, u32[]{:S(2)}) collective-permute-start(bf16[256,1536]{1,0:T(8,128)(2,1)} %get-tuple-element.183), channel_id=1, source_target_pairs={{0,24},{1,25},{2,26},{3,27},{4,28},{5,29},{6,30},{7,31},{8,0},{9,1... | collective-permute-start | bytes 2359304 | tf_op jit(solution)/shard_map/ppermute | solution.py:405
  675.8 103.2 %all-to-all-start.7 = ((bf16[8,288,1536]{2,1,0:T(8,128)(2,1)}), bf16[8,288,1536]{2,1,0:T(8,128)(2,1)}, u32[]{:S(2)}, u32[]{:S(2)}) async-start(bf16[8,288,1536]{2,1,0:T(8,128)(2,1)} %bitcast.208), calls=%async_computation.7 | async-start | bytes 14155776 | tf_op jit(solution)/shard_map/all_to_all | solution.py:409
  680.7 390.5 %reduce-scatter.7.cloned.1.call-start = ((), (), s32[]{:S(2)}) async-start(), calls=%async_computation.15 | async-start | bytes 5271552
  854.6 93.9 %all-to-all-start.8 = ((bf16[8,288,1536]{2,1,0:T(8,128)(2,1)}), bf16[8,288,1536]{2,1,0:T(8,128)(2,1)}, u32[]{:S(2)}, u32[]{:S(2)}) async-start(bf16[8,288,1536]{2,1,0:T(8,128)(2,1)} %bitcast.206), calls=%async_computation.8 | async-start | bytes 14155776 | tf_op jit(solution)/shard_map/all_to_all | solution.py:409
  859.4 345.3 %reduce-scatter.5.cloned.1.call-start = ((), (), s32[]{:S(2)}) async-start(), calls=%async_computation.14 | async-start | bytes 8515584 | tf_op jit(solution)/shard_map/reduce_scatter | solution.py:646
  948.6 89.8 %all-to-all-start.9 = ((bf16[8,288,1536]{2,1,0:T(8,128)(2,1)}), bf16[8,288,1536]{2,1,0:T(8,128)(2,1)}, u32[]{:S(2)}, u32[]{:S(2)}) async-start(bf16[8,288,1536]{2,1,0:T(8,128)(2,1)} %bitcast.207), calls=%async_computation.9 | async-start | bytes 14155776 | tf_op jit(solution)/shard_map/all_to_all | solution.py:409
  976.2 85.8 %collective-permute-start.21 = (bf16[256,1536]{1,0:T(8,128)(2,1)}, bf16[256,1536]{1,0:T(8,128)(2,1)S(1)}, u32[]{:S(2)}, u32[]{:S(2)}) collective-permute-start(bf16[256,1536]{1,0:T(8,128)(2,1)} %get-tuple-element.172), channel_id=1, source_target_pairs={{0,24},{1,25},{2,26},{3,27},{4,28},{5,29},{6,30},{7,31},{8,0},{9,1... | collective-permute-start | bytes 2359304 | tf_op jit(solution)/shard_map/ppermute | solution.py:405
  979.7 85.3 %collective-permute-start.23 = (bf16[256,1536]{1,0:T(8,128)(2,1)S(1)}, bf16[256,1536]{1,0:T(8,128)(2,1)S(1)}, u32[]{:S(2)}, u32[]{:S(2)}) collective-permute-start(bf16[256,1536]{1,0:T(8,128)(2,1)S(1)} %get-tuple-element.173), channel_id=1, source_target_pairs={{0,8},{1,9},{2,10},{3,11},{4,12},{5,13},{6,14},{7,15},{8,16},{9,17... | collective-permute-start | bytes 2359304 | tf_op jit(solution)/shard_map/ppermute | solution.py:405
  992.6 76.4 %collective-permute-start.22 = (bf16[256,1536]{1,0:T(8,128)(2,1)S(1)}, bf16[256,1536]{1,0:T(8,128)(2,1)}, u32[]{:S(2)}, u32[]{:S(2)}) collective-permute-start(bf16[256,1536]{1,0:T(8,128)(2,1)S(1)} %get-tuple-element.174), channel_id=1, source_target_pairs={{0,16},{1,17},{2,18},{3,19},{4,20},{5,21},{6,22},{7,23},{8,24},{9,... | collective-permute-start | bytes 2359304 | tf_op jit(solution)/shard_map/ppermute | solution.py:405
  1046.5 163.1 %collective-permute-start.27 = (bf16[256,1536]{1,0:T(8,128)(2,1)}, bf16[256,1536]{1,0:T(8,128)(2,1)}, u32[]{:S(2)}, u32[]{:S(2)}) collective-permute-start(bf16[256,1536]{1,0:T(8,128)(2,1)} %get-tuple-element.175), channel_id=1, source_target_pairs={{0,24},{1,25},{2,26},{3,27},{4,28},{5,29},{6,30},{7,31},{8,0},{9,1... | collective-permute-start | bytes 2359304 | tf_op jit(solution)/shard_map/ppermute | solution.py:405
  1050.0 159.6 %collective-permute-start.29 = (bf16[256,1536]{1,0:T(8,128)(2,1)}, bf16[256,1536]{1,0:T(8,128)(2,1)}, u32[]{:S(2)}, u32[]{:S(2)}) collective-permute-start(bf16[256,1536]{1,0:T(8,128)(2,1)} %get-tuple-element.176), channel_id=1, source_target_pairs={{0,8},{1,9},{2,10},{3,11},{4,12},{5,13},{6,14},{7,15},{8,16},{9,17... | collective-permute-start | bytes 2359304 | tf_op jit(solution)/shard_map/ppermute | solution.py:405
  1062.0 147.5 %collective-permute-start.28 = (bf16[256,1536]{1,0:T(8,128)(2,1)}, bf16[256,1536]{1,0:T(8,128)(2,1)}, u32[]{:S(2)}, u32[]{:S(2)}) collective-permute-start(bf16[256,1536]{1,0:T(8,128)(2,1)} %get-tuple-element.177), channel_id=1, source_target_pairs={{0,16},{1,17},{2,18},{3,19},{4,20},{5,21},{6,22},{7,23},{8,24},{9,... | collective-permute-start | bytes 2359304 | tf_op jit(solution)/shard_map/ppermute | solution.py:405
  (78 other events, 1666.4 us)
Sparse Core Ops, SparseCore 0:
  11.4 130.9 all-gather.2
  145.4 134.0 all-gather.4
  854.7 204.2 reduce-scatter.6
  1064.8 139.9 reduce-scatter.4

commit v4 on v3

--- a/solution.py
+++ b/solution.py
@@ -354,6 +354,41 @@
     )
 
 
+def weights_kernel(left_ref, right_ref, *refs):
+    out_ref = refs[-1]
+    width = right_ref.shape[1]
+    product = head_product(left_ref[...], right_ref[...], 0, 0)
+    if len(refs) == 1:
+        out_ref[...] = product.astype(out_ref.dtype)
+    else:
+        out_ref[:, :width] = product.astype(out_ref.dtype)
+        out_ref[:, width:] = refs[0][...].astype(out_ref.dtype)
+
+
+def run_weights(left, right, extra, dtype):
+    tokens, height = left.shape
+    width = right.shape[1]
+    block = 256 if height % 256 == 0 else height
+    in_specs = [
+        pl.BlockSpec((tokens, block), lambda i: (0, i)),
+        pl.BlockSpec((tokens, width), lambda i: (0, 0)),
+    ]
+    operands = [left, right]
+    if extra is not None:
+        in_specs.append(pl.BlockSpec((block, extra.shape[1]), lambda i: (i, 0)))
+        operands.append(extra)
+        width += extra.shape[1]
+    return pl.pallas_call(
+        weights_kernel,
+        grid=(height // block,),
+        in_specs=in_specs,
+        out_specs=pl.BlockSpec((block, width), lambda i: (i, 0)),
+        out_shape=jax.ShapeDtypeStruct((height, width), dtype),
+        cost_estimate=pl.CostEstimate(flops=1000, bytes_accessed=1000, transcendentals=0),
+        name="weights",
+    )(*operands)
+
+
 def on_device(
     hidden,
     cotangent,
@@ -405,6 +440,40 @@
             lax.ppermute(blocks[step], "dp", line_shift(-step)) for step in range(1, LINES)
         ]
 
+    def hold(value, *after):
+        return lax.optimization_barrier((value, after))[0]
+
+    def reduce_rows(value, early, late):
+        if plane != 8:
+            return lax.psum_scatter(
+                value.astype(bf16), "dp", scatter_dimension=0, tiled=True
+            ).astype(f32)
+        index = lax.axis_index("dp")
+        rows = value.shape[0] // devices
+        half = value.shape[1] // 256 * 128
+
+        def fold(block, axis, bit):
+            side = (index // bit) % 2
+            kept = lax.dynamic_index_in_dim(block, side, axis, keepdims=False)
+            sent = lax.dynamic_index_in_dim(block, 1 - side, axis, keepdims=False)
+            other = lax.ppermute(
+                sent.astype(bf16), "dp", [(i, i ^ bit) for i in range(devices)]
+            )
+            return kept + other.astype(f32)
+
+        block = fold(value.reshape(LINES, 2, 2, 2, rows, value.shape[1]), 3, 1)
+        left, right = block[..., :half], block[..., half:]
+        left, right = fold(left, 1, 4), fold(right, 2, 2)
+        left, right = hold((left, right), early)
+        left, right = fold(left, 1, 2), fold(right, 1, 4)
+        block = hold(jnp.concatenate([left, right], axis=2), late)
+        total = lax.dynamic_index_in_dim(block, here, 0, keepdims=False)
+        for step in range(1, LINES):
+            sent = lax.dynamic_index_in_dim(block, (here + step) % LINES, 0, keepdims=False)
+            total = total + lax.ppermute(sent.astype(bf16), "dp", line_shift(step)).astype(f32)
+        return total
+
+
     def exchange(block):
         return lax.all_to_all(
             block, "dp", split_axis=0, concat_axis=0, tiled=True, axis_index_groups=plane_groups
@@ -412,19 +481,20 @@
 
     small = jnp.concatenate([norm1_gain[:, None], norm2_gain[:, None], w_router], axis=1)
     pad = -small.shape[1] % 128
-    first = lax.all_gather(
+    shared = lax.all_gather(
         jnp.concatenate(
-            [w_query, w_key, w_value, jnp.pad(small, ((0, 0), (0, pad)))], axis=1
+            [w_query, w_key, w_value, w_out, jnp.pad(small, ((0, 0), (0, pad)))], axis=1
         ),
         "dp",
         axis=0,
         tiled=True,
     )
-    out_proj = lax.all_gather(w_out, "dp", axis=0, tiled=True)
-    qkv_proj = first[:, :qkv_width]
-    gain_first = first[:, qkv_width].astype(f32)
-    gain_second = first[:, qkv_width + 1].astype(f32)
-    router = first[:, qkv_width + 2 : qkv_width + 2 + experts]
+    qkv_proj = shared[:, :qkv_width]
+    first_small = qkv_width + model_width
+    out_proj = shared[:, qkv_width:first_small]
+    gain_first = shared[:, first_small].astype(f32)
+    gain_second = shared[:, first_small + 1].astype(f32)
+    router = shared[:, first_small + 2 : first_small + 2 + experts]
 
     labels = jnp.arange(experts, dtype=jnp.int32)
     route_seq = routes.reshape(micro_count, seq_len, top_count)
@@ -446,9 +516,6 @@
 
     cotan_seq = cotangent.reshape(micro_count, seq_len, model_width)
     hidden_seq = hidden.reshape(micro_count, seq_len, model_width)
-
-    def hold(value, *after):
-        return lax.optimization_barrier((value, after))[0]
 
     def build(micro, blocks):
         if capacity % 8 == 0:
@@ -530,13 +597,11 @@
         both = jnp.stack(token_grads, axis=1)
         return give_back([both[step] for step in range(LINES)])
 
-    def attend_back(micro, grad_mid_sum, pair_blocks, gates):
+    def attend_back(micro, grad_mid_sum, pair_blocks, gates, before):
         tokens_in = hidden_seq[micro]
         cotan_in = cotan_seq[micro]
         residual, recip_second, normed_mid = after[micro]
-        first_recip, first_normed, mixed = (
-            rows_of(part, micro) for part in (recip_first, normed_in, mixture)
-        )
+        first_recip = rows_of(recip_first, micro)
         pair_grads = jnp.zeros((experts, seq_len), f32)
         for step in range(LINES):
             pair_grads = lax.dynamic_update_slice_in_dim(
@@ -545,9 +610,6 @@
         grad_logits = (
             gates * (pair_grads - jnp.sum(gates * pair_grads, axis=0, keepdims=True))
         ).astype(bf16)
-        router_w = jnp.einsum(
-            "td,et->de", normed_mid, grad_logits, preferred_element_type=f32
-        )
         grad_mid = grad_mid_sum + jnp.einsum(
             "et,de->td", grad_logits, router, preferred_element_type=f32
         )
@@ -555,34 +617,32 @@
         gain_second_w = grad_gain
         grad_residual = cotan_in + grad_residual
         grad_attn = (res_scale * grad_residual).astype(bf16)
-        out_w = jnp.einsum("tc,td->cd", mixed, grad_attn, preferred_element_type=f32)
         grad_mixture = jnp.einsum(
             "td,cd->tc", grad_attn, out_proj, preferred_element_type=f32
         ).astype(bf16)
         grad_queries, grad_keys, grad_values = run_attention_back(
-            queries, keys, values, grad_mixture, tables, block_ids, micro
+            queries, keys, values, hold(grad_mixture, before(grad_attn)), tables, block_ids, micro
         )
         grad_qkv = jnp.concatenate([grad_queries, grad_keys, grad_values], axis=1)
-        qkv_w = jnp.einsum("td,tc->dc", first_normed, grad_qkv, preferred_element_type=f32)
         grad_normed = jnp.einsum("tc,dc->td", grad_qkv, qkv_proj, preferred_element_type=f32)
         grad_source, grad_gain = norm_backward(grad_normed, tokens_in, first_recip, gain_first)
         return (
             grad_residual + grad_source,
-            out_w,
-            qkv_w,
+            grad_attn,
+            grad_qkv,
+            grad_logits,
+            gain_second_w,
             grad_gain,
-            gain_second_w,
-            router_w,
         )
 
     blend_rows = [(res_scale * cotan_seq[m]).astype(bf16) for m in range(2)]
     blend_blocks = [
         spread(hold(blend_rows[0], slot_blocks)),
-        spread(hold(blend_rows[1], first)),
+        spread(hold(blend_rows[1], slot_blocks)),
     ]
     blend0 = build(0, blend_blocks[0])
     moved_blend0 = exchange(blend0)
-    recip_first, normed_in, queries, keys, values, mixture = attend(hold(hidden, blend0))
+    recip_first, normed_in, queries, keys, values, mixture = attend(hold(hidden, blend0, blend_blocks[1]))
 
     def rows_of(value, micro):
         return value[micro * seq_len : (micro + 1) * seq_len]
@@ -612,15 +672,26 @@
     moved_scaled0 = exchange(hold(scaled0, moved_grads1, back0))
     back1 = sums_of(1, moved_grads1)
     result0 = attend_back(
-        0, hold(total_of(back0), back1[0]), [block[0] for block in pair_blocks], gates0
+        0,
+        hold(total_of(back0), back1[0]),
+        [block[0] for block in pair_blocks],
+        gates0,
+        lambda grad_attn: (),
     )
     moved_scaled1 = exchange(hold(scaled1, moved_scaled0, back1[1], result0))
     blend_back0 = sums_of(0, hold(moved_scaled0, result0))
+
+    def out_grads(grad_attn):
+        return run_weights(
+            mixture, jnp.concatenate([result0[1], grad_attn], axis=0), None, bf16
+        )
+
     result1 = attend_back(
         1,
-        hold(total_of(back1), result0, blend_back0[0]),
+        hold(total_of(back1), result0),
         [block[1] for block in pair_blocks],
         gates1,
+        lambda grad_attn: (moved_scaled0, blend_back0[0], out_grads(grad_attn)),
     )
     blend_back1 = sums_of(1, hold(moved_scaled1, result1))
     outputs = [
@@ -628,39 +699,39 @@
         after[1][0] + res_scale * total_of(blend_back1),
     ]
     token_grads_out = [result0[0], result1[0]]
-    out_w, qkv_w, gain_first_w, gain_second_w, router_w = (
-        a + b for a, b in zip(result0[1:], result1[1:], strict=True)
-    )
+    grad_qkv = jnp.concatenate([result0[2], result1[2]], axis=0)
+    out_w = out_grads(result1[1])
+    router_w = jnp.einsum(
+        "td,et->de",
+        jnp.concatenate([after[0][2], after[1][2]], axis=0),
+        jnp.concatenate([result0[3], result1[3]], axis=1),
+        preferred_element_type=f32,
+    )
+    gain_second_w = result0[4] + result1[4]
+    gain_first_w = result0[5] + result1[5]
     grad_gate_w, grad_up_w, grad_down_w = (
         a + b for a, b in zip(weights0, weights1, strict=True)
     )
 
-    small_w = jnp.concatenate([gain_second_w[:, None], router_w], axis=1)
+    small_w = jnp.concatenate([gain_first_w[:, None], gain_second_w[:, None], router_w], axis=1)
     small_w = jnp.pad(small_w, ((0, 0), (0, -small_w.shape[1] % 128)))
-    out_sum = lax.psum_scatter(
-        jnp.concatenate([out_w, small_w], axis=1).astype(bf16),
-        "dp",
-        scatter_dimension=0,
-        tiled=True,
-    ).astype(f32)
-    qkv_sum = lax.psum_scatter(
-        jnp.concatenate([qkv_w, jnp.pad(gain_first_w[:, None], ((0, 0), (0, 127)))], axis=1).astype(
-            bf16
-        ),
-        "dp",
-        scatter_dimension=0,
-        tiled=True,
-    ).astype(f32)
+    out_sum = lax.psum_scatter(out_w, "dp", scatter_dimension=0, tiled=True)
+    qkv_sum = reduce_rows(
+        run_weights(normed_in, grad_qkv, small_w, f32),
+        (blend_back0, moved_scaled1),
+        blend_back1[0],
+    )
+    out_sum = hold(out_sum, qkv_sum).astype(f32)
     return (
         jnp.concatenate(outputs, axis=0),
         jnp.concatenate(token_grads_out, axis=0),
         qkv_sum[:, qkv_width],
-        out_sum[:, model_width],
+        qkv_sum[:, qkv_width + 1],
         qkv_sum[:, :query_width],
         qkv_sum[:, query_width : query_width + kv_width],
         qkv_sum[:, query_width + kv_width : qkv_width],
-        out_sum[:, :model_width],
-        out_sum[:, model_width + 1 : model_width + 1 + experts],
+        out_sum,
+        qkv_sum[:, qkv_width + 2 : qkv_width + 2 + experts],
         grad_gate_w[None],
         grad_up_w[None],
         grad_down_w[None],

time: 1230 us -> 1150 us (0.935)
  waiting for transfers between devices: 633 us -> 558 us
  matrix products: 93.5 us -> 73 us
  Pallas kernels: 173 us -> 190 us
    ppermute x15, waiting for transfers between devices: 81.7 us -> 245 us  [give_back(): lax.ppermute(blocks[step], 'dp', line_shift(-step))]
    reduce_scatter x1, waiting for transfers between devices: 126 us -> 0.01 us  [on_device(): out_sum = lax.psum_scatter(out_w, 'dp', scatter_dimension=0, tiled=True)]
    all_to_all x9, waiting for transfers between devices: 140 us -> 62.6 us  [exchange(): lax.all_to_all(block, 'dp', split_axis=0, concat_axis=0, tiled=True, axis...]
    ppermute x15, waiting for transfers between devices: 265 us -> 227 us  [spread(): lax.ppermute(block, 'dp', line_shift(step))]
    ppermute x15, starting transfers between devices: 48.2 us -> 73.5 us  [spread(): lax.ppermute(block, 'dp', line_shift(step))]
    ppermute x0 -> x8, waiting for transfers between devices: none -> 22.8 us  [the longest x5 19.8 us: fold(): lax.ppermute(sent.astype(bf16), 'dp', [(i, i ^ bit) for i in range(device...]
    dot_general x6 -> x1, matrix products: 23.5 us -> 1.05 us  [on_device(): jnp.einsum('td,et->de', jnp.concatenate([after[0][2], after[1][2]], axis=...]
    all_to_all x9, starting transfers between devices: 67 us -> 47.4 us  [exchange(): lax.all_to_all(block, 'dp', split_axis=0, concat_axis=0, tiled=True, axis...]
  transfers between devices with their start and end apart: 43 -> 49, of which waited for: 19 -> 26; matrix products, arithmetic and copies ran while one was open for 13% -> 12% of each run, Pallas kernels for 14% -> 14%
where the time goes in v4:
time: 1150 us; the launch traced here: 1140 us
  waiting for transfers between devices  558 us (49%)
  Pallas kernels  190 us (17%)
  starting transfers between devices  187 us (16%)
  matrix products  73 us (6%)
  other arithmetic  60.3 us (5%)
  local copies, waits for them, and re-layouts  47.3 us (4%)
  between operations  15.6 us (1%)
    ppermute x15, waiting for transfers between devices, give_back(): lax.ppermute(blocks[step], 'dp', line_shift(-step))  245 us
    ppermute x15, waiting for transfers between devices, spread(): lax.ppermute(block, 'dp', line_shift(step))  227 us
    pallas_call x2, Pallas kernels, run_experts(): pl.pallas_call(expert_kernel, grid=(count // block,), in_specs=[wide, wid...  93.2 us
    ppermute x15, starting transfers between devices, spread(): lax.ppermute(block, 'dp', line_shift(step))  73.5 us
    all_to_all x9, waiting for transfers between devices, exchange(): lax.all_to_all(block, 'dp', split_axis=0, concat_axis=0, tiled=True, axis...  62.6 us
    ppermute x15, starting transfers between devices, give_back(): lax.ppermute(blocks[step], 'dp', line_shift(-step))  54.8 us
    all_to_all x9, starting transfers between devices, exchange(): lax.all_to_all(block, 'dp', split_axis=0, concat_axis=0, tiled=True, axis...  47.4 us
    pallas_call x2, Pallas kernels, run_attention_back(): pl.pallas_call(attend_back_kernel, grid=(1, KVH // 2), in_specs=[at(wide,...  33.7 us
  transfers between devices with their start and end apart: 49, of which 26 were waited for; matrix products, arithmetic and copies ran while one was open for 12% of the time, Pallas kernels for 14%

profile of v4, /device:TPU:0, one launch (start us, length us, event | category | flops | bytes accessed | tf_op | source)
XLA Modules:
  0.0 1139.8 jit_solution(6477590002461089591)
XLA Ops:
  35.1 21.7 %collective-permute-done.3.refs_1_ = bf16[256,1536]{1,0:T(8,128)(2,1)S(1)} collective-permute-done((bf16[256,1536]{1,0:T(8,128)(2,1)S(1)}, bf16[256,1536]{1,0:T(8,128)(2,1)S(1)}, u32[]{:S(2)}, u32[]{:S(2)}) %collective-permute-start.3) | collective-permute-done | bytes 786464 | tf_op jit(solution)/shard_map/ppermute | solution.py:435
  56.8 45.3 %collective-permute-done.4.refs_2_ = bf16[256,1536]{1,0:T(8,128)(2,1)S(1)} collective-permute-done((bf16[256,1536]{1,0:T(8,128)(2,1)S(1)}, bf16[256,1536]{1,0:T(8,128)(2,1)S(1)}, u32[]{:S(2)}, u32[]{:S(2)}) %collective-permute-start.4) | collective-permute-done | bytes 786464 | tf_op jit(solution)/shard_map/ppermute | solution.py:435
  115.1 22.3 %collective-permute-start.6 = (bf16[256,1536]{1,0:T(8,128)(2,1)}, bf16[256,1536]{1,0:T(8,128)(2,1)}, u32[]{:S(2)}, u32[]{:S(2)}) collective-permute-start(bf16[256,1536]{1,0:T(8,128)(2,1)} %get-tuple-element.64.refs_0_), channel_id=1, source_target_pairs={{0,8},{1,9},{2,10},{3,11},{4,12},{5,13},{6,14},{7,15},{8,16},{9,17... | collective-permute-start | bytes 2359304 | tf_op jit(solution)/shard_map/ppermute | solution.py:435
  145.8 27.5 %collective-permute-done.6.refs_1_ = bf16[256,1536]{1,0:T(8,128)(2,1)} collective-permute-done((bf16[256,1536]{1,0:T(8,128)(2,1)}, bf16[256,1536]{1,0:T(8,128)(2,1)}, u32[]{:S(2)}, u32[]{:S(2)}) %collective-permute-start.6) | collective-permute-done | bytes 786464 | tf_op jit(solution)/shard_map/ppermute | solution.py:435
  173.4 35.3 %collective-permute-done.7.refs_2_ = bf16[256,1536]{1,0:T(8,128)(2,1)} collective-permute-done((bf16[256,1536]{1,0:T(8,128)(2,1)}, bf16[256,1536]{1,0:T(8,128)(2,1)}, u32[]{:S(2)}, u32[]{:S(2)}) %collective-permute-start.7) | collective-permute-done | bytes 786464 | tf_op jit(solution)/shard_map/ppermute | solution.py:435
  221.2 18.7 %attention.1 = (bf16[512,1536]{1,0:T(8,128)(2,1)}, bf16[512,512]{1,0:T(8,128)(2,1)}, bf16[512,512]{1,0:T(8,128)(2,1)}, bf16[512,1536]{1,0:T(8,128)(2,1)}) custom-call(f32[512,2560]{1,0:T(8,128)} %fusion.14.query_ref.key_ref.value_ref, f32[512,2560]{1,0:T(8,128)} %fusion.14.query_ref.key_ref.value_ref, f32[512,2560]{1,0:T(8,128)} %fusion.14.query_ref.key_ref.value_ref, ...), custom_call_target="tpu_custom_call" | custom-call | flops 1000 | bytes 1000 | tf_op jit(solution)/shard_map/attention/pallas_call | solution.py:286
  281.9 31.9 %collective-permute-done.10.refs_2_ = bf16[256,1536]{1,0:T(8,128)(2,1)S(1)} collective-permute-done((bf16[256,1536]{1,0:T(8,128)(2,1)S(1)}, bf16[256,1536]{1,0:T(8,128)(2,1)S(1)}, u32[]{:S(2)}, u32[]{:S(2)}) %collective-permute-start.10) | collective-permute-done | bytes 786464 | tf_op jit(solution)/shard_map/ppermute | solution.py:435
  315.6 18.2 %collective-permute-done.9.refs_1_ = bf16[256,1536]{1,0:T(8,128)(2,1)} collective-permute-done((bf16[256,1536]{1,0:T(8,128)(2,1)S(1)}, bf16[256,1536]{1,0:T(8,128)(2,1)}, u32[]{:S(2)}, u32[]{:S(2)}) %collective-permute-start.9) | collective-permute-done | bytes 786464 | tf_op jit(solution)/shard_map/ppermute | solution.py:435
  345.4 15.0 %collective-permute-start.12 = (bf16[256,1536]{1,0:T(8,128)(2,1)}, bf16[256,1536]{1,0:T(8,128)(2,1)}, u32[]{:S(2)}, u32[]{:S(2)}) collective-permute-start(bf16[256,1536]{1,0:T(8,128)(2,1)} %get-tuple-element.222.refs_0_), channel_id=1, source_target_pairs={{0,8},{1,9},{2,10},{3,11},{4,12},{5,13},{6,14},{7,15},{8,16},{9,17... | collective-permute-start | bytes 2359304 | tf_op jit(solution)/shard_map/ppermute | solution.py:435
  378.7 28.9 %collective-permute-done.13.refs_2_ = bf16[256,1536]{1,0:T(8,128)(2,1)} collective-permute-done((bf16[256,1536]{1,0:T(8,128)(2,1)}, bf16[256,1536]{1,0:T(8,128)(2,1)}, u32[]{:S(2)}, u32[]{:S(2)}) %collective-permute-start.13) | collective-permute-done | bytes 786464 | tf_op jit(solution)/shard_map/ppermute | solution.py:435
  442.8 46.6 %experts.2 = (bf16[2304,1536]{1,0:T(8,128)(2,1)}, bf16[2304,1536]{1,0:T(8,128)(2,1)}, f32[2304,1]{1,0:T(8,128)}, f32[1536,512]{1,0:T(8,128)}, f32[1536,512]{1,0:T(8,128)}, /*index=5*/f32[512,1536]{1,0:T(8,128)}) custom-call(bf16[2304,1536]{1,0:T(8,128)(2,1)} %bitcast.18.rows_ref, bf16[2304,1536]{1,0:T(8,128)(2,1)} %bitcast.19.blend_ref, ...), custom_call_target="tpu_custom_call" | custom-call | flops 1000 | bytes 1000 | tf_op jit(solution)/shard_map/experts/pallas_call | solution.py:105
  489.4 31.3 %all-to-all-done.4 = bf16[8,288,1536]{2,1,0:T(8,128)(2,1)} async-done(((bf16[8,288,1536]{2,1,0:T(8,128)(2,1)}), bf16[8,288,1536]{2,1,0:T(8,128)(2,1)}, u32[]{:S(2)}, u32[]{:S(2)}) %all-to-all-start.4) | async-done | bytes 7077920 | tf_op jit(solution)/shard_map/all_to_all | solution.py:478
  530.3 46.6 %experts.3 = (bf16[2304,1536]{1,0:T(8,128)(2,1)}, bf16[2304,1536]{1,0:T(8,128)(2,1)}, f32[2304,1]{1,0:T(8,128)}, f32[1536,512]{1,0:T(8,128)}, f32[1536,512]{1,0:T(8,128)}, /*index=5*/f32[512,1536]{1,0:T(8,128)}) custom-call(bf16[2304,1536]{1,0:T(8,128)(2,1)} %bitcast.39.rows_ref, bf16[2304,1536]{1,0:T(8,128)(2,1)} %bitcast.40.blend_ref, ...), custom_call_target="tpu_custom_call" | custom-call | flops 1000 | bytes 1000 | tf_op jit(solution)/shard_map/experts/pallas_call | solution.py:105
  578.7 27.2 %all-to-all-done.5 = bf16[8,288,1536]{2,1,0:T(8,128)(2,1)} async-done(((bf16[8,288,1536]{2,1,0:T(8,128)(2,1)}), bf16[8,288,1536]{2,1,0:T(8,128)(2,1)}, u32[]{:S(2)}, u32[]{:S(2)}) %all-to-all-start.5) | async-done | bytes 7077920 | tf_op jit(solution)/shard_map/all_to_all | solution.py:478
  627.4 21.5 %collective-permute-start.15 = (bf16[256,1536]{1,0:T(8,128)(2,1)}, bf16[256,1536]{1,0:T(8,128)(2,1)}, u32[]{:S(2)}, u32[]{:S(2)}) collective-permute-start(bf16[256,1536]{1,0:T(8,128)(2,1)} %get-tuple-element.200), channel_id=1, source_target_pairs={{0,24},{1,25},{2,26},{3,27},{4,28},{5,29},{6,30},{7,31},{8,0},{9,1... | collective-permute-start | bytes 2359304 | tf_op jit(solution)/shard_map/ppermute | solution.py:440
  655.8 45.0 %collective-permute-done.18 = f32[2,8,256]{2,1,0:T(8,128)S(1)} collective-permute-done((f32[2,8,256]{2,1,0:T(8,128)S(1)}, f32[2,8,256]{2,1,0:T(8,128)S(1)}, u32[]{:S(2)}, u32[]{:S(2)}) %collective-permute-start.18) | collective-permute-done | bytes 16416 | tf_op jit(solution)/shard_map/ppermute | solution.py:440
  700.8 17.1 %collective-permute-start.20 = (f32[2,8,256]{2,1,0:T(8,128)S(1)}, f32[2,8,256]{2,1,0:T(8,128)S(1)}, u32[]{:S(2)}, u32[]{:S(2)}) collective-permute-start(f32[2,8,256]{2,1,0:T(8,128)S(1)} %get-tuple-element.212), channel_id=1, source_target_pairs={{0,8},{1,9},{2,10},{3,11},{4,12},{5,13},{6,14},{7,15},{8,16},{9,17... | collective-permute-start | bytes 49160 | tf_op jit(solution)/shard_map/ppermute | solution.py:440
  730.5 16.9 %attention_back.2 = (bf16[256,1536]{1,0:T(8,128)(2,1)}, bf16[256,512]{1,0:T(8,128)(2,1)}, bf16[256,512]{1,0:T(8,128)(2,1)}) custom-call(bf16[512,1536]{1,0:T(8,128)(2,1)} %get-tuple-element.83.query_ref, bf16[512,512]{1,0:T(8,128)(2,1)} %get-tuple-element.84.key_ref, bf16[512,512]{1,0:T(8,128)(2,1)} %get-tuple-element.85.value_ref, ...), custom_call_target="tpu_custom_call" | custom-call | flops 1000 | bytes 1000 | tf_op jit(solution)/shard_map/attention_back/pallas_call | solution.py:325
  770.6 14.6 %collective-permute-done.24 = bf16[256,1536]{1,0:T(8,128)(2,1)S(1)} collective-permute-done((bf16[256,1536]{1,0:T(8,128)(2,1)S(1)}, bf16[256,1536]{1,0:T(8,128)(2,1)S(1)}, u32[]{:S(2)}, u32[]{:S(2)}) %collective-permute-start.24) | collective-permute-done | bytes 786464 | tf_op jit(solution)/shard_map/ppermute | solution.py:440
  785.2 51.7 %collective-permute-done.25 = bf16[256,1536]{1,0:T(8,128)(2,1)S(1)} collective-permute-done((bf16[256,1536]{1,0:T(8,128)(2,1)S(1)}, bf16[256,1536]{1,0:T(8,128)(2,1)S(1)}, u32[]{:S(2)}, u32[]{:S(2)}) %collective-permute-start.25) | collective-permute-done | bytes 786464 | tf_op jit(solution)/shard_map/ppermute | solution.py:440
  865.2 16.8 %attention_back.3 = (bf16[256,1536]{1,0:T(8,128)(2,1)}, bf16[256,512]{1,0:T(8,128)(2,1)}, bf16[256,512]{1,0:T(8,128)(2,1)}) custom-call(bf16[512,1536]{1,0:T(8,128)(2,1)} %get-tuple-element.83.query_ref, bf16[512,512]{1,0:T(8,128)(2,1)} %get-tuple-element.84.key_ref, bf16[512,512]{1,0:T(8,128)(2,1)} %get-tuple-element.85.value_ref, ...), custom_call_target="tpu_custom_call" | custom-call | flops 1000 | bytes 1000 | tf_op jit(solution)/shard_map/attention_back/pallas_call | solution.py:325
  950.5 56.3 %collective-permute-done.22 = bf16[256,1536]{1,0:T(8,128)(2,1)} collective-permute-done((bf16[256,1536]{1,0:T(8,128)(2,1)}, bf16[256,1536]{1,0:T(8,128)(2,1)}, u32[]{:S(2)}, u32[]{:S(2)}) %collective-permute-start.22) | collective-permute-done | bytes 786464 | tf_op jit(solution)/shard_map/ppermute | solution.py:440
  1010.2 15.4 %collective-permute-done.31 = bf16[4,2,48,1280]{3,2,1,0:T(8,128)(2,1)S(1)} collective-permute-done((bf16[4,2,48,1280]{3,2,1,0:T(8,128)(2,1)S(1)}, bf16[4,2,48,1280]{3,2,1,0:T(8,128)(2,1)S(1)}, u32[]{:S(2)}, u32[]{:S(2)}) %collective-permute-start.31) | collective-permute-done | bytes 983072 | tf_op jit(solution)/shard_map/ppermute | solution.py:459
  1060.1 62.4 %collective-permute-done.28 = bf16[256,1536]{1,0:T(8,128)(2,1)S(1)} collective-permute-done((bf16[256,1536]{1,0:T(8,128)(2,1)S(1)}, bf16[256,1536]{1,0:T(8,128)(2,1)S(1)}, u32[]{:S(2)}, u32[]{:S(2)}) %collective-permute-start.28) | collective-permute-done | bytes 786464 | tf_op jit(solution)/shard_map/ppermute | solution.py:440
  (368 shorter events, 389.9 us)
Async XLA Ops:
  7.2 201.9 %all-gather.2.cloned.1.call-start = ((), (), s32[]{:S(2)}) async-start(), calls=%async_computation.11 | async-start | bytes 13381632 | tf_op jit(solution)/shard_map/all_gather | solution.py:484
  30.3 71.8 %collective-permute-start.4 = (bf16[256,1536]{1,0:T(8,128)(2,1)S(1)}, bf16[256,1536]{1,0:T(8,128)(2,1)S(1)}, u32[]{:S(2)}, u32[]{:S(2)}) collective-permute-start(bf16[256,1536]{1,0:T(8,128)(2,1)S(1)} %get-tuple-element.60.refs_0_), channel_id=1, source_target_pairs={{0,16},{1,17},{2,18},{3,19},{4,20},{5,21},{6,22},{7,23},{8,24},{9,... | collective-permute-start | bytes 2359304 | tf_op jit(solution)/shard_map/ppermute | solution.py:435
  110.0 136.7 %all-to-all-start = ((bf16[8,288,1536]{2,1,0:T(8,128)(2,1)}), bf16[8,288,1536]{2,1,0:T(8,128)(2,1)}, u32[]{:S(2)}, u32[]{:S(2)}) async-start(bf16[8,288,1536]{2,1,0:T(8,128)(2,1)} %bitcast.230), calls=%async_computation | async-start | bytes 14155776 | tf_op jit(solution)/shard_map/all_to_all | solution.py:478
  137.4 71.4 %collective-permute-start.7 = (bf16[256,1536]{1,0:T(8,128)(2,1)}, bf16[256,1536]{1,0:T(8,128)(2,1)}, u32[]{:S(2)}, u32[]{:S(2)}) collective-permute-start(bf16[256,1536]{1,0:T(8,128)(2,1)} %get-tuple-element.64.refs_0_), channel_id=1, source_target_pairs={{0,16},{1,17},{2,18},{3,19},{4,20},{5,21},{6,22},{7,23},{8,24},{9,... | collective-permute-start | bytes 2359304 | tf_op jit(solution)/shard_map/ppermute | solution.py:435
  246.6 93.8 %all-to-all-start.1 = ((bf16[8,288,1536]{2,1,0:T(8,128)(2,1)}), bf16[8,288,1536]{2,1,0:T(8,128)(2,1)}, u32[]{:S(2)}, u32[]{:S(2)}) async-start(bf16[8,288,1536]{2,1,0:T(8,128)(2,1)} %bitcast.232), calls=%async_computation.1 | async-start | bytes 14155776 | tf_op jit(solution)/shard_map/all_to_all | solution.py:478
  340.5 86.5 %all-to-all-start.2 = ((bf16[8,288,1536]{2,1,0:T(8,128)(2,1)}), bf16[8,288,1536]{2,1,0:T(8,128)(2,1)}, u32[]{:S(2)}, u32[]{:S(2)}) async-start(bf16[8,288,1536]{2,1,0:T(8,128)(2,1)} %bitcast.229), calls=%async_computation.2 | async-start | bytes 14155776 | tf_op jit(solution)/shard_map/all_to_all | solution.py:478
  435.4 85.3 %all-to-all-start.4 = ((bf16[8,288,1536]{2,1,0:T(8,128)(2,1)}), bf16[8,288,1536]{2,1,0:T(8,128)(2,1)}, u32[]{:S(2)}, u32[]{:S(2)}) async-start(bf16[8,288,1536]{2,1,0:T(8,128)(2,1)} %bitcast.231), calls=%async_computation.4 | async-start | bytes 14155776 | tf_op jit(solution)/shard_map/all_to_all | solution.py:478
  520.7 85.2 %all-to-all-start.5 = ((bf16[8,288,1536]{2,1,0:T(8,128)(2,1)}), bf16[8,288,1536]{2,1,0:T(8,128)(2,1)}, u32[]{:S(2)}, u32[]{:S(2)}) async-start(bf16[8,288,1536]{2,1,0:T(8,128)(2,1)} %bitcast.236), calls=%async_computation.5 | async-start | bytes 14155776 | tf_op jit(solution)/shard_map/all_to_all | solution.py:478
  614.5 132.8 %all-to-all-start.7 = ((bf16[8,288,1536]{2,1,0:T(8,128)(2,1)}), bf16[8,288,1536]{2,1,0:T(8,128)(2,1)}, u32[]{:S(2)}, u32[]{:S(2)}) async-start(bf16[8,288,1536]{2,1,0:T(8,128)(2,1)} %bitcast.235), calls=%async_computation.7 | async-start | bytes 14155776 | tf_op jit(solution)/shard_map/all_to_all | solution.py:478
  627.4 92.1 %collective-permute-start.15 = (bf16[256,1536]{1,0:T(8,128)(2,1)}, bf16[256,1536]{1,0:T(8,128)(2,1)}, u32[]{:S(2)}, u32[]{:S(2)}) collective-permute-start(bf16[256,1536]{1,0:T(8,128)(2,1)} %get-tuple-element.200), channel_id=1, source_target_pairs={{0,24},{1,25},{2,26},{3,27},{4,28},{5,29},{6,30},{7,31},{8,0},{9,1... | collective-permute-start | bytes 2359304 | tf_op jit(solution)/shard_map/ppermute | solution.py:440
  648.9 70.6 %collective-permute-start.16 = (bf16[256,1536]{1,0:T(8,128)(2,1)}, bf16[256,1536]{1,0:T(8,128)(2,1)}, u32[]{:S(2)}, u32[]{:S(2)}) collective-permute-start(bf16[256,1536]{1,0:T(8,128)(2,1)} %get-tuple-element.199), channel_id=1, source_target_pairs={{0,16},{1,17},{2,18},{3,19},{4,20},{5,21},{6,22},{7,23},{8,24},{9,... | collective-permute-start | bytes 2359304 | tf_op jit(solution)/shard_map/ppermute | solution.py:440
  648.9 70.6 %collective-permute-start.17 = (bf16[256,1536]{1,0:T(8,128)(2,1)}, bf16[256,1536]{1,0:T(8,128)(2,1)}, u32[]{:S(2)}, u32[]{:S(2)}) collective-permute-start(bf16[256,1536]{1,0:T(8,128)(2,1)} %get-tuple-element.198), channel_id=1, source_target_pairs={{0,8},{1,9},{2,10},{3,11},{4,12},{5,13},{6,14},{7,15},{8,16},{9,17... | collective-permute-start | bytes 2359304 | tf_op jit(solution)/shard_map/ppermute | solution.py:440
  747.4 109.1 %all-to-all-start.8 = ((bf16[8,288,1536]{2,1,0:T(8,128)(2,1)}), bf16[8,288,1536]{2,1,0:T(8,128)(2,1)}, u32[]{:S(2)}, u32[]{:S(2)}) async-start(bf16[8,288,1536]{2,1,0:T(8,128)(2,1)} %bitcast.234), calls=%async_computation.8 | async-start | bytes 14155776 | tf_op jit(solution)/shard_map/all_to_all | solution.py:478
  912.3 115.7 %all-to-all-start.9 = ((bf16[8,288,1536]{2,1,0:T(8,128)(2,1)}), bf16[8,288,1536]{2,1,0:T(8,128)(2,1)}, u32[]{:S(2)}, u32[]{:S(2)}) async-start(bf16[8,288,1536]{2,1,0:T(8,128)(2,1)} %bitcast.233), calls=%async_computation.9 | async-start | bytes 14155776 | tf_op jit(solution)/shard_map/all_to_all | solution.py:478
  917.2 213.2 %reduce-scatter.2.cloned.1.call-start = ((), (), s32[]{:S(2)}) async-start(), calls=%async_computation.12 | async-start | bytes 4866048 | tf_op jit(solution)/shard_map/reduce_scatter | solution.py:718
  929.1 77.8 %collective-permute-start.22 = (bf16[256,1536]{1,0:T(8,128)(2,1)}, bf16[256,1536]{1,0:T(8,128)(2,1)}, u32[]{:S(2)}, u32[]{:S(2)}) collective-permute-start(bf16[256,1536]{1,0:T(8,128)(2,1)} %get-tuple-element.190), channel_id=1, source_target_pairs={{0,16},{1,17},{2,18},{3,19},{4,20},{5,21},{6,22},{7,23},{8,24},{9,... | collective-permute-start | bytes 2359304 | tf_op jit(solution)/shard_map/ppermute | solution.py:440
  930.4 76.5 %collective-permute-start.23 = (bf16[256,1536]{1,0:T(8,128)(2,1)}, bf16[256,1536]{1,0:T(8,128)(2,1)}, u32[]{:S(2)}, u32[]{:S(2)}) collective-permute-start(bf16[256,1536]{1,0:T(8,128)(2,1)} %get-tuple-element.189), channel_id=1, source_target_pairs={{0,8},{1,9},{2,10},{3,11},{4,12},{5,13},{6,14},{7,15},{8,16},{9,17... | collective-permute-start | bytes 2359304 | tf_op jit(solution)/shard_map/ppermute | solution.py:440
  941.0 84.6 %collective-permute-start.31 = (bf16[4,2,48,1280]{3,2,1,0:T(8,128)(2,1)S(1)}, bf16[4,2,48,1280]{3,2,1,0:T(8,128)(2,1)S(1)}, u32[]{:S(2)}, u32[]{:S(2)}) collective-permute-start(bf16[4,2,48,1280]{3,2,1,0:T(8,128)(2,1)S(1)} %fusion.94), channel_id=1, source_target_pairs={{0,4},{1,5},{2,6},{3,7},{4,0},{5,1},{6,2},{7,3},{8,12},{9,13},{10,... | collective-permute-start | bytes 2949128 | tf_op jit(solution)/shard_map/ppermute | solution.py:459
  945.3 82.6 %collective-permute-start.32 = (bf16[4,2,48,1408]{3,2,1,0:T(8,128)(2,1)S(1)}, bf16[4,2,48,1408]{3,2,1,0:T(8,128)(2,1)S(1)}, u32[]{:S(2)}, u32[]{:S(2)}) collective-permute-start(bf16[4,2,48,1408]{3,2,1,0:T(8,128)(2,1)S(1)} %fusion.93), channel_id=1, source_target_pairs={{0,2},{1,3},{2,0},{3,1},{4,6},{5,7},{6,4},{7,5},{8,10},{9,11},{10,... | collective-permute-start | bytes 3244040 | tf_op jit(solution)/shard_map/ppermute | solution.py:459
  1037.4 85.1 %collective-permute-start.28 = (bf16[256,1536]{1,0:T(8,128)(2,1)S(1)}, bf16[256,1536]{1,0:T(8,128)(2,1)S(1)}, u32[]{:S(2)}, u32[]{:S(2)}) collective-permute-start(bf16[256,1536]{1,0:T(8,128)(2,1)S(1)} %get-tuple-element.194), channel_id=1, source_target_pairs={{0,16},{1,17},{2,18},{3,19},{4,20},{5,21},{6,22},{7,23},{8,24},{9,... | collective-permute-start | bytes 2359304 | tf_op jit(solution)/shard_map/ppermute | solution.py:440
  1038.8 83.8 %collective-permute-start.29 = (bf16[256,1536]{1,0:T(8,128)(2,1)S(1)}, bf16[256,1536]{1,0:T(8,128)(2,1)S(1)}, u32[]{:S(2)}, u32[]{:S(2)}) collective-permute-start(bf16[256,1536]{1,0:T(8,128)(2,1)S(1)} %get-tuple-element.193), channel_id=1, source_target_pairs={{0,8},{1,9},{2,10},{3,11},{4,12},{5,13},{6,14},{7,15},{8,16},{9,17... | collective-permute-start | bytes 2359304 | tf_op jit(solution)/shard_map/ppermute | solution.py:440
  1044.8 80.2 %collective-permute-start.35 = (bf16[48,2688]{1,0:T(8,128)(2,1)S(1)}, bf16[48,2688]{1,0:T(8,128)(2,1)S(1)}, u32[]{:S(2)}, u32[]{:S(2)}) collective-permute-start(bf16[48,2688]{1,0:T(8,128)(2,1)S(1)} %get-tuple-element.203), channel_id=1, source_target_pairs={{0,8},{1,9},{2,10},{3,11},{4,12},{5,13},{6,14},{7,15},{8,16},{9,17... | collective-permute-start | bytes 774152 | tf_op jit(solution)/shard_map/ppermute | solution.py:473
  1046.3 81.8 %collective-permute-start.36 = (bf16[48,2688]{1,0:T(8,128)(2,1)S(1)}, bf16[48,2688]{1,0:T(8,128)(2,1)S(1)}, u32[]{:S(2)}, u32[]{:S(2)}) collective-permute-start(bf16[48,2688]{1,0:T(8,128)(2,1)S(1)} %get-tuple-element.205), channel_id=1, source_target_pairs={{0,16},{1,17},{2,18},{3,19},{4,20},{5,21},{6,22},{7,23},{8,24},{9,... | collective-permute-start | bytes 774152 | tf_op jit(solution)/shard_map/ppermute | solution.py:473
  1057.4 70.7 %collective-permute-start.37 = (bf16[48,2688]{1,0:T(8,128)(2,1)S(1)}, bf16[48,2688]{1,0:T(8,128)(2,1)S(1)}, u32[]{:S(2)}, u32[]{:S(2)}) collective-permute-start(bf16[48,2688]{1,0:T(8,128)(2,1)S(1)} %get-tuple-element.204), channel_id=1, source_target_pairs={{0,24},{1,25},{2,26},{3,27},{4,28},{5,29},{6,30},{7,31},{8,0},{9,1... | collective-permute-start | bytes 774152 | tf_op jit(solution)/shard_map/ppermute | solution.py:473
  (88 other events, 1889.6 us)
Sparse Core Ops, SparseCore 0:
  14.0 192.1 all-gather.1
  929.2 179.7 reduce-scatter.1

commit v5 on v4

--- a/solution.py
+++ b/solution.py
@@ -597,7 +597,7 @@
         both = jnp.stack(token_grads, axis=1)
         return give_back([both[step] for step in range(LINES)])
 
-    def attend_back(micro, grad_mid_sum, pair_blocks, gates, before):
+    def attend_back(micro, grad_mid_sum, pair_blocks, gates, before, then):
         tokens_in = hidden_seq[micro]
         cotan_in = cotan_seq[micro]
         residual, recip_second, normed_mid = after[micro]
@@ -623,7 +623,7 @@
         grad_queries, grad_keys, grad_values = run_attention_back(
             queries, keys, values, hold(grad_mixture, before(grad_attn)), tables, block_ids, micro
         )
-        grad_qkv = jnp.concatenate([grad_queries, grad_keys, grad_values], axis=1)
+        grad_qkv = hold(jnp.concatenate([grad_queries, grad_keys, grad_values], axis=1), then)
         grad_normed = jnp.einsum("tc,dc->td", grad_qkv, qkv_proj, preferred_element_type=f32)
         grad_source, grad_gain = norm_backward(grad_normed, tokens_in, first_recip, gain_first)
         return (
@@ -669,14 +669,15 @@
     moved_grads1 = exchange(hold(grads1, pair_back))
     pair_blocks = pairs_home(pair_back)
     back0 = sums_of(0, moved_grads0)
-    moved_scaled0 = exchange(hold(scaled0, moved_grads1, back0))
+    moved_scaled0 = exchange(hold(scaled0, moved_grads1))
     back1 = sums_of(1, moved_grads1)
     result0 = attend_back(
         0,
         hold(total_of(back0), back1[0]),
         [block[0] for block in pair_blocks],
         gates0,
-        lambda grad_attn: (),
+        lambda grad_attn: (moved_grads1, back1[0]),
+        (),
     )
     moved_scaled1 = exchange(hold(scaled1, moved_scaled0, back1[1], result0))
     blend_back0 = sums_of(0, hold(moved_scaled0, result0))
@@ -692,6 +693,7 @@
         [block[1] for block in pair_blocks],
         gates1,
         lambda grad_attn: (moved_scaled0, blend_back0[0], out_grads(grad_attn)),
+        blend_back0,
     )
     blend_back1 = sums_of(1, hold(moved_scaled1, result1))
     outputs = [
@@ -717,8 +719,8 @@
     small_w = jnp.pad(small_w, ((0, 0), (0, -small_w.shape[1] % 128)))
     out_sum = lax.psum_scatter(out_w, "dp", scatter_dimension=0, tiled=True)
     qkv_sum = reduce_rows(
-        run_weights(normed_in, grad_qkv, small_w, f32),
-        (blend_back0, moved_scaled1),
+        run_weights(normed_in, hold(grad_qkv, moved_scaled1), small_w, f32),
+        blend_back0,
         blend_back1[0],
     )
     out_sum = hold(out_sum, qkv_sum).astype(f32)

time: 1150 us -> 1110 us (0.965)
  waiting for transfers between devices: 558 us -> 500 us
    ppermute x15, waiting for transfers between devices: 245 us -> 138 us  [give_back(): lax.ppermute(blocks[step], 'dp', line_shift(-step))]
    all_to_all x9 -> x8, waiting for transfers between devices: 62.6 us -> 91 us  [exchange(): lax.all_to_all(block, 'dp', split_axis=0, concat_axis=0, tiled=True, axis...]
    ppermute x15, starting transfers between devices: 54.8 us -> 66.6 us  [give_back(): lax.ppermute(blocks[step], 'dp', line_shift(-step))]
    all_to_all x9 -> x8, starting transfers between devices: 47.4 us -> 42.2 us  [exchange(): lax.all_to_all(block, 'dp', split_axis=0, concat_axis=0, tiled=True, axis...]
  transfers between devices with their start and end apart: 49 -> 48, of which waited for: 26 -> 23; matrix products, arithmetic and copies ran while one was open for 12% -> 14% of each run, Pallas kernels for 14% -> 16%
where the time goes in v5:
time: 1110 us; the launch traced here: 1100 us
  waiting for transfers between devices  500 us (45%)
  starting transfers between devices  196 us (18%)
  Pallas kernels  191 us (17%)
  matrix products  73 us (7%)
  other arithmetic  64.2 us (6%)
  local copies, waits for them, and re-layouts  45.7 us (4%)
  between operations  15.9 us (1%)
  blocking collectives  15.6 us (1%)
    ppermute x15, waiting for transfers between devices, spread(): lax.ppermute(block, 'dp', line_shift(step))  228 us
    ppermute x15, waiting for transfers between devices, give_back(): lax.ppermute(blocks[step], 'dp', line_shift(-step))  138 us
    pallas_call x2, Pallas kernels, run_experts(): pl.pallas_call(expert_kernel, grid=(count // block,), in_specs=[wide, wid...  93.2 us
    all_to_all x8, waiting for transfers between devices, exchange(): lax.all_to_all(block, 'dp', split_axis=0, concat_axis=0, tiled=True, axis...  91 us
    ppermute x15, starting transfers between devices, spread(): lax.ppermute(block, 'dp', line_shift(step))  74.9 us
    ppermute x15, starting transfers between devices, give_back(): lax.ppermute(blocks[step], 'dp', line_shift(-step))  66.6 us
    all_to_all x8, starting transfers between devices, exchange(): lax.all_to_all(block, 'dp', split_axis=0, concat_axis=0, tiled=True, axis...  42.2 us
    pallas_call x2, Pallas kernels, run_attention_back(): pl.pallas_call(attend_back_kernel, grid=(1, KVH // 2), in_specs=[at(wide,...  33.7 us
  transfers between devices with their start and end apart: 48, of which 23 were waited for; matrix products, arithmetic and copies ran while one was open for 14% of the time, Pallas kernels for 16%

profile of v5, /device:TPU:0, one launch (start us, length us, event | category | flops | bytes accessed | tf_op | source)
XLA Modules:
  0.0 1101.0 jit_solution(17217347852794450625)
XLA Ops:
  38.7 19.3 %collective-permute-done.3.refs_1_ = bf16[256,1536]{1,0:T(8,128)(2,1)S(1)} collective-permute-done((bf16[256,1536]{1,0:T(8,128)(2,1)S(1)}, bf16[256,1536]{1,0:T(8,128)(2,1)S(1)}, u32[]{:S(2)}, u32[]{:S(2)}) %collective-permute-start.3) | collective-permute-done | bytes 786464 | tf_op jit(solution)/shard_map/ppermute | solution.py:435
  58.1 44.6 %collective-permute-done.4.refs_2_ = bf16[256,1536]{1,0:T(8,128)(2,1)S(1)} collective-permute-done((bf16[256,1536]{1,0:T(8,128)(2,1)S(1)}, bf16[256,1536]{1,0:T(8,128)(2,1)S(1)}, u32[]{:S(2)}, u32[]{:S(2)}) %collective-permute-start.4) | collective-permute-done | bytes 786464 | tf_op jit(solution)/shard_map/ppermute | solution.py:435
  115.7 22.1 %collective-permute-start.6 = (bf16[256,1536]{1,0:T(8,128)(2,1)}, bf16[256,1536]{1,0:T(8,128)(2,1)}, u32[]{:S(2)}, u32[]{:S(2)}) collective-permute-start(bf16[256,1536]{1,0:T(8,128)(2,1)} %get-tuple-element.67.refs_0_), channel_id=1, source_target_pairs={{0,8},{1,9},{2,10},{3,11},{4,12},{5,13},{6,14},{7,15},{8,16},{9,17... | collective-permute-start | bytes 2359304 | tf_op jit(solution)/shard_map/ppermute | solution.py:435
  145.8 27.3 %collective-permute-done.6.refs_1_ = bf16[256,1536]{1,0:T(8,128)(2,1)} collective-permute-done((bf16[256,1536]{1,0:T(8,128)(2,1)}, bf16[256,1536]{1,0:T(8,128)(2,1)}, u32[]{:S(2)}, u32[]{:S(2)}) %collective-permute-start.6) | collective-permute-done | bytes 786464 | tf_op jit(solution)/shard_map/ppermute | solution.py:435
  173.0 38.1 %collective-permute-done.7.refs_2_ = bf16[256,1536]{1,0:T(8,128)(2,1)} collective-permute-done((bf16[256,1536]{1,0:T(8,128)(2,1)}, bf16[256,1536]{1,0:T(8,128)(2,1)}, u32[]{:S(2)}, u32[]{:S(2)}) %collective-permute-start.7) | collective-permute-done | bytes 786464 | tf_op jit(solution)/shard_map/ppermute | solution.py:435
  223.7 18.7 %attention.1 = (bf16[512,1536]{1,0:T(8,128)(2,1)}, bf16[512,512]{1,0:T(8,128)(2,1)}, bf16[512,512]{1,0:T(8,128)(2,1)}, bf16[512,1536]{1,0:T(8,128)(2,1)}) custom-call(f32[512,2560]{1,0:T(8,128)} %fusion.14.query_ref.key_ref.value_ref, f32[512,2560]{1,0:T(8,128)} %fusion.14.query_ref.key_ref.value_ref, f32[512,2560]{1,0:T(8,128)} %fusion.14.query_ref.key_ref.value_ref, ...), custom_call_target="tpu_custom_call" | custom-call | flops 1000 | bytes 1000 | tf_op jit(solution)/shard_map/attention/pallas_call | solution.py:286
  267.0 14.2 %collective-permute-start.10 = (bf16[256,1536]{1,0:T(8,128)(2,1)S(1)}, bf16[256,1536]{1,0:T(8,128)(2,1)S(1)}, u32[]{:S(2)}, u32[]{:S(2)}) collective-permute-start(bf16[256,1536]{1,0:T(8,128)(2,1)S(1)} %get-tuple-element.228.refs_0_), channel_id=1, source_target_pairs={{0,16},{1,17},{2,18},{3,19},{4,20},{5,21},{6,22},{7,23},{8,24},{9,... | collective-permute-start | bytes 2359304 | tf_op jit(solution)/shard_map/ppermute | solution.py:435
  284.5 31.9 %collective-permute-done.10.refs_2_ = bf16[256,1536]{1,0:T(8,128)(2,1)S(1)} collective-permute-done((bf16[256,1536]{1,0:T(8,128)(2,1)S(1)}, bf16[256,1536]{1,0:T(8,128)(2,1)S(1)}, u32[]{:S(2)}, u32[]{:S(2)}) %collective-permute-start.10) | collective-permute-done | bytes 786464 | tf_op jit(solution)/shard_map/ppermute | solution.py:435
  318.1 18.2 %collective-permute-done.9.refs_1_ = bf16[256,1536]{1,0:T(8,128)(2,1)} collective-permute-done((bf16[256,1536]{1,0:T(8,128)(2,1)S(1)}, bf16[256,1536]{1,0:T(8,128)(2,1)}, u32[]{:S(2)}, u32[]{:S(2)}) %collective-permute-start.9) | collective-permute-done | bytes 786464 | tf_op jit(solution)/shard_map/ppermute | solution.py:435
  348.1 15.0 %collective-permute-start.12 = (bf16[256,1536]{1,0:T(8,128)(2,1)}, bf16[256,1536]{1,0:T(8,128)(2,1)}, u32[]{:S(2)}, u32[]{:S(2)}) collective-permute-start(bf16[256,1536]{1,0:T(8,128)(2,1)} %get-tuple-element.229.refs_0_), channel_id=1, source_target_pairs={{0,8},{1,9},{2,10},{3,11},{4,12},{5,13},{6,14},{7,15},{8,16},{9,17... | collective-permute-start | bytes 2359304 | tf_op jit(solution)/shard_map/ppermute | solution.py:435
  368.0 13.3 %collective-permute-done.12.refs_1_ = bf16[256,1536]{1,0:T(8,128)(2,1)} collective-permute-done((bf16[256,1536]{1,0:T(8,128)(2,1)}, bf16[256,1536]{1,0:T(8,128)(2,1)}, u32[]{:S(2)}, u32[]{:S(2)}) %collective-permute-start.12) | collective-permute-done | bytes 786464 | tf_op jit(solution)/shard_map/ppermute | solution.py:435
  381.3 28.3 %collective-permute-done.13.refs_2_ = bf16[256,1536]{1,0:T(8,128)(2,1)} collective-permute-done((bf16[256,1536]{1,0:T(8,128)(2,1)}, bf16[256,1536]{1,0:T(8,128)(2,1)}, u32[]{:S(2)}, u32[]{:S(2)}) %collective-permute-start.13) | collective-permute-done | bytes 786464 | tf_op jit(solution)/shard_map/ppermute | solution.py:435
  445.3 46.6 %experts.2 = (bf16[2304,1536]{1,0:T(8,128)(2,1)}, bf16[2304,1536]{1,0:T(8,128)(2,1)}, f32[2304,1]{1,0:T(8,128)}, f32[1536,512]{1,0:T(8,128)}, f32[1536,512]{1,0:T(8,128)}, /*index=5*/f32[512,1536]{1,0:T(8,128)}) custom-call(bf16[2304,1536]{1,0:T(8,128)(2,1)} %bitcast.18.rows_ref, bf16[2304,1536]{1,0:T(8,128)(2,1)} %bitcast.19.blend_ref, ...), custom_call_target="tpu_custom_call" | custom-call | flops 1000 | bytes 1000 | tf_op jit(solution)/shard_map/experts/pallas_call | solution.py:105
  491.9 31.3 %all-to-all-done.4 = bf16[8,288,1536]{2,1,0:T(8,128)(2,1)} async-done(((bf16[8,288,1536]{2,1,0:T(8,128)(2,1)}), bf16[8,288,1536]{2,1,0:T(8,128)(2,1)}, u32[]{:S(2)}, u32[]{:S(2)}) %all-to-all-start.4) | async-done | bytes 7077920 | tf_op jit(solution)/shard_map/all_to_all | solution.py:478
  532.1 46.6 %experts.3 = (bf16[2304,1536]{1,0:T(8,128)(2,1)}, bf16[2304,1536]{1,0:T(8,128)(2,1)}, f32[2304,1]{1,0:T(8,128)}, f32[1536,512]{1,0:T(8,128)}, f32[1536,512]{1,0:T(8,128)}, /*index=5*/f32[512,1536]{1,0:T(8,128)}) custom-call(bf16[2304,1536]{1,0:T(8,128)(2,1)} %bitcast.39.rows_ref, bf16[2304,1536]{1,0:T(8,128)(2,1)} %bitcast.40.blend_ref, ...), custom_call_target="tpu_custom_call" | custom-call | flops 1000 | bytes 1000 | tf_op jit(solution)/shard_map/experts/pallas_call | solution.py:105
  580.4 27.9 %all-to-all-done.5 = bf16[8,288,1536]{2,1,0:T(8,128)(2,1)} async-done(((bf16[8,288,1536]{2,1,0:T(8,128)(2,1)}), bf16[8,288,1536]{2,1,0:T(8,128)(2,1)}, u32[]{:S(2)}, u32[]{:S(2)}) %all-to-all-start.5) | async-done | bytes 7077920 | tf_op jit(solution)/shard_map/all_to_all | solution.py:478
  629.8 21.5 %collective-permute-start.15 = (bf16[256,1536]{1,0:T(8,128)(2,1)}, bf16[256,1536]{1,0:T(8,128)(2,1)}, u32[]{:S(2)}, u32[]{:S(2)}) collective-permute-start(bf16[256,1536]{1,0:T(8,128)(2,1)} %get-tuple-element.205), channel_id=1, source_target_pairs={{0,24},{1,25},{2,26},{3,27},{4,28},{5,29},{6,30},{7,31},{8,0},{9,1... | collective-permute-start | bytes 2359304 | tf_op jit(solution)/shard_map/ppermute | solution.py:440
  669.9 33.1 %collective-permute-done.18 = f32[2,8,256]{2,1,0:T(8,128)S(1)} collective-permute-done((f32[2,8,256]{2,1,0:T(8,128)S(1)}, f32[2,8,256]{2,1,0:T(8,128)S(1)}, u32[]{:S(2)}, u32[]{:S(2)}) %collective-permute-start.18) | collective-permute-done | bytes 16416 | tf_op jit(solution)/shard_map/ppermute | solution.py:440
  703.0 17.1 %collective-permute-start.20 = (f32[2,8,256]{2,1,0:T(8,128)S(1)}, f32[2,8,256]{2,1,0:T(8,128)S(1)}, u32[]{:S(2)}, u32[]{:S(2)}) collective-permute-start(f32[2,8,256]{2,1,0:T(8,128)S(1)} %get-tuple-element.219), channel_id=1, source_target_pairs={{0,8},{1,9},{2,10},{3,11},{4,12},{5,13},{6,14},{7,15},{8,16},{9,17... | collective-permute-start | bytes 49160 | tf_op jit(solution)/shard_map/ppermute | solution.py:440
  749.8 16.9 %attention_back.2 = (bf16[256,1536]{1,0:T(8,128)(2,1)}, bf16[256,512]{1,0:T(8,128)(2,1)}, bf16[256,512]{1,0:T(8,128)(2,1)}) custom-call(bf16[512,1536]{1,0:T(8,128)(2,1)} %get-tuple-element.86.query_ref, bf16[512,512]{1,0:T(8,128)(2,1)} %get-tuple-element.87.key_ref, bf16[512,512]{1,0:T(8,128)(2,1)} %get-tuple-element.88.value_ref, ...), custom_call_target="tpu_custom_call" | custom-call | flops 1000 | bytes 1000 | tf_op jit(solution)/shard_map/attention_back/pallas_call | solution.py:325
  775.1 31.9 %all-to-all-done.8 = bf16[8,288,1536]{2,1,0:T(8,128)(2,1)} async-done(((bf16[8,288,1536]{2,1,0:T(8,128)(2,1)}), bf16[8,288,1536]{2,1,0:T(8,128)(2,1)}, u32[]{:S(2)}, u32[]{:S(2)}) %all-to-all-start.8) | async-done | bytes 7077920 | tf_op jit(solution)/shard_map/all_to_all | solution.py:478
  845.4 16.9 %attention_back.3 = (bf16[256,1536]{1,0:T(8,128)(2,1)}, bf16[256,512]{1,0:T(8,128)(2,1)}, bf16[256,512]{1,0:T(8,128)(2,1)}) custom-call(bf16[512,1536]{1,0:T(8,128)(2,1)} %get-tuple-element.86.query_ref, bf16[512,512]{1,0:T(8,128)(2,1)} %get-tuple-element.87.key_ref, bf16[512,512]{1,0:T(8,128)(2,1)} %get-tuple-element.88.value_ref, ...), custom_call_target="tpu_custom_call" | custom-call | flops 1000 | bytes 1000 | tf_op jit(solution)/shard_map/attention_back/pallas_call | solution.py:325
  863.7 45.7 %collective-permute-done.22 = bf16[256,1536]{1,0:T(8,128)(2,1)} collective-permute-done((bf16[256,1536]{1,0:T(8,128)(2,1)}, bf16[256,1536]{1,0:T(8,128)(2,1)}, u32[]{:S(2)}, u32[]{:S(2)}) %collective-permute-start.22) | collective-permute-done | bytes 786464 | tf_op jit(solution)/shard_map/ppermute | solution.py:440
  1000.0 57.8 %collective-permute-done.28 = bf16[256,1536]{1,0:T(8,128)(2,1)S(1)} collective-permute-done((bf16[256,1536]{1,0:T(8,128)(2,1)S(1)}, bf16[256,1536]{1,0:T(8,128)(2,1)S(1)}, u32[]{:S(2)}, u32[]{:S(2)}) %collective-permute-start.28) | collective-permute-done | bytes 786464 | tf_op jit(solution)/shard_map/ppermute | solution.py:440
  (373 shorter events, 400.8 us)
Async XLA Ops:
  7.2 204.3 %all-gather.2.cloned.1.call-start = ((), (), s32[]{:S(2)}) async-start(), calls=%async_computation.11 | async-start | bytes 13381632 | tf_op jit(solution)/shard_map/all_gather | solution.py:484
  35.7 67.0 %collective-permute-start.4 = (bf16[256,1536]{1,0:T(8,128)(2,1)S(1)}, bf16[256,1536]{1,0:T(8,128)(2,1)S(1)}, u32[]{:S(2)}, u32[]{:S(2)}) collective-permute-start(bf16[256,1536]{1,0:T(8,128)(2,1)S(1)} %get-tuple-element.63.refs_0_), channel_id=1, source_target_pairs={{0,16},{1,17},{2,18},{3,19},{4,20},{5,21},{6,22},{7,23},{8,24},{9,... | collective-permute-start | bytes 2359304 | tf_op jit(solution)/shard_map/ppermute | solution.py:435
  36.9 65.9 %collective-permute-start.5 = (bf16[256,1536]{1,0:T(8,128)(2,1)S(1)}, bf16[256,1536]{1,0:T(8,128)(2,1)S(1)}, u32[]{:S(2)}, u32[]{:S(2)}) collective-permute-start(bf16[256,1536]{1,0:T(8,128)(2,1)S(1)} %get-tuple-element.63.refs_0_), channel_id=1, source_target_pairs={{0,24},{1,25},{2,26},{3,27},{4,28},{5,29},{6,30},{7,31},{8,0},{9,1... | collective-permute-start | bytes 2359304 | tf_op jit(solution)/shard_map/ppermute | solution.py:435
  110.6 138.6 %all-to-all-start = ((bf16[8,288,1536]{2,1,0:T(8,128)(2,1)}), bf16[8,288,1536]{2,1,0:T(8,128)(2,1)}, u32[]{:S(2)}, u32[]{:S(2)}) async-start(bf16[8,288,1536]{2,1,0:T(8,128)(2,1)} %bitcast.231), calls=%async_computation | async-start | bytes 14155776 | tf_op jit(solution)/shard_map/all_to_all | solution.py:478
  137.8 73.3 %collective-permute-start.7 = (bf16[256,1536]{1,0:T(8,128)(2,1)}, bf16[256,1536]{1,0:T(8,128)(2,1)}, u32[]{:S(2)}, u32[]{:S(2)}) collective-permute-start(bf16[256,1536]{1,0:T(8,128)(2,1)} %get-tuple-element.67.refs_0_), channel_id=1, source_target_pairs={{0,16},{1,17},{2,18},{3,19},{4,20},{5,21},{6,22},{7,23},{8,24},{9,... | collective-permute-start | bytes 2359304 | tf_op jit(solution)/shard_map/ppermute | solution.py:435
  140.4 70.7 %collective-permute-start.8 = (bf16[256,1536]{1,0:T(8,128)(2,1)}, bf16[256,1536]{1,0:T(8,128)(2,1)}, u32[]{:S(2)}, u32[]{:S(2)}) collective-permute-start(bf16[256,1536]{1,0:T(8,128)(2,1)} %get-tuple-element.67.refs_0_), channel_id=1, source_target_pairs={{0,24},{1,25},{2,26},{3,27},{4,28},{5,29},{6,30},{7,31},{8,0},{9,1... | collective-permute-start | bytes 2359304 | tf_op jit(solution)/shard_map/ppermute | solution.py:435
  249.2 94.0 %all-to-all-start.1 = ((bf16[8,288,1536]{2,1,0:T(8,128)(2,1)}), bf16[8,288,1536]{2,1,0:T(8,128)(2,1)}, u32[]{:S(2)}, u32[]{:S(2)}) async-start(bf16[8,288,1536]{2,1,0:T(8,128)(2,1)} %bitcast.233), calls=%async_computation.1 | async-start | bytes 14155776 | tf_op jit(solution)/shard_map/all_to_all | solution.py:478
  343.1 86.5 %all-to-all-start.2 = ((bf16[8,288,1536]{2,1,0:T(8,128)(2,1)}), bf16[8,288,1536]{2,1,0:T(8,128)(2,1)}, u32[]{:S(2)}, u32[]{:S(2)}) async-start(bf16[8,288,1536]{2,1,0:T(8,128)(2,1)} %bitcast.230), calls=%async_computation.2 | async-start | bytes 14155776 | tf_op jit(solution)/shard_map/all_to_all | solution.py:478
  438.1 85.1 %all-to-all-start.4 = ((bf16[8,288,1536]{2,1,0:T(8,128)(2,1)}), bf16[8,288,1536]{2,1,0:T(8,128)(2,1)}, u32[]{:S(2)}, u32[]{:S(2)}) async-start(bf16[8,288,1536]{2,1,0:T(8,128)(2,1)} %bitcast.232), calls=%async_computation.4 | async-start | bytes 14155776 | tf_op jit(solution)/shard_map/all_to_all | solution.py:478
  523.2 85.1 %all-to-all-start.5 = ((bf16[8,288,1536]{2,1,0:T(8,128)(2,1)}), bf16[8,288,1536]{2,1,0:T(8,128)(2,1)}, u32[]{:S(2)}, u32[]{:S(2)}) async-start(bf16[8,288,1536]{2,1,0:T(8,128)(2,1)} %bitcast.237), calls=%async_computation.5 | async-start | bytes 14155776 | tf_op jit(solution)/shard_map/all_to_all | solution.py:478
  615.5 106.7 %all-to-all-start.7 = ((bf16[8,288,1536]{2,1,0:T(8,128)(2,1)}), bf16[8,288,1536]{2,1,0:T(8,128)(2,1)}, u32[]{:S(2)}, u32[]{:S(2)}) async-start(bf16[8,288,1536]{2,1,0:T(8,128)(2,1)} %bitcast.236), calls=%async_computation.7 | async-start | bytes 14155776 | tf_op jit(solution)/shard_map/all_to_all | solution.py:478
  629.8 97.3 %collective-permute-start.15 = (bf16[256,1536]{1,0:T(8,128)(2,1)}, bf16[256,1536]{1,0:T(8,128)(2,1)}, u32[]{:S(2)}, u32[]{:S(2)}) collective-permute-start(bf16[256,1536]{1,0:T(8,128)(2,1)} %get-tuple-element.205), channel_id=1, source_target_pairs={{0,24},{1,25},{2,26},{3,27},{4,28},{5,29},{6,30},{7,31},{8,0},{9,1... | collective-permute-start | bytes 2359304 | tf_op jit(solution)/shard_map/ppermute | solution.py:440
  651.3 75.7 %collective-permute-start.16 = (bf16[256,1536]{1,0:T(8,128)(2,1)}, bf16[256,1536]{1,0:T(8,128)(2,1)}, u32[]{:S(2)}, u32[]{:S(2)}) collective-permute-start(bf16[256,1536]{1,0:T(8,128)(2,1)} %get-tuple-element.207), channel_id=1, source_target_pairs={{0,16},{1,17},{2,18},{3,19},{4,20},{5,21},{6,22},{7,23},{8,24},{9,... | collective-permute-start | bytes 2359304 | tf_op jit(solution)/shard_map/ppermute | solution.py:440
  651.3 75.8 %collective-permute-start.17 = (bf16[256,1536]{1,0:T(8,128)(2,1)}, bf16[256,1536]{1,0:T(8,128)(2,1)}, u32[]{:S(2)}, u32[]{:S(2)}) collective-permute-start(bf16[256,1536]{1,0:T(8,128)(2,1)} %get-tuple-element.206), channel_id=1, source_target_pairs={{0,8},{1,9},{2,10},{3,11},{4,12},{5,13},{6,14},{7,15},{8,16},{9,17... | collective-permute-start | bytes 2359304 | tf_op jit(solution)/shard_map/ppermute | solution.py:440
  722.2 84.8 %all-to-all-start.8 = ((bf16[8,288,1536]{2,1,0:T(8,128)(2,1)}), bf16[8,288,1536]{2,1,0:T(8,128)(2,1)}, u32[]{:S(2)}, u32[]{:S(2)}) async-start(bf16[8,288,1536]{2,1,0:T(8,128)(2,1)} %bitcast.235), calls=%async_computation.8 | async-start | bytes 14155776 | tf_op jit(solution)/shard_map/all_to_all | solution.py:478
  739.7 72.4 %collective-permute-start.25 = (bf16[256,1536]{1,0:T(8,128)(2,1)}, bf16[256,1536]{1,0:T(8,128)(2,1)}, u32[]{:S(2)}, u32[]{:S(2)}) collective-permute-start(bf16[256,1536]{1,0:T(8,128)(2,1)} %get-tuple-element.201), channel_id=1, source_target_pairs={{0,16},{1,17},{2,18},{3,19},{4,20},{5,21},{6,22},{7,23},{8,24},{9,... | collective-permute-start | bytes 2359304 | tf_op jit(solution)/shard_map/ppermute | solution.py:440
  741.1 70.9 %collective-permute-start.26 = (bf16[256,1536]{1,0:T(8,128)(2,1)}, bf16[256,1536]{1,0:T(8,128)(2,1)}, u32[]{:S(2)}, u32[]{:S(2)}) collective-permute-start(bf16[256,1536]{1,0:T(8,128)(2,1)} %get-tuple-element.202), channel_id=1, source_target_pairs={{0,8},{1,9},{2,10},{3,11},{4,12},{5,13},{6,14},{7,15},{8,16},{9,17... | collective-permute-start | bytes 2359304 | tf_op jit(solution)/shard_map/ppermute | solution.py:440
  807.0 115.5 %all-to-all-start.9 = ((bf16[8,288,1536]{2,1,0:T(8,128)(2,1)}), bf16[8,288,1536]{2,1,0:T(8,128)(2,1)}, u32[]{:S(2)}, u32[]{:S(2)}) async-start(bf16[8,288,1536]{2,1,0:T(8,128)(2,1)} %bitcast.234), calls=%async_computation.9 | async-start | bytes 14155776 | tf_op jit(solution)/shard_map/all_to_all | solution.py:478
  812.0 279.5 %reduce-scatter.2.cloned.1.call-start = ((), (), s32[]{:S(2)}) async-start(), calls=%async_computation.12 | async-start | bytes 4866048 | tf_op jit(solution)/shard_map/reduce_scatter | solution.py:720
  839.4 70.0 %collective-permute-start.22 = (bf16[256,1536]{1,0:T(8,128)(2,1)}, bf16[256,1536]{1,0:T(8,128)(2,1)}, u32[]{:S(2)}, u32[]{:S(2)}) collective-permute-start(bf16[256,1536]{1,0:T(8,128)(2,1)} %get-tuple-element.198), channel_id=1, source_target_pairs={{0,16},{1,17},{2,18},{3,19},{4,20},{5,21},{6,22},{7,23},{8,24},{9,... | collective-permute-start | bytes 2359304 | tf_op jit(solution)/shard_map/ppermute | solution.py:440
  840.8 68.6 %collective-permute-start.23 = (bf16[256,1536]{1,0:T(8,128)(2,1)}, bf16[256,1536]{1,0:T(8,128)(2,1)}, u32[]{:S(2)}, u32[]{:S(2)}) collective-permute-start(bf16[256,1536]{1,0:T(8,128)(2,1)} %get-tuple-element.197), channel_id=1, source_target_pairs={{0,8},{1,9},{2,10},{3,11},{4,12},{5,13},{6,14},{7,15},{8,16},{9,17... | collective-permute-start | bytes 2359304 | tf_op jit(solution)/shard_map/ppermute | solution.py:440
  973.1 84.7 %collective-permute-start.28 = (bf16[256,1536]{1,0:T(8,128)(2,1)S(1)}, bf16[256,1536]{1,0:T(8,128)(2,1)S(1)}, u32[]{:S(2)}, u32[]{:S(2)}) collective-permute-start(bf16[256,1536]{1,0:T(8,128)(2,1)S(1)} %get-tuple-element.196), channel_id=1, source_target_pairs={{0,16},{1,17},{2,18},{3,19},{4,20},{5,21},{6,22},{7,23},{8,24},{9,... | collective-permute-start | bytes 2359304 | tf_op jit(solution)/shard_map/ppermute | solution.py:440
  974.5 83.4 %collective-permute-start.29 = (bf16[256,1536]{1,0:T(8,128)(2,1)S(1)}, bf16[256,1536]{1,0:T(8,128)(2,1)S(1)}, u32[]{:S(2)}, u32[]{:S(2)}) collective-permute-start(bf16[256,1536]{1,0:T(8,128)(2,1)S(1)} %get-tuple-element.195), channel_id=1, source_target_pairs={{0,8},{1,9},{2,10},{3,11},{4,12},{5,13},{6,14},{7,15},{8,16},{9,17... | collective-permute-start | bytes 2359304 | tf_op jit(solution)/shard_map/ppermute | solution.py:440
  997.7 60.6 %collective-permute-start.33 = (bf16[4,48,1280]{2,1,0:T(8,128)(2,1)S(1)}, bf16[4,48,1280]{2,1,0:T(8,128)(2,1)S(1)}, u32[]{:S(2)}, u32[]{:S(2)}) collective-permute-start(bf16[4,48,1280]{2,1,0:T(8,128)(2,1)S(1)} %fusion.103), channel_id=1, source_target_pairs={{0,2},{1,3},{2,0},{3,1},{4,6},{5,7},{6,4},{7,5},{8,10},{9,11},{10,... | collective-permute-start | bytes 1474568 | tf_op jit(solution)/shard_map/ppermute | solution.py:459
  (92 other events, 1576.9 us)
Sparse Core Ops, SparseCore 0:
  14.0 194.4 all-gather.1
  949.8 141.6 reduce-scatter.1

commit v6 on v4

--- a/solution.py
+++ b/solution.py
@@ -24,14 +24,6 @@
 
 
 LINES = 4
-
-
-def norm_backward(grad_normed, source, recip, gain):
-    scaled_grad = grad_normed * gain
-    grad_source = recip * scaled_grad - source * (recip * recip * recip) * jnp.mean(
-        scaled_grad * source, axis=1, keepdims=True
-    )
-    return (grad_source, jnp.sum(grad_normed * source * recip, axis=0))
 
 
 def masked_gates(logits, routed):
@@ -389,6 +381,100 @@
     )(*operands)
 
 
+def sums_kernel(slots_ref, rows_ref, *out_refs):
+    plane, lines, capacity, width = rows_ref.shape
+    for line in range(lines):
+        slots = slots_ref[line]
+        places = lax.broadcasted_iota(jnp.int32, (plane, capacity, slots.shape[1]), 1)
+        picks = jnp.where(slots[:, None, :] == places, 1.0, 0.0)
+        rows = rows_ref[:, line].astype(jnp.float32).reshape(plane * capacity, width)
+        out_refs[line][...] = head_product(
+            picks.reshape(plane * capacity, slots.shape[1]).astype(jnp.bfloat16),
+            rows.astype(jnp.bfloat16),
+            0,
+            0,
+        ).astype(jnp.bfloat16)
+
+
+def sum_rows(slots, rows):
+    lines, unused, tokens = slots.shape
+    return pl.pallas_call(
+        sums_kernel,
+        out_shape=[jax.ShapeDtypeStruct((tokens, rows.shape[3]), rows.dtype)] * lines,
+        cost_estimate=pl.CostEstimate(flops=1000, bytes_accessed=1000, transcendentals=0),
+        name="sum_rows",
+    )(slots, rows)
+
+
+def norm_grads(grad_normed, source, recip, gain):
+    scaled = grad_normed * gain
+    centre = jnp.mean(scaled * source, axis=1, keepdims=True)
+    grad_source = recip * scaled - source * (recip * recip * recip) * centre
+    return grad_source, jnp.sum(grad_normed * source * recip, axis=0, keepdims=True)
+
+
+def middle_kernel(*refs):
+    parts = refs[:LINES]
+    logits_ref, router_ref, residual_ref, recip_ref, gain_ref, cotan_ref, proj_ref = refs[LINES:-4]
+    residual_out, attn_out, mixture_out, gain_out = refs[-4:]
+    bf16 = jnp.bfloat16
+    grad_mid = head_product(logits_ref[...], router_ref[...], 0, 1)
+    for part in parts:
+        grad_mid = grad_mid + part[...].astype(jnp.float32)
+    grad_source, grad_gain = norm_grads(
+        grad_mid, residual_ref[...], recip_ref[...], gain_ref[...]
+    )
+    grad_residual = cotan_ref[...] + grad_source
+    grad_attn = (res_scale * grad_residual).astype(bf16)
+    residual_out[...] = grad_residual
+    attn_out[...] = grad_attn
+    mixture_out[...] = head_product(grad_attn, proj_ref[...], 1, 1).astype(bf16)
+    gain_out[...] = grad_gain
+
+
+def run_middle(parts, grad_logits, router, residual, recip, gain, cotangent, out_proj):
+    tokens, width = residual.shape
+    shape = jax.ShapeDtypeStruct
+    return pl.pallas_call(
+        middle_kernel,
+        out_shape=[
+            shape((tokens, width), jnp.float32),
+            shape((tokens, width), jnp.bfloat16),
+            shape((tokens, out_proj.shape[0]), jnp.bfloat16),
+            shape((1, width), jnp.float32),
+        ],
+        cost_estimate=pl.CostEstimate(flops=1000, bytes_accessed=1000, transcendentals=0),
+        name="middle_back",
+    )(*parts, grad_logits, router, residual, recip, gain[None], cotangent, out_proj)
+
+
+def first_kernel(
+    query_ref, key_ref, value_ref, proj_ref, tokens_ref, recip_ref, gain_ref, residual_ref,
+    out_ref, gain_out,
+):
+    start = 0
+    grad_normed = 0.0
+    for ref in (query_ref, key_ref, value_ref):
+        stop = start + ref.shape[1]
+        grad_normed = grad_normed + head_product(ref[...], proj_ref[:, start:stop], 1, 1)
+        start = stop
+    grad_source, grad_gain = norm_grads(
+        grad_normed, tokens_ref[...], recip_ref[...], gain_ref[...]
+    )
+    out_ref[...] = residual_ref[...] + grad_source
+    gain_out[...] = grad_gain
+
+
+def run_first(queries, keys, values, qkv_proj, tokens, recip, gain, grad_residual):
+    shape = jax.ShapeDtypeStruct
+    return pl.pallas_call(
+        first_kernel,
+        out_shape=[shape(tokens.shape, jnp.float32), shape((1, tokens.shape[1]), jnp.float32)],
+        cost_estimate=pl.CostEstimate(flops=1000, bytes_accessed=1000, transcendentals=0),
+        name="first_back",
+    )(queries, keys, values, qkv_proj, tokens, recip, gain[None], grad_residual)
+
+
 def on_device(
     hidden,
     cotangent,
@@ -443,7 +529,7 @@
     def hold(value, *after):
         return lax.optimization_barrier((value, after))[0]
 
-    def reduce_rows(value, early, late):
+    def reduce_rows(value, first, early, late):
         if plane != 8:
             return lax.psum_scatter(
                 value.astype(bf16), "dp", scatter_dimension=0, tiled=True
@@ -461,12 +547,13 @@
             )
             return kept + other.astype(f32)
 
-        block = fold(value.reshape(LINES, 2, 2, 2, rows, value.shape[1]), 3, 1)
+        value = hold(value, first)
+        block = hold(fold(value.reshape(LINES, 2, 2, 2, rows, value.shape[1]), 3, 1), early)
         left, right = block[..., :half], block[..., half:]
         left, right = fold(left, 1, 4), fold(right, 2, 2)
-        left, right = hold((left, right), early)
+        left, right = hold((left, right), late)
         left, right = fold(left, 1, 2), fold(right, 1, 4)
-        block = hold(jnp.concatenate([left, right], axis=2), late)
+        block = jnp.concatenate([left, right], axis=2)
         total = lax.dynamic_index_in_dim(block, here, 0, keepdims=False)
         for step in range(1, LINES):
             sent = lax.dynamic_index_in_dim(block, (here + step) % LINES, 0, keepdims=False)
@@ -527,11 +614,11 @@
         return rows.reshape(plane, LINES * capacity, model_width)
 
     def sums_of(micro, arrived):
+        arrived = arrived.reshape(plane, LINES, capacity, model_width)
+        if capacity % 8 == 0:
+            return give_back(sum_rows(slots_here[:, micro], arrived))
         sums = jnp.einsum(
-            "ject,ejcd->jtd",
-            picks[micro],
-            arrived.reshape(plane, LINES, capacity, model_width),
-            preferred_element_type=f32,
+            "ject,ejcd->jtd", picks[micro], arrived, preferred_element_type=f32
         ).astype(bf16)
         return give_back([sums[step] for step in range(LINES)])
 
@@ -597,11 +684,8 @@
         both = jnp.stack(token_grads, axis=1)
         return give_back([both[step] for step in range(LINES)])
 
-    def attend_back(micro, grad_mid_sum, pair_blocks, gates, before):
-        tokens_in = hidden_seq[micro]
-        cotan_in = cotan_seq[micro]
-        residual, recip_second, normed_mid = after[micro]
-        first_recip = rows_of(recip_first, micro)
+    def attend_back(micro, parts, pair_blocks, gates, before, then):
+        residual, recip_second, unused = after[micro]
         pair_grads = jnp.zeros((experts, seq_len), f32)
         for step in range(LINES):
             pair_grads = lax.dynamic_update_slice_in_dim(
@@ -610,29 +694,34 @@
         grad_logits = (
             gates * (pair_grads - jnp.sum(gates * pair_grads, axis=0, keepdims=True))
         ).astype(bf16)
-        grad_mid = grad_mid_sum + jnp.einsum(
-            "et,de->td", grad_logits, router, preferred_element_type=f32
-        )
-        grad_residual, grad_gain = norm_backward(grad_mid, residual, recip_second, gain_second)
-        gain_second_w = grad_gain
-        grad_residual = cotan_in + grad_residual
-        grad_attn = (res_scale * grad_residual).astype(bf16)
-        grad_mixture = jnp.einsum(
-            "td,cd->tc", grad_attn, out_proj, preferred_element_type=f32
-        ).astype(bf16)
-        grad_queries, grad_keys, grad_values = run_attention_back(
+        grad_residual, grad_attn, grad_mixture, gain_second_w = run_middle(
+            parts,
+            grad_logits,
+            router,
+            residual,
+            recip_second,
+            gain_second,
+            cotan_seq[micro],
+            out_proj,
+        )
+        grads = run_attention_back(
             queries, keys, values, hold(grad_mixture, before(grad_attn)), tables, block_ids, micro
         )
-        grad_qkv = jnp.concatenate([grad_queries, grad_keys, grad_values], axis=1)
-        grad_normed = jnp.einsum("tc,dc->td", grad_qkv, qkv_proj, preferred_element_type=f32)
-        grad_source, grad_gain = norm_backward(grad_normed, tokens_in, first_recip, gain_first)
+        grad_tokens, gain_first_w = run_first(
+            *hold(grads, then),
+            qkv_proj,
+            hidden_seq[micro],
+            rows_of(recip_first, micro),
+            gain_first,
+            grad_residual,
+        )
         return (
-            grad_residual + grad_source,
+            grad_tokens,
             grad_attn,
-            grad_qkv,
+            jnp.concatenate(grads, axis=1),
             grad_logits,
             gain_second_w,
-            grad_gain,
+            gain_first_w,
         )
 
     blend_rows = [(res_scale * cotan_seq[m]).astype(bf16) for m in range(2)]
@@ -673,12 +762,13 @@
     back1 = sums_of(1, moved_grads1)
     result0 = attend_back(
         0,
-        hold(total_of(back0), back1[0]),
+        hold(back0, back1[0]),
         [block[0] for block in pair_blocks],
         gates0,
-        lambda grad_attn: (),
-    )
-    moved_scaled1 = exchange(hold(scaled1, moved_scaled0, back1[1], result0))
+        lambda grad_attn: (moved_grads1, back1[0]),
+        (),
+    )
+    moved_scaled1 = exchange(hold(scaled1, moved_scaled0, back1, result0))
     blend_back0 = sums_of(0, hold(moved_scaled0, result0))
 
     def out_grads(grad_attn):
@@ -688,10 +778,11 @@
 
     result1 = attend_back(
         1,
-        hold(total_of(back1), result0),
+        hold(back1, result0),
         [block[1] for block in pair_blocks],
         gates1,
         lambda grad_attn: (moved_scaled0, blend_back0[0], out_grads(grad_attn)),
+        (),
     )
     blend_back1 = sums_of(1, hold(moved_scaled1, result1))
     outputs = [
@@ -707,8 +798,8 @@
         jnp.concatenate([result0[3], result1[3]], axis=1),
         preferred_element_type=f32,
     )
-    gain_second_w = result0[4] + result1[4]
-    gain_first_w = result0[5] + result1[5]
+    gain_second_w = (result0[4] + result1[4])[0]
+    gain_first_w = (result0[5] + result1[5])[0]
     grad_gate_w, grad_up_w, grad_down_w = (
         a + b for a, b in zip(weights0, weights1, strict=True)
     )
@@ -720,6 +811,7 @@
         run_weights(normed_in, grad_qkv, small_w, f32),
         (blend_back0, moved_scaled1),
         blend_back1[0],
+        blend_back1,
     )
     out_sum = hold(out_sum, qkv_sum).astype(f32)
     return (

time: 1150 us -> 1150 us (level)
  Pallas kernels: 190 us -> 249 us
  matrix products: 73 us -> 24.8 us
  starting transfers between devices: 187 us -> 169 us
    pallas_call x0 -> x8, Pallas kernels: none -> 59.1 us  [the longest x4 26.3 us: sum_rows(): pl.pallas_call(sums_kernel, out_shape=[jax.ShapeDtypeStruct((tokens, rows...]
    dot_general x10 -> x0, matrix products: 48.2 us -> none  [the longest x4 22.6 us: sums_of(): jnp.einsum('ject,ejcd->jtd', picks[micro], arrived.reshape(plane, LINES,...]
    ppermute x15, waiting for transfers between devices: 245 us -> 216 us  [give_back(): lax.ppermute(blocks[step], 'dp', line_shift(-step))]
    ppermute x5, waiting for transfers between devices: 19.8 us -> 35.5 us  [fold(): lax.ppermute(sent.astype(bf16), 'dp', [(i, i ^ bit) for i in range(device...]
    slice x0 -> x4, local copies, waits for them, and re-layouts: none -> 15.4 us  [the longest x1 6.83 us: on_device(): qkv_proj = shared[:, :qkv_width]]
    ppermute x15, starting transfers between devices: 54.8 us -> 39.5 us  [give_back(): lax.ppermute(blocks[step], 'dp', line_shift(-step))]
    all_to_all x9 -> x8, starting transfers between devices: 47.4 us -> 42.3 us  [exchange(): lax.all_to_all(block, 'dp', split_axis=0, concat_axis=0, tiled=True, axis...]
    all_to_all x9 -> x8, waiting for transfers between devices: 62.6 us -> 59.1 us  [exchange(): lax.all_to_all(block, 'dp', split_axis=0, concat_axis=0, tiled=True, axis...]
  transfers between devices with their start and end apart: 49 -> 48, of which waited for: 26 -> 28; matrix products, arithmetic and copies ran while one was open for 12% -> 10% of each run, Pallas kernels for 14% -> 22%
where the time goes in v6:
time: 1150 us; the launch traced here: 1140 us
  waiting for transfers between devices  559 us (49%)
  Pallas kernels  249 us (22%)
  starting transfers between devices  169 us (15%)
  local copies, waits for them, and re-layouts  53.5 us (5%)
  other arithmetic  51.3 us (4%)
  matrix products  24.8 us (2%)
  blocking collectives  15.6 us (1%)
  between operations  15.6 us (1%)
    ppermute x15, waiting for transfers between devices, spread(): lax.ppermute(block, 'dp', line_shift(step))  228 us
    ppermute x15, waiting for transfers between devices, give_back(): lax.ppermute(blocks[step], 'dp', line_shift(-step))  216 us
    pallas_call x2, Pallas kernels, run_experts(): pl.pallas_call(expert_kernel, grid=(count // block,), in_specs=[wide, wid...  93.2 us
    ppermute x15, starting transfers between devices, spread(): lax.ppermute(block, 'dp', line_shift(step))  74.5 us
    all_to_all x8, waiting for transfers between devices, exchange(): lax.all_to_all(block, 'dp', split_axis=0, concat_axis=0, tiled=True, axis...  59.1 us
    all_to_all x8, starting transfers between devices, exchange(): lax.all_to_all(block, 'dp', split_axis=0, concat_axis=0, tiled=True, axis...  42.3 us
    ppermute x15, starting transfers between devices, give_back(): lax.ppermute(blocks[step], 'dp', line_shift(-step))  39.5 us
    ppermute x5, waiting for transfers between devices, fold(): lax.ppermute(sent.astype(bf16), 'dp', [(i, i ^ bit) for i in range(device...  35.5 us
  transfers between devices with their start and end apart: 48, of which 28 were waited for; matrix products, arithmetic and copies ran while one was open for 10% of the time, Pallas kernels for 22%

profile of v6, /device:TPU:0, one launch (start us, length us, event | category | flops | bytes accessed | tf_op | source)
XLA Modules:
  0.0 1138.1 jit_solution(15233946600427564020)
XLA Ops:
  38.1 20.0 %collective-permute-done.3.refs_1_ = bf16[256,1536]{1,0:T(8,128)(2,1)S(1)} collective-permute-done((bf16[256,1536]{1,0:T(8,128)(2,1)S(1)}, bf16[256,1536]{1,0:T(8,128)(2,1)S(1)}, u32[]{:S(2)}, u32[]{:S(2)}) %collective-permute-start.3) | collective-permute-done | bytes 786464 | tf_op jit(solution)/shard_map/ppermute | solution.py:521
  58.1 44.5 %collective-permute-done.4.refs_2_ = bf16[256,1536]{1,0:T(8,128)(2,1)S(1)} collective-permute-done((bf16[256,1536]{1,0:T(8,128)(2,1)S(1)}, bf16[256,1536]{1,0:T(8,128)(2,1)S(1)}, u32[]{:S(2)}, u32[]{:S(2)}) %collective-permute-start.4) | collective-permute-done | bytes 786464 | tf_op jit(solution)/shard_map/ppermute | solution.py:521
  115.7 22.2 %collective-permute-start.6 = (bf16[256,1536]{1,0:T(8,128)(2,1)}, bf16[256,1536]{1,0:T(8,128)(2,1)}, u32[]{:S(2)}, u32[]{:S(2)}) collective-permute-start(bf16[256,1536]{1,0:T(8,128)(2,1)} %get-tuple-element.106.refs_0_), channel_id=1, source_target_pairs={{0,8},{1,9},{2,10},{3,11},{4,12},{5,13},{6,14},{7,15},{8,16},{9,17... | collective-permute-start | bytes 2359304 | tf_op jit(solution)/shard_map/ppermute | solution.py:521
  145.9 27.2 %collective-permute-done.6.refs_1_ = bf16[256,1536]{1,0:T(8,128)(2,1)} collective-permute-done((bf16[256,1536]{1,0:T(8,128)(2,1)}, bf16[256,1536]{1,0:T(8,128)(2,1)}, u32[]{:S(2)}, u32[]{:S(2)}) %collective-permute-start.6) | collective-permute-done | bytes 786464 | tf_op jit(solution)/shard_map/ppermute | solution.py:521
  173.0 38.0 %collective-permute-done.7.refs_2_ = bf16[256,1536]{1,0:T(8,128)(2,1)} collective-permute-done((bf16[256,1536]{1,0:T(8,128)(2,1)}, bf16[256,1536]{1,0:T(8,128)(2,1)}, u32[]{:S(2)}, u32[]{:S(2)}) %collective-permute-start.7) | collective-permute-done | bytes 786464 | tf_op jit(solution)/shard_map/ppermute | solution.py:521
  223.0 18.7 %attention.1 = (bf16[512,1536]{1,0:T(8,128)(2,1)}, bf16[512,512]{1,0:T(8,128)(2,1)}, bf16[512,512]{1,0:T(8,128)(2,1)}, bf16[512,1536]{1,0:T(8,128)(2,1)}) custom-call(f32[512,2560]{1,0:T(8,128)} %fusion.99.query_ref.key_ref.value_ref, f32[512,2560]{1,0:T(8,128)} %fusion.99.query_ref.key_ref.value_ref, f32[512,2560]{1,0:T(8,128)} %fusion.99.query_ref.key_ref.value_ref, ...), custom_call_target="tpu_custom_call" | custom-call | flops 1000 | bytes 1000 | tf_op jit(solution)/shard_map/attention/pallas_call | solution.py:278
  265.7 14.3 %collective-permute-start.10 = (bf16[256,1536]{1,0:T(8,128)(2,1)S(1)}, bf16[256,1536]{1,0:T(8,128)(2,1)S(1)}, u32[]{:S(2)}, u32[]{:S(2)}) collective-permute-start(bf16[256,1536]{1,0:T(8,128)(2,1)S(1)} %get-tuple-element.296.refs_0_), channel_id=1, source_target_pairs={{0,16},{1,17},{2,18},{3,19},{4,20},{5,21},{6,22},{7,23},{8,24},{9,... | collective-permute-start | bytes 2359304 | tf_op jit(solution)/shard_map/ppermute | solution.py:521
  283.4 31.9 %collective-permute-done.10.refs_2_ = bf16[256,1536]{1,0:T(8,128)(2,1)S(1)} collective-permute-done((bf16[256,1536]{1,0:T(8,128)(2,1)S(1)}, bf16[256,1536]{1,0:T(8,128)(2,1)S(1)}, u32[]{:S(2)}, u32[]{:S(2)}) %collective-permute-start.10) | collective-permute-done | bytes 786464 | tf_op jit(solution)/shard_map/ppermute | solution.py:521
  317.0 18.1 %collective-permute-done.9.refs_1_ = bf16[256,1536]{1,0:T(8,128)(2,1)} collective-permute-done((bf16[256,1536]{1,0:T(8,128)(2,1)S(1)}, bf16[256,1536]{1,0:T(8,128)(2,1)}, u32[]{:S(2)}, u32[]{:S(2)}) %collective-permute-start.9) | collective-permute-done | bytes 786464 | tf_op jit(solution)/shard_map/ppermute | solution.py:521
  346.8 15.0 %collective-permute-start.12 = (bf16[256,1536]{1,0:T(8,128)(2,1)}, bf16[256,1536]{1,0:T(8,128)(2,1)}, u32[]{:S(2)}, u32[]{:S(2)}) collective-permute-start(bf16[256,1536]{1,0:T(8,128)(2,1)} %get-tuple-element.297.refs_0_), channel_id=1, source_target_pairs={{0,8},{1,9},{2,10},{3,11},{4,12},{5,13},{6,14},{7,15},{8,16},{9,17... | collective-permute-start | bytes 2359304 | tf_op jit(solution)/shard_map/ppermute | solution.py:521
  366.1 13.9 %collective-permute-done.12.refs_1_ = bf16[256,1536]{1,0:T(8,128)(2,1)} collective-permute-done((bf16[256,1536]{1,0:T(8,128)(2,1)}, bf16[256,1536]{1,0:T(8,128)(2,1)}, u32[]{:S(2)}, u32[]{:S(2)}) %collective-permute-start.12) | collective-permute-done | bytes 786464 | tf_op jit(solution)/shard_map/ppermute | solution.py:521
  380.0 29.0 %collective-permute-done.13.refs_2_ = bf16[256,1536]{1,0:T(8,128)(2,1)} collective-permute-done((bf16[256,1536]{1,0:T(8,128)(2,1)}, bf16[256,1536]{1,0:T(8,128)(2,1)}, u32[]{:S(2)}, u32[]{:S(2)}) %collective-permute-start.13) | collective-permute-done | bytes 786464 | tf_op jit(solution)/shard_map/ppermute | solution.py:521
  443.9 46.6 %experts.2 = (bf16[2304,1536]{1,0:T(8,128)(2,1)}, bf16[2304,1536]{1,0:T(8,128)(2,1)}, f32[2304,1]{1,0:T(8,128)}, f32[1536,512]{1,0:T(8,128)}, f32[1536,512]{1,0:T(8,128)}, /*index=5*/f32[512,1536]{1,0:T(8,128)}) custom-call(bf16[2304,1536]{1,0:T(8,128)(2,1)} %bitcast.18.rows_ref, bf16[2304,1536]{1,0:T(8,128)(2,1)} %bitcast.19.blend_ref, ...), custom_call_target="tpu_custom_call" | custom-call | flops 1000 | bytes 1000 | tf_op jit(solution)/shard_map/experts/pallas_call | solution.py:97
  490.5 31.3 %all-to-all-done.4 = bf16[8,288,1536]{2,1,0:T(8,128)(2,1)} async-done(((bf16[8,288,1536]{2,1,0:T(8,128)(2,1)}), bf16[8,288,1536]{2,1,0:T(8,128)(2,1)}, u32[]{:S(2)}, u32[]{:S(2)}) %all-to-all-start.4) | async-done | bytes 7077920 | tf_op jit(solution)/shard_map/all_to_all | solution.py:565
  530.7 46.6 %experts.3 = (bf16[2304,1536]{1,0:T(8,128)(2,1)}, bf16[2304,1536]{1,0:T(8,128)(2,1)}, f32[2304,1]{1,0:T(8,128)}, f32[1536,512]{1,0:T(8,128)}, f32[1536,512]{1,0:T(8,128)}, /*index=5*/f32[512,1536]{1,0:T(8,128)}) custom-call(bf16[2304,1536]{1,0:T(8,128)(2,1)} %bitcast.39.rows_ref, bf16[2304,1536]{1,0:T(8,128)(2,1)} %bitcast.40.blend_ref, ...), custom_call_target="tpu_custom_call" | custom-call | flops 1000 | bytes 1000 | tf_op jit(solution)/shard_map/experts/pallas_call | solution.py:97
  579.0 27.8 %all-to-all-done.5 = bf16[8,288,1536]{2,1,0:T(8,128)(2,1)} async-done(((bf16[8,288,1536]{2,1,0:T(8,128)(2,1)}), bf16[8,288,1536]{2,1,0:T(8,128)(2,1)}, u32[]{:S(2)}, u32[]{:S(2)}) %all-to-all-start.5) | async-done | bytes 7077920 | tf_op jit(solution)/shard_map/all_to_all | solution.py:565
  625.5 21.6 %collective-permute-start.15 = (bf16[256,1536]{1,0:T(8,128)(2,1)}, bf16[256,1536]{1,0:T(8,128)(2,1)}, u32[]{:S(2)}, u32[]{:S(2)}) collective-permute-start(bf16[256,1536]{1,0:T(8,128)(2,1)} %get-tuple-element.124), channel_id=1, source_target_pairs={{0,24},{1,25},{2,26},{3,27},{4,28},{5,29},{6,30},{7,31},{8,0},{9,1... | collective-permute-start | bytes 2359304 | tf_op jit(solution)/shard_map/ppermute | solution.py:526
  647.6 17.8 %collective-permute-done.15.refs_1_ = bf16[256,1536]{1,0:T(8,128)(2,1)} collective-permute-done((bf16[256,1536]{1,0:T(8,128)(2,1)}, bf16[256,1536]{1,0:T(8,128)(2,1)}, u32[]{:S(2)}, u32[]{:S(2)}) %collective-permute-start.15) | collective-permute-done | bytes 786464 | tf_op jit(solution)/shard_map/ppermute | solution.py:526
  665.4 49.0 %collective-permute-done.16.refs_2_ = bf16[256,1536]{1,0:T(8,128)(2,1)} collective-permute-done((bf16[256,1536]{1,0:T(8,128)(2,1)}, bf16[256,1536]{1,0:T(8,128)(2,1)}, u32[]{:S(2)}, u32[]{:S(2)}) %collective-permute-start.16) | collective-permute-done | bytes 786464 | tf_op jit(solution)/shard_map/ppermute | solution.py:526
  770.5 16.9 %attention_back.2 = (bf16[256,1536]{1,0:T(8,128)(2,1)}, bf16[256,512]{1,0:T(8,128)(2,1)}, bf16[256,512]{1,0:T(8,128)(2,1)}) custom-call(bf16[512,1536]{1,0:T(8,128)(2,1)} %get-tuple-element.128.query_ref, bf16[512,512]{1,0:T(8,128)(2,1)} %get-tuple-element.129.key_ref, bf16[512,512]{1,0:T(8,128)(2,1)} %get-tuple-element.130.value_ref, ...), custom_call_target="tpu_custom_call" | custom-call | flops 1000 | bytes 1000 | tf_op jit(solution)/shard_map/attention_back/pallas_call | solution.py:317
  795.9 31.5 %collective-permute-done.25.refs_2_ = bf16[256,1536]{1,0:T(8,128)(2,1)} collective-permute-done((bf16[256,1536]{1,0:T(8,128)(2,1)}, bf16[256,1536]{1,0:T(8,128)(2,1)}, u32[]{:S(2)}, u32[]{:S(2)}) %collective-permute-start.25) | collective-permute-done | bytes 786464 | tf_op jit(solution)/shard_map/ppermute | solution.py:526
  859.8 16.9 %attention_back.3 = (bf16[256,1536]{1,0:T(8,128)(2,1)}, bf16[256,512]{1,0:T(8,128)(2,1)}, bf16[256,512]{1,0:T(8,128)(2,1)}) custom-call(bf16[512,1536]{1,0:T(8,128)(2,1)} %get-tuple-element.128.query_ref, bf16[512,512]{1,0:T(8,128)(2,1)} %get-tuple-element.129.key_ref, bf16[512,512]{1,0:T(8,128)(2,1)} %get-tuple-element.130.value_ref, ...), custom_call_target="tpu_custom_call" | custom-call | flops 1000 | bytes 1000 | tf_op jit(solution)/shard_map/attention_back/pallas_call | solution.py:317
  908.0 51.3 %collective-permute-done.22 = bf16[256,1536]{1,0:T(8,128)(2,1)} collective-permute-done((bf16[256,1536]{1,0:T(8,128)(2,1)}, bf16[256,1536]{1,0:T(8,128)(2,1)}, u32[]{:S(2)}, u32[]{:S(2)}) %collective-permute-start.22) | collective-permute-done | bytes 786464 | tf_op jit(solution)/shard_map/ppermute | solution.py:526
  1019.2 59.0 %collective-permute-done.28 = bf16[256,1536]{1,0:T(8,128)(2,1)S(1)} collective-permute-done((bf16[256,1536]{1,0:T(8,128)(2,1)S(1)}, bf16[256,1536]{1,0:T(8,128)(2,1)S(1)}, u32[]{:S(2)}, u32[]{:S(2)}) %collective-permute-start.28) | collective-permute-done | bytes 786464 | tf_op jit(solution)/shard_map/ppermute | solution.py:526
  (350 shorter events, 413.4 us)
Async XLA Ops:
  7.2 204.2 %all-gather.2.cloned.1.call-start = ((), (), s32[]{:S(2)}) async-start(), calls=%async_computation.11 | async-start | bytes 13381632 | tf_op jit(solution)/shard_map/all_gather | solution.py:571
  35.0 67.6 %collective-permute-start.4 = (bf16[256,1536]{1,0:T(8,128)(2,1)S(1)}, bf16[256,1536]{1,0:T(8,128)(2,1)S(1)}, u32[]{:S(2)}, u32[]{:S(2)}) collective-permute-start(bf16[256,1536]{1,0:T(8,128)(2,1)S(1)} %get-tuple-element.102.refs_0_), channel_id=1, source_target_pairs={{0,16},{1,17},{2,18},{3,19},{4,20},{5,21},{6,22},{7,23},{8,24},{9,... | collective-permute-start | bytes 2359304 | tf_op jit(solution)/shard_map/ppermute | solution.py:521
  36.9 65.8 %collective-permute-start.5 = (bf16[256,1536]{1,0:T(8,128)(2,1)S(1)}, bf16[256,1536]{1,0:T(8,128)(2,1)S(1)}, u32[]{:S(2)}, u32[]{:S(2)}) collective-permute-start(bf16[256,1536]{1,0:T(8,128)(2,1)S(1)} %get-tuple-element.102.refs_0_), channel_id=1, source_target_pairs={{0,24},{1,25},{2,26},{3,27},{4,28},{5,29},{6,30},{7,31},{8,0},{9,1... | collective-permute-start | bytes 2359304 | tf_op jit(solution)/shard_map/ppermute | solution.py:521
  110.6 137.9 %all-to-all-start = ((bf16[8,288,1536]{2,1,0:T(8,128)(2,1)}), bf16[8,288,1536]{2,1,0:T(8,128)(2,1)}, u32[]{:S(2)}, u32[]{:S(2)}) async-start(bf16[8,288,1536]{2,1,0:T(8,128)(2,1)} %bitcast.176), calls=%async_computation | async-start | bytes 14155776 | tf_op jit(solution)/shard_map/all_to_all | solution.py:565
  115.7 57.3 %collective-permute-start.6 = (bf16[256,1536]{1,0:T(8,128)(2,1)}, bf16[256,1536]{1,0:T(8,128)(2,1)}, u32[]{:S(2)}, u32[]{:S(2)}) collective-permute-start(bf16[256,1536]{1,0:T(8,128)(2,1)} %get-tuple-element.106.refs_0_), channel_id=1, source_target_pairs={{0,8},{1,9},{2,10},{3,11},{4,12},{5,13},{6,14},{7,15},{8,16},{9,17... | collective-permute-start | bytes 2359304 | tf_op jit(solution)/shard_map/ppermute | solution.py:521
  138.0 73.1 %collective-permute-start.7 = (bf16[256,1536]{1,0:T(8,128)(2,1)}, bf16[256,1536]{1,0:T(8,128)(2,1)}, u32[]{:S(2)}, u32[]{:S(2)}) collective-permute-start(bf16[256,1536]{1,0:T(8,128)(2,1)} %get-tuple-element.106.refs_0_), channel_id=1, source_target_pairs={{0,16},{1,17},{2,18},{3,19},{4,20},{5,21},{6,22},{7,23},{8,24},{9,... | collective-permute-start | bytes 2359304 | tf_op jit(solution)/shard_map/ppermute | solution.py:521
  140.4 70.6 %collective-permute-start.8 = (bf16[256,1536]{1,0:T(8,128)(2,1)}, bf16[256,1536]{1,0:T(8,128)(2,1)}, u32[]{:S(2)}, u32[]{:S(2)}) collective-permute-start(bf16[256,1536]{1,0:T(8,128)(2,1)} %get-tuple-element.106.refs_0_), channel_id=1, source_target_pairs={{0,24},{1,25},{2,26},{3,27},{4,28},{5,29},{6,30},{7,31},{8,0},{9,1... | collective-permute-start | bytes 2359304 | tf_op jit(solution)/shard_map/ppermute | solution.py:521
  248.5 93.3 %all-to-all-start.1 = ((bf16[8,288,1536]{2,1,0:T(8,128)(2,1)}), bf16[8,288,1536]{2,1,0:T(8,128)(2,1)}, u32[]{:S(2)}, u32[]{:S(2)}) async-start(bf16[8,288,1536]{2,1,0:T(8,128)(2,1)} %bitcast.178), calls=%async_computation.1 | async-start | bytes 14155776 | tf_op jit(solution)/shard_map/all_to_all | solution.py:565
  283.4 51.7 %collective-permute-start.9 = (bf16[256,1536]{1,0:T(8,128)(2,1)S(1)}, bf16[256,1536]{1,0:T(8,128)(2,1)}, u32[]{:S(2)}, u32[]{:S(2)}) collective-permute-start(bf16[256,1536]{1,0:T(8,128)(2,1)S(1)} %get-tuple-element.296.refs_0_), channel_id=1, source_target_pairs={{0,8},{1,9},{2,10},{3,11},{4,12},{5,13},{6,14},{7,15},{8,16},{9,17... | collective-permute-start | bytes 2359304 | tf_op jit(solution)/shard_map/ppermute | solution.py:521
  341.8 86.5 %all-to-all-start.2 = ((bf16[8,288,1536]{2,1,0:T(8,128)(2,1)}), bf16[8,288,1536]{2,1,0:T(8,128)(2,1)}, u32[]{:S(2)}, u32[]{:S(2)}) async-start(bf16[8,288,1536]{2,1,0:T(8,128)(2,1)} %bitcast.175), calls=%async_computation.2 | async-start | bytes 14155776 | tf_op jit(solution)/shard_map/all_to_all | solution.py:565
  436.7 85.0 %all-to-all-start.4 = ((bf16[8,288,1536]{2,1,0:T(8,128)(2,1)}), bf16[8,288,1536]{2,1,0:T(8,128)(2,1)}, u32[]{:S(2)}, u32[]{:S(2)}) async-start(bf16[8,288,1536]{2,1,0:T(8,128)(2,1)} %bitcast.177), calls=%async_computation.4 | async-start | bytes 14155776 | tf_op jit(solution)/shard_map/all_to_all | solution.py:565
  521.8 85.1 %all-to-all-start.5 = ((bf16[8,288,1536]{2,1,0:T(8,128)(2,1)}), bf16[8,288,1536]{2,1,0:T(8,128)(2,1)}, u32[]{:S(2)}, u32[]{:S(2)}) async-start(bf16[8,288,1536]{2,1,0:T(8,128)(2,1)} %bitcast.182), calls=%async_computation.5 | async-start | bytes 14155776 | tf_op jit(solution)/shard_map/all_to_all | solution.py:565
  614.0 100.3 %all-to-all-start.7 = ((bf16[8,288,1536]{2,1,0:T(8,128)(2,1)}), bf16[8,288,1536]{2,1,0:T(8,128)(2,1)}, u32[]{:S(2)}, u32[]{:S(2)}) async-start(bf16[8,288,1536]{2,1,0:T(8,128)(2,1)} %bitcast.181), calls=%async_computation.7 | async-start | bytes 14155776 | tf_op jit(solution)/shard_map/all_to_all | solution.py:565
  647.1 67.3 %collective-permute-start.16 = (bf16[256,1536]{1,0:T(8,128)(2,1)}, bf16[256,1536]{1,0:T(8,128)(2,1)}, u32[]{:S(2)}, u32[]{:S(2)}) collective-permute-start(bf16[256,1536]{1,0:T(8,128)(2,1)} %get-tuple-element.125), channel_id=1, source_target_pairs={{0,16},{1,17},{2,18},{3,19},{4,20},{5,21},{6,22},{7,23},{8,24},{9,... | collective-permute-start | bytes 2359304 | tf_op jit(solution)/shard_map/ppermute | solution.py:526
  647.1 67.3 %collective-permute-start.17 = (bf16[256,1536]{1,0:T(8,128)(2,1)}, bf16[256,1536]{1,0:T(8,128)(2,1)}, u32[]{:S(2)}, u32[]{:S(2)}) collective-permute-start(bf16[256,1536]{1,0:T(8,128)(2,1)} %get-tuple-element.126), channel_id=1, source_target_pairs={{0,8},{1,9},{2,10},{3,11},{4,12},{5,13},{6,14},{7,15},{8,16},{9,17... | collective-permute-start | bytes 2359304 | tf_op jit(solution)/shard_map/ppermute | solution.py:526
  714.4 113.1 %all-to-all-start.8 = ((bf16[8,288,1536]{2,1,0:T(8,128)(2,1)}), bf16[8,288,1536]{2,1,0:T(8,128)(2,1)}, u32[]{:S(2)}, u32[]{:S(2)}) async-start(bf16[8,288,1536]{2,1,0:T(8,128)(2,1)} %bitcast.180), calls=%async_computation.8 | async-start | bytes 14155776 | tf_op jit(solution)/shard_map/all_to_all | solution.py:565
  759.2 68.3 %collective-permute-start.25 = (bf16[256,1536]{1,0:T(8,128)(2,1)}, bf16[256,1536]{1,0:T(8,128)(2,1)}, u32[]{:S(2)}, u32[]{:S(2)}) collective-permute-start(bf16[256,1536]{1,0:T(8,128)(2,1)} %get-tuple-element.156), channel_id=1, source_target_pairs={{0,16},{1,17},{2,18},{3,19},{4,20},{5,21},{6,22},{7,23},{8,24},{9,... | collective-permute-start | bytes 2359304 | tf_op jit(solution)/shard_map/ppermute | solution.py:526
  759.8 67.6 %collective-permute-start.26 = (bf16[256,1536]{1,0:T(8,128)(2,1)}, bf16[256,1536]{1,0:T(8,128)(2,1)}, u32[]{:S(2)}, u32[]{:S(2)}) collective-permute-start(bf16[256,1536]{1,0:T(8,128)(2,1)} %get-tuple-element.157), channel_id=1, source_target_pairs={{0,8},{1,9},{2,10},{3,11},{4,12},{5,13},{6,14},{7,15},{8,16},{9,17... | collective-permute-start | bytes 2359304 | tf_op jit(solution)/shard_map/ppermute | solution.py:526
  827.5 131.9 %all-to-all-start.9 = ((bf16[8,288,1536]{2,1,0:T(8,128)(2,1)}), bf16[8,288,1536]{2,1,0:T(8,128)(2,1)}, u32[]{:S(2)}, u32[]{:S(2)}) async-start(bf16[8,288,1536]{2,1,0:T(8,128)(2,1)} %bitcast.179), calls=%async_computation.9 | async-start | bytes 14155776 | tf_op jit(solution)/shard_map/all_to_all | solution.py:565
  832.3 296.1 %reduce-scatter.2.cloned.1.call-start = ((), (), s32[]{:S(2)}) async-start(), calls=%async_computation.12 | async-start | bytes 4866048 | tf_op jit(solution)/shard_map/reduce_scatter | solution.py:809
  888.0 71.4 %collective-permute-start.22 = (bf16[256,1536]{1,0:T(8,128)(2,1)}, bf16[256,1536]{1,0:T(8,128)(2,1)}, u32[]{:S(2)}, u32[]{:S(2)}) collective-permute-start(bf16[256,1536]{1,0:T(8,128)(2,1)} %get-tuple-element.152), channel_id=1, source_target_pairs={{0,16},{1,17},{2,18},{3,19},{4,20},{5,21},{6,22},{7,23},{8,24},{9,... | collective-permute-start | bytes 2359304 | tf_op jit(solution)/shard_map/ppermute | solution.py:526
  890.6 68.8 %collective-permute-start.23 = (bf16[256,1536]{1,0:T(8,128)(2,1)}, bf16[256,1536]{1,0:T(8,128)(2,1)}, u32[]{:S(2)}, u32[]{:S(2)}) collective-permute-start(bf16[256,1536]{1,0:T(8,128)(2,1)} %get-tuple-element.153), channel_id=1, source_target_pairs={{0,8},{1,9},{2,10},{3,11},{4,12},{5,13},{6,14},{7,15},{8,16},{9,17... | collective-permute-start | bytes 2359304 | tf_op jit(solution)/shard_map/ppermute | solution.py:526
  996.7 81.5 %collective-permute-start.28 = (bf16[256,1536]{1,0:T(8,128)(2,1)S(1)}, bf16[256,1536]{1,0:T(8,128)(2,1)S(1)}, u32[]{:S(2)}, u32[]{:S(2)}) collective-permute-start(bf16[256,1536]{1,0:T(8,128)(2,1)S(1)} %copy-done.58), channel_id=1, source_target_pairs={{0,16},{1,17},{2,18},{3,19},{4,20},{5,21},{6,22},{7,23},{8,24},{9,... | collective-permute-start | bytes 2359304 | tf_op jit(solution)/shard_map/ppermute | solution.py:526
  997.2 81.0 %collective-permute-start.29 = (bf16[256,1536]{1,0:T(8,128)(2,1)S(1)}, bf16[256,1536]{1,0:T(8,128)(2,1)S(1)}, u32[]{:S(2)}, u32[]{:S(2)}) collective-permute-start(bf16[256,1536]{1,0:T(8,128)(2,1)S(1)} %copy-done.57), channel_id=1, source_target_pairs={{0,8},{1,9},{2,10},{3,11},{4,12},{5,13},{6,14},{7,15},{8,16},{9,17... | collective-permute-start | bytes 2359304 | tf_op jit(solution)/shard_map/ppermute | solution.py:526
  (84 other events, 1304.1 us)
Sparse Core Ops, SparseCore 0:
  14.0 194.3 all-gather.1
  976.2 152.2 reduce-scatter.1

commit v7 on v6

--- a/solution.py
+++ b/solution.py
@@ -1,3 +1,5 @@
+import functools
+
 import jax
 import jax.numpy as jnp
 from jax import lax
@@ -346,32 +348,39 @@
     )
 
 
-def weights_kernel(left_ref, right_ref, *refs):
-    out_ref = refs[-1]
-    width = right_ref.shape[1]
-    product = head_product(left_ref[...], right_ref[...], 0, 0)
-    if len(refs) == 1:
-        out_ref[...] = product.astype(out_ref.dtype)
-    else:
-        out_ref[:, :width] = product.astype(out_ref.dtype)
-        out_ref[:, width:] = refs[0][...].astype(out_ref.dtype)
-
-
-def run_weights(left, right, extra, dtype):
+def weights_kernel(*refs, counts):
+    left_ref, out_ref = refs[0], refs[-1]
+    rights = refs[1 : 1 + sum(counts)]
+    tokens = left_ref.shape[0] // len(counts)
+    start = 0
+    for i in range(counts[0]):
+        width = rights[i].shape[1]
+        product = 0.0
+        for m in range(len(counts)):
+            product = product + head_product(
+                left_ref[m * tokens : (m + 1) * tokens], rights[m * counts[0] + i][...], 0, 0
+            )
+        out_ref[:, start : start + width] = product.astype(out_ref.dtype)
+        start += width
+    if len(refs) > 2 + sum(counts):
+        out_ref[:, start:] = refs[-2][...].astype(out_ref.dtype)
+
+
+def run_weights(left, groups, extra, dtype):
     tokens, height = left.shape
-    width = right.shape[1]
     block = 256 if height % 256 == 0 else height
-    in_specs = [
-        pl.BlockSpec((tokens, block), lambda i: (0, i)),
-        pl.BlockSpec((tokens, width), lambda i: (0, 0)),
+    rights = [right for group in groups for right in group]
+    width = sum(right.shape[1] for right in groups[0])
+    in_specs = [pl.BlockSpec((tokens, block), lambda i: (0, i))] + [
+        pl.BlockSpec(right.shape, lambda i: (0, 0)) for right in rights
     ]
-    operands = [left, right]
+    operands = [left, *rights]
     if extra is not None:
         in_specs.append(pl.BlockSpec((block, extra.shape[1]), lambda i: (i, 0)))
         operands.append(extra)
         width += extra.shape[1]
     return pl.pallas_call(
-        weights_kernel,
+        functools.partial(weights_kernel, counts=tuple(len(group) for group in groups)),
         grid=(height // block,),
         in_specs=in_specs,
         out_specs=pl.BlockSpec((block, width), lambda i: (i, 0)),
@@ -702,23 +711,24 @@
             recip_second,
             gain_second,
             cotan_seq[micro],
-            out_proj,
+            proj_copy[1],
         )
         grads = run_attention_back(
             queries, keys, values, hold(grad_mixture, before(grad_attn)), tables, block_ids, micro
         )
         grad_tokens, gain_first_w = run_first(
-            *hold(grads, then),
-            qkv_proj,
+            *grads,
+            proj_copy[0],
             hidden_seq[micro],
             rows_of(recip_first, micro),
             gain_first,
             grad_residual,
         )
+        grads, gain_first_w = hold((grads, gain_first_w), then)
         return (
             grad_tokens,
             grad_attn,
-            jnp.concatenate(grads, axis=1),
+            grads,
             grad_logits,
             gain_second_w,
             gain_first_w,
@@ -753,12 +763,15 @@
         hold(moved_mid0, mid1), moved_blend0, gate_rows[:, 0]
     )
     moved_grads0 = exchange(hold(grads0, moved_mid1))
-    grads1, scaled1, pairs1, weights1 = run_expert(moved_mid1, moved_blend1, gate_rows[:, 1])
+    proj_copy = hold((qkv_proj, out_proj), moved_mid0)
+    grads1, scaled1, pairs1, weights1 = run_expert(
+        hold(moved_mid1, proj_copy), moved_blend1, gate_rows[:, 1]
+    )
     pair_back = exchange(hold(jnp.stack([pairs0, pairs1], axis=1), moved_grads0))
     moved_grads1 = exchange(hold(grads1, pair_back))
     pair_blocks = pairs_home(pair_back)
     back0 = sums_of(0, moved_grads0)
-    moved_scaled0 = exchange(hold(scaled0, moved_grads1, back0))
+    moved_scaled0 = exchange(hold(scaled0, moved_grads1, back0, pair_blocks))
     back1 = sums_of(1, moved_grads1)
     result0 = attend_back(
         0,
@@ -773,16 +786,16 @@
 
     def out_grads(grad_attn):
         return run_weights(
-            mixture, jnp.concatenate([result0[1], grad_attn], axis=0), None, bf16
+            mixture, [[result0[1]], [grad_attn]], None, bf16
         )
 
     result1 = attend_back(
         1,
-        hold(back1, result0),
+        hold(back1, result0, blend_back0[0]),
         [block[1] for block in pair_blocks],
         gates1,
         lambda grad_attn: (moved_scaled0, blend_back0[0], out_grads(grad_attn)),
-        (),
+        blend_back0,
     )
     blend_back1 = sums_of(1, hold(moved_scaled1, result1))
     outputs = [
@@ -790,7 +803,6 @@
         after[1][0] + res_scale * total_of(blend_back1),
     ]
     token_grads_out = [result0[0], result1[0]]
-    grad_qkv = jnp.concatenate([result0[2], result1[2]], axis=0)
     out_w = out_grads(result1[1])
     router_w = jnp.einsum(
         "td,et->de",
@@ -808,8 +820,8 @@
     small_w = jnp.pad(small_w, ((0, 0), (0, -small_w.shape[1] % 128)))
     out_sum = lax.psum_scatter(out_w, "dp", scatter_dimension=0, tiled=True)
     qkv_sum = reduce_rows(
-        run_weights(normed_in, grad_qkv, small_w, f32),
-        (blend_back0, moved_scaled1),
+        run_weights(normed_in, [result0[2], result1[2]], small_w, f32),
+        moved_scaled1,
         blend_back1[0],
         blend_back1,
     )

time: 1150 us -> 1100 us (0.957)
  starting transfers between devices: 169 us -> 101 us
  waiting for transfers between devices: 559 us -> 583 us
    ppermute x15, waiting for transfers between devices: 228 us -> 297 us  [spread(): lax.ppermute(block, 'dp', line_shift(step))]
    ppermute x15, starting transfers between devices: 74.5 us -> 28.8 us  [spread(): lax.ppermute(block, 'dp', line_shift(step))]
    ppermute x15, waiting for transfers between devices: 216 us -> 182 us  [give_back(): lax.ppermute(blocks[step], 'dp', line_shift(-step))]
    ppermute x15, starting transfers between devices: 39.5 us -> 20.5 us  [give_back(): lax.ppermute(blocks[step], 'dp', line_shift(-step))]
  transfers between devices with their start and end apart: 48 -> 48, of which waited for: 28 -> 25; matrix products, arithmetic and copies ran while one was open for 10% -> 10% of each run, Pallas kernels for 22% -> 23%
where the time goes in v7:
time: 1100 us; the launch traced here: 1090 us
  waiting for transfers between devices  583 us (53%)
  Pallas kernels  250 us (23%)
  starting transfers between devices  101 us (9%)
  local copies, waits for them, and re-layouts  54.5 us (5%)
  other arithmetic  46.1 us (4%)
  matrix products  24.7 us (2%)
  blocking collectives  15.6 us (1%)
  between operations  15.6 us (1%)
    ppermute x15, waiting for transfers between devices, spread(): lax.ppermute(block, 'dp', line_shift(step))  297 us
    ppermute x15, waiting for transfers between devices, give_back(): lax.ppermute(blocks[step], 'dp', line_shift(-step))  182 us
    pallas_call x2, Pallas kernels, run_experts(): pl.pallas_call(expert_kernel, grid=(count // block,), in_specs=[wide, wid...  93.2 us
    all_to_all x8, waiting for transfers between devices, exchange(): lax.all_to_all(block, 'dp', split_axis=0, concat_axis=0, tiled=True, axis...  48.1 us
    all_to_all x8, starting transfers between devices, exchange(): lax.all_to_all(block, 'dp', split_axis=0, concat_axis=0, tiled=True, axis...  40.2 us
    ppermute x5, waiting for transfers between devices, fold(): lax.ppermute(sent.astype(bf16), 'dp', [(i, i ^ bit) for i in range(device...  34.7 us
    pallas_call x2, Pallas kernels, run_attention_back(): pl.pallas_call(attend_back_kernel, grid=(1, KVH // 2), in_specs=[at(wide,...  33.8 us
    ppermute x15, starting transfers between devices, spread(): lax.ppermute(block, 'dp', line_shift(step))  28.8 us
  transfers between devices with their start and end apart: 48, of which 25 were waited for; matrix products, arithmetic and copies ran while one was open for 10% of the time, Pallas kernels for 23%

profile of v7, /device:TPU:0, one launch (start us, length us, event | category | flops | bytes accessed | tf_op | source)
XLA Modules:
  0.0 1090.0 jit_solution(3394826708957216318)
XLA Ops:
  42.2 15.2 %collective-permute-done.5.refs_3_ = bf16[256,1536]{1,0:T(8,128)(2,1)S(1)} collective-permute-done((bf16[256,1536]{1,0:T(8,128)(2,1)S(1)}, bf16[256,1536]{1,0:T(8,128)(2,1)S(1)}, u32[]{:S(2)}, u32[]{:S(2)}) %collective-permute-start.5) | collective-permute-done | bytes 786464 | tf_op jit(solution)/shard_map/ppermute | solution.py:530
  57.5 67.3 %collective-permute-done.4.refs_2_ = bf16[256,1536]{1,0:T(8,128)(2,1)S(1)} collective-permute-done((bf16[256,1536]{1,0:T(8,128)(2,1)S(1)}, bf16[256,1536]{1,0:T(8,128)(2,1)S(1)}, u32[]{:S(2)}, u32[]{:S(2)}) %collective-permute-start.4) | collective-permute-done | bytes 786464 | tf_op jit(solution)/shard_map/ppermute | solution.py:530
  152.3 21.1 %collective-permute-done.8.refs_3_ = bf16[256,1536]{1,0:T(8,128)(2,1)} collective-permute-done((bf16[256,1536]{1,0:T(8,128)(2,1)}, bf16[256,1536]{1,0:T(8,128)(2,1)}, u32[]{:S(2)}, u32[]{:S(2)}) %collective-permute-start.8) | collective-permute-done | bytes 786464 | tf_op jit(solution)/shard_map/ppermute | solution.py:530
  173.5 55.3 %collective-permute-done.7.refs_2_ = bf16[256,1536]{1,0:T(8,128)(2,1)} collective-permute-done((bf16[256,1536]{1,0:T(8,128)(2,1)}, bf16[256,1536]{1,0:T(8,128)(2,1)}, u32[]{:S(2)}, u32[]{:S(2)}) %collective-permute-start.7) | collective-permute-done | bytes 786464 | tf_op jit(solution)/shard_map/ppermute | solution.py:530
  231.0 9.7 fusion.100.query_ref.key_ref.value_ref
  240.7 18.7 %attention.1 = (bf16[512,1536]{1,0:T(8,128)(2,1)}, bf16[512,512]{1,0:T(8,128)(2,1)}, bf16[512,512]{1,0:T(8,128)(2,1)}, bf16[512,1536]{1,0:T(8,128)(2,1)}) custom-call(f32[512,2560]{1,0:T(8,128)} %fusion.100.query_ref.key_ref.value_ref, f32[512,2560]{1,0:T(8,128)} %fusion.100.query_ref.key_ref.value_ref, f32[512,2560]{1,0:T(8,128)} %fusion.100.query_ref.key_ref.value_ref, ...), custom_call_target="tpu_custom_call" | custom-call | flops 1000 | bytes 1000 | tf_op jit(solution)/shard_map/attention/pallas_call | solution.py:280
  283.5 19.2 %collective-permute-done.11.refs_3_ = bf16[256,1536]{1,0:T(8,128)(2,1)S(1)} collective-permute-done((bf16[256,1536]{1,0:T(8,128)(2,1)S(1)}, bf16[256,1536]{1,0:T(8,128)(2,1)S(1)}, u32[]{:S(2)}, u32[]{:S(2)}) %collective-permute-start.11) | collective-permute-done | bytes 786464 | tf_op jit(solution)/shard_map/ppermute | solution.py:530
  302.7 47.2 %collective-permute-done.10.refs_2_ = bf16[256,1536]{1,0:T(8,128)(2,1)S(1)} collective-permute-done((bf16[256,1536]{1,0:T(8,128)(2,1)S(1)}, bf16[256,1536]{1,0:T(8,128)(2,1)S(1)}, u32[]{:S(2)}, u32[]{:S(2)}) %collective-permute-start.10) | collective-permute-done | bytes 786464 | tf_op jit(solution)/shard_map/ppermute | solution.py:530
  367.1 15.5 %collective-permute-done.14.refs_3_ = bf16[256,1536]{1,0:T(8,128)(2,1)} collective-permute-done((bf16[256,1536]{1,0:T(8,128)(2,1)}, bf16[256,1536]{1,0:T(8,128)(2,1)}, u32[]{:S(2)}, u32[]{:S(2)}) %collective-permute-start.14) | collective-permute-done | bytes 786464 | tf_op jit(solution)/shard_map/ppermute | solution.py:530
  382.6 51.4 %collective-permute-done.13.refs_2_ = bf16[256,1536]{1,0:T(8,128)(2,1)} collective-permute-done((bf16[256,1536]{1,0:T(8,128)(2,1)}, bf16[256,1536]{1,0:T(8,128)(2,1)}, u32[]{:S(2)}, u32[]{:S(2)}) %collective-permute-start.13) | collective-permute-done | bytes 786464 | tf_op jit(solution)/shard_map/ppermute | solution.py:530
  465.9 46.6 %experts.2 = (bf16[2304,1536]{1,0:T(8,128)(2,1)}, bf16[2304,1536]{1,0:T(8,128)(2,1)}, f32[2304,1]{1,0:T(8,128)}, f32[1536,512]{1,0:T(8,128)}, f32[1536,512]{1,0:T(8,128)}, /*index=5*/f32[512,1536]{1,0:T(8,128)}) custom-call(bf16[2304,1536]{1,0:T(8,128)(2,1)} %bitcast.18.rows_ref, bf16[2304,1536]{1,0:T(8,128)(2,1)} %bitcast.19.blend_ref, ...), custom_call_target="tpu_custom_call" | custom-call | flops 1000 | bytes 1000 | tf_op jit(solution)/shard_map/experts/pallas_call | solution.py:99
  512.5 31.3 %all-to-all-done.4 = bf16[8,288,1536]{2,1,0:T(8,128)(2,1)} async-done(((bf16[8,288,1536]{2,1,0:T(8,128)(2,1)}), bf16[8,288,1536]{2,1,0:T(8,128)(2,1)}, u32[]{:S(2)}, u32[]{:S(2)}) %all-to-all-start.4) | async-done | bytes 7077920 | tf_op jit(solution)/shard_map/all_to_all | solution.py:574
  564.4 46.6 %experts.3 = (bf16[2304,1536]{1,0:T(8,128)(2,1)}, bf16[2304,1536]{1,0:T(8,128)(2,1)}, f32[2304,1]{1,0:T(8,128)}, f32[1536,512]{1,0:T(8,128)}, f32[1536,512]{1,0:T(8,128)}, /*index=5*/f32[512,1536]{1,0:T(8,128)}) custom-call(bf16[2304,1536]{1,0:T(8,128)(2,1)} %bitcast.39.rows_ref, bf16[2304,1536]{1,0:T(8,128)(2,1)} %bitcast.40.blend_ref, ...), custom_call_target="tpu_custom_call" | custom-call | flops 1000 | bytes 1000 | tf_op jit(solution)/shard_map/experts/pallas_call | solution.py:99
  612.8 16.3 %all-to-all-done.5 = bf16[8,288,1536]{2,1,0:T(8,128)(2,1)} async-done(((bf16[8,288,1536]{2,1,0:T(8,128)(2,1)}), bf16[8,288,1536]{2,1,0:T(8,128)(2,1)}, u32[]{:S(2)}, u32[]{:S(2)}) %all-to-all-start.5) | async-done | bytes 7077920 | tf_op jit(solution)/shard_map/all_to_all | solution.py:574
  654.6 47.4 %collective-permute-done.20 = f32[2,8,256]{2,1,0:T(8,128)S(1)} collective-permute-done((f32[2,8,256]{2,1,0:T(8,128)S(1)}, f32[2,8,256]{2,1,0:T(8,128)S(1)}, u32[]{:S(2)}, u32[]{:S(2)}) %collective-permute-start.20) | collective-permute-done | bytes 16416 | tf_op jit(solution)/shard_map/ppermute | solution.py:535
  703.9 14.2 %collective-permute-done.19 = f32[2,8,256]{2,1,0:T(8,128)S(1)} collective-permute-done((f32[2,8,256]{2,1,0:T(8,128)S(1)}, f32[2,8,256]{2,1,0:T(8,128)S(1)}, u32[]{:S(2)}, u32[]{:S(2)}) %collective-permute-start.19) | collective-permute-done | bytes 16416 | tf_op jit(solution)/shard_map/ppermute | solution.py:535
  754.6 16.9 %attention_back.2 = (bf16[256,1536]{1,0:T(8,128)(2,1)}, bf16[256,512]{1,0:T(8,128)(2,1)}, bf16[256,512]{1,0:T(8,128)(2,1)}) custom-call(bf16[512,1536]{1,0:T(8,128)(2,1)} %get-tuple-element.136.query_ref, bf16[512,512]{1,0:T(8,128)(2,1)} %get-tuple-element.137.key_ref, bf16[512,512]{1,0:T(8,128)(2,1)} %get-tuple-element.138.value_ref, ...), custom_call_target="tpu_custom_call" | custom-call | flops 1000 | bytes 1000 | tf_op jit(solution)/shard_map/attention_back/pallas_call | solution.py:319
  779.8 32.8 %collective-permute-done.25.refs_2_ = bf16[256,1536]{1,0:T(8,128)(2,1)S(1)} collective-permute-done((bf16[256,1536]{1,0:T(8,128)(2,1)}, bf16[256,1536]{1,0:T(8,128)(2,1)S(1)}, u32[]{:S(2)}, u32[]{:S(2)}) %collective-permute-start.25) | collective-permute-done | bytes 786464 | tf_op jit(solution)/shard_map/ppermute | solution.py:535
  846.8 16.8 %attention_back.3 = (bf16[256,1536]{1,0:T(8,128)(2,1)}, bf16[256,512]{1,0:T(8,128)(2,1)}, bf16[256,512]{1,0:T(8,128)(2,1)}) custom-call(bf16[512,1536]{1,0:T(8,128)(2,1)} %get-tuple-element.136.query_ref, bf16[512,512]{1,0:T(8,128)(2,1)} %get-tuple-element.137.key_ref, bf16[512,512]{1,0:T(8,128)(2,1)} %get-tuple-element.138.value_ref, ...), custom_call_target="tpu_custom_call" | custom-call | flops 1000 | bytes 1000 | tf_op jit(solution)/shard_map/attention_back/pallas_call | solution.py:319
  872.2 25.3 %collective-permute-done.22 = bf16[256,1536]{1,0:T(8,128)(2,1)S(1)} collective-permute-done((bf16[256,1536]{1,0:T(8,128)(2,1)}, bf16[256,1536]{1,0:T(8,128)(2,1)S(1)}, u32[]{:S(2)}, u32[]{:S(2)}) %collective-permute-start.22) | collective-permute-done | bytes 786464 | tf_op jit(solution)/shard_map/ppermute | solution.py:535
  899.5 10.5 weights.3
  950.7 13.1 %collective-permute-done.31 = bf16[4,2,48,1280]{3,2,1,0:T(8,128)(2,1)S(1)} collective-permute-done((bf16[4,2,48,1280]{3,2,1,0:T(8,128)(2,1)S(1)}, bf16[4,2,48,1280]{3,2,1,0:T(8,128)(2,1)S(1)}, u32[]{:S(2)}, u32[]{:S(2)}) %collective-permute-start.31) | collective-permute-done | bytes 983072 | tf_op jit(solution)/shard_map/ppermute | solution.py:554
  969.9 59.8 %collective-permute-done.28 = bf16[256,1536]{1,0:T(8,128)(2,1)S(1)} collective-permute-done((bf16[256,1536]{1,0:T(8,128)(2,1)S(1)}, bf16[256,1536]{1,0:T(8,128)(2,1)S(1)}, u32[]{:S(2)}, u32[]{:S(2)}) %collective-permute-start.28) | collective-permute-done | bytes 786464 | tf_op jit(solution)/shard_map/ppermute | solution.py:535
  1033.7 11.2 %collective-permute-done.33 = bf16[4,48,1280]{2,1,0:T(8,128)(2,1)S(1)} collective-permute-done((bf16[4,48,1280]{2,1,0:T(8,128)(2,1)S(1)}, bf16[4,48,1280]{2,1,0:T(8,128)(2,1)S(1)}, u32[]{:S(2)}, u32[]{:S(2)}) %collective-permute-start.33) | collective-permute-done | bytes 491552 | tf_op jit(solution)/shard_map/ppermute | solution.py:554
  (340 shorter events, 364.9 us)
Async XLA Ops:
  7.2 221.9 %all-gather.2.cloned.1.call-start = ((), (), s32[]{:S(2)}) async-start(), calls=%async_computation.11 | async-start | bytes 13381632 | tf_op jit(solution)/shard_map/all_gather | solution.py:580
  35.8 89.0 %collective-permute-start.4 = (bf16[256,1536]{1,0:T(8,128)(2,1)S(1)}, bf16[256,1536]{1,0:T(8,128)(2,1)S(1)}, u32[]{:S(2)}, u32[]{:S(2)}) collective-permute-start(bf16[256,1536]{1,0:T(8,128)(2,1)S(1)} %get-tuple-element.107.refs_0_), channel_id=1, source_target_pairs={{0,16},{1,17},{2,18},{3,19},{4,20},{5,21},{6,22},{7,23},{8,24},{9,... | collective-permute-start | bytes 2359304 | tf_op jit(solution)/shard_map/ppermute | solution.py:530
  39.7 85.1 %collective-permute-start.3 = (bf16[256,1536]{1,0:T(8,128)(2,1)S(1)}, bf16[256,1536]{1,0:T(8,128)(2,1)S(1)}, u32[]{:S(2)}, u32[]{:S(2)}) collective-permute-start(bf16[256,1536]{1,0:T(8,128)(2,1)S(1)} %get-tuple-element.107.refs_0_), channel_id=1, source_target_pairs={{0,8},{1,9},{2,10},{3,11},{4,12},{5,13},{6,14},{7,15},{8,16},{9,17... | collective-permute-start | bytes 2359304 | tf_op jit(solution)/shard_map/ppermute | solution.py:530
  132.7 133.4 %all-to-all-start = ((bf16[8,288,1536]{2,1,0:T(8,128)(2,1)}), bf16[8,288,1536]{2,1,0:T(8,128)(2,1)}, u32[]{:S(2)}, u32[]{:S(2)}) async-start(bf16[8,288,1536]{2,1,0:T(8,128)(2,1)} %bitcast.176), calls=%async_computation | async-start | bytes 14155776 | tf_op jit(solution)/shard_map/all_to_all | solution.py:574
  137.9 90.8 %collective-permute-start.7 = (bf16[256,1536]{1,0:T(8,128)(2,1)}, bf16[256,1536]{1,0:T(8,128)(2,1)}, u32[]{:S(2)}, u32[]{:S(2)}) collective-permute-start(bf16[256,1536]{1,0:T(8,128)(2,1)} %get-tuple-element.111.refs_0_), channel_id=1, source_target_pairs={{0,16},{1,17},{2,18},{3,19},{4,20},{5,21},{6,22},{7,23},{8,24},{9,... | collective-permute-start | bytes 2359304 | tf_op jit(solution)/shard_map/ppermute | solution.py:530
  145.4 83.3 %collective-permute-start.6 = (bf16[256,1536]{1,0:T(8,128)(2,1)}, bf16[256,1536]{1,0:T(8,128)(2,1)}, u32[]{:S(2)}, u32[]{:S(2)}) collective-permute-start(bf16[256,1536]{1,0:T(8,128)(2,1)} %get-tuple-element.111.refs_0_), channel_id=1, source_target_pairs={{0,8},{1,9},{2,10},{3,11},{4,12},{5,13},{6,14},{7,15},{8,16},{9,17... | collective-permute-start | bytes 2359304 | tf_op jit(solution)/shard_map/ppermute | solution.py:530
  266.1 91.3 %all-to-all-start.1 = ((bf16[8,288,1536]{2,1,0:T(8,128)(2,1)}), bf16[8,288,1536]{2,1,0:T(8,128)(2,1)}, u32[]{:S(2)}, u32[]{:S(2)}) async-start(bf16[8,288,1536]{2,1,0:T(8,128)(2,1)} %bitcast.178), calls=%async_computation.1 | async-start | bytes 14155776 | tf_op jit(solution)/shard_map/all_to_all | solution.py:574
  357.5 92.9 %all-to-all-start.2 = ((bf16[8,288,1536]{2,1,0:T(8,128)(2,1)}), bf16[8,288,1536]{2,1,0:T(8,128)(2,1)}, u32[]{:S(2)}, u32[]{:S(2)}) async-start(bf16[8,288,1536]{2,1,0:T(8,128)(2,1)} %bitcast.175), calls=%async_computation.2 | async-start | bytes 14155776 | tf_op jit(solution)/shard_map/all_to_all | solution.py:574
  362.5 71.4 %collective-permute-start.13 = (bf16[256,1536]{1,0:T(8,128)(2,1)}, bf16[256,1536]{1,0:T(8,128)(2,1)}, u32[]{:S(2)}, u32[]{:S(2)}) collective-permute-start(bf16[256,1536]{1,0:T(8,128)(2,1)} %get-tuple-element.307.refs_0_), channel_id=1, source_target_pairs={{0,16},{1,17},{2,18},{3,19},{4,20},{5,21},{6,22},{7,23},{8,24},{9,... | collective-permute-start | bytes 2359304 | tf_op jit(solution)/shard_map/ppermute | solution.py:530
  365.1 68.8 %collective-permute-start.12 = (bf16[256,1536]{1,0:T(8,128)(2,1)}, bf16[256,1536]{1,0:T(8,128)(2,1)}, u32[]{:S(2)}, u32[]{:S(2)}) collective-permute-start(bf16[256,1536]{1,0:T(8,128)(2,1)} %get-tuple-element.307.refs_0_), channel_id=1, source_target_pairs={{0,8},{1,9},{2,10},{3,11},{4,12},{5,13},{6,14},{7,15},{8,16},{9,17... | collective-permute-start | bytes 2359304 | tf_op jit(solution)/shard_map/ppermute | solution.py:530
  458.8 85.0 %all-to-all-start.4 = ((bf16[8,288,1536]{2,1,0:T(8,128)(2,1)}), bf16[8,288,1536]{2,1,0:T(8,128)(2,1)}, u32[]{:S(2)}, u32[]{:S(2)}) async-start(bf16[8,288,1536]{2,1,0:T(8,128)(2,1)} %bitcast.177), calls=%async_computation.4 | async-start | bytes 14155776 | tf_op jit(solution)/shard_map/all_to_all | solution.py:574
  543.8 85.2 %all-to-all-start.5 = ((bf16[8,288,1536]{2,1,0:T(8,128)(2,1)}), bf16[8,288,1536]{2,1,0:T(8,128)(2,1)}, u32[]{:S(2)}, u32[]{:S(2)}) async-start(bf16[8,288,1536]{2,1,0:T(8,128)(2,1)} %bitcast.182), calls=%async_computation.5 | async-start | bytes 14155776 | tf_op jit(solution)/shard_map/all_to_all | solution.py:574
  636.2 84.9 %all-to-all-start.7 = ((bf16[8,288,1536]{2,1,0:T(8,128)(2,1)}), bf16[8,288,1536]{2,1,0:T(8,128)(2,1)}, u32[]{:S(2)}, u32[]{:S(2)}) async-start(bf16[8,288,1536]{2,1,0:T(8,128)(2,1)} %bitcast.181), calls=%async_computation.7 | async-start | bytes 14155776 | tf_op jit(solution)/shard_map/all_to_all | solution.py:574
  647.7 72.8 %collective-permute-start.15 = (bf16[256,1536]{1,0:T(8,128)(2,1)}, bf16[256,1536]{1,0:T(8,128)(2,1)}, u32[]{:S(2)}, u32[]{:S(2)}) collective-permute-start(bf16[256,1536]{1,0:T(8,128)(2,1)} %get-tuple-element.132), channel_id=1, source_target_pairs={{0,24},{1,25},{2,26},{3,27},{4,28},{5,29},{6,30},{7,31},{8,0},{9,1... | collective-permute-start | bytes 2359304 | tf_op jit(solution)/shard_map/ppermute | solution.py:535
  647.7 72.8 %collective-permute-start.16 = (bf16[256,1536]{1,0:T(8,128)(2,1)}, bf16[256,1536]{1,0:T(8,128)(2,1)}, u32[]{:S(2)}, u32[]{:S(2)}) collective-permute-start(bf16[256,1536]{1,0:T(8,128)(2,1)} %get-tuple-element.133), channel_id=1, source_target_pairs={{0,16},{1,17},{2,18},{3,19},{4,20},{5,21},{6,22},{7,23},{8,24},{9,... | collective-permute-start | bytes 2359304 | tf_op jit(solution)/shard_map/ppermute | solution.py:535
  648.1 72.4 %collective-permute-start.17 = (bf16[256,1536]{1,0:T(8,128)(2,1)}, bf16[256,1536]{1,0:T(8,128)(2,1)}, u32[]{:S(2)}, u32[]{:S(2)}) collective-permute-start(bf16[256,1536]{1,0:T(8,128)(2,1)} %get-tuple-element.134), channel_id=1, source_target_pairs={{0,8},{1,9},{2,10},{3,11},{4,12},{5,13},{6,14},{7,15},{8,16},{9,17... | collective-permute-start | bytes 2359304 | tf_op jit(solution)/shard_map/ppermute | solution.py:535
  721.1 91.5 %all-to-all-start.8 = ((bf16[8,288,1536]{2,1,0:T(8,128)(2,1)}), bf16[8,288,1536]{2,1,0:T(8,128)(2,1)}, u32[]{:S(2)}, u32[]{:S(2)}) async-start(bf16[8,288,1536]{2,1,0:T(8,128)(2,1)} %bitcast.180), calls=%async_computation.8 | async-start | bytes 14155776 | tf_op jit(solution)/shard_map/all_to_all | solution.py:574
  743.1 69.6 %collective-permute-start.25 = (bf16[256,1536]{1,0:T(8,128)(2,1)}, bf16[256,1536]{1,0:T(8,128)(2,1)S(1)}, u32[]{:S(2)}, u32[]{:S(2)}) collective-permute-start(bf16[256,1536]{1,0:T(8,128)(2,1)} %get-tuple-element.165), channel_id=1, source_target_pairs={{0,16},{1,17},{2,18},{3,19},{4,20},{5,21},{6,22},{7,23},{8,24},{9,... | collective-permute-start | bytes 2359304 | tf_op jit(solution)/shard_map/ppermute | solution.py:535
  813.9 96.2 %all-to-all-start.9 = ((bf16[8,288,1536]{2,1,0:T(8,128)(2,1)}), bf16[8,288,1536]{2,1,0:T(8,128)(2,1)}, u32[]{:S(2)}, u32[]{:S(2)}) async-start(bf16[8,288,1536]{2,1,0:T(8,128)(2,1)} %bitcast.179), calls=%async_computation.9 | async-start | bytes 14155776 | tf_op jit(solution)/shard_map/all_to_all | solution.py:574
  818.7 261.7 %reduce-scatter.2.cloned.1.call-start = ((), (), s32[]{:S(2)}) async-start(), calls=%async_computation.12 | async-start | bytes 4866048 | tf_op jit(solution)/shard_map/reduce_scatter | solution.py:821
  827.1 70.4 %collective-permute-start.22 = (bf16[256,1536]{1,0:T(8,128)(2,1)}, bf16[256,1536]{1,0:T(8,128)(2,1)S(1)}, u32[]{:S(2)}, u32[]{:S(2)}) collective-permute-start(bf16[256,1536]{1,0:T(8,128)(2,1)} %get-tuple-element.161), channel_id=1, source_target_pairs={{0,16},{1,17},{2,18},{3,19},{4,20},{5,21},{6,22},{7,23},{8,24},{9,... | collective-permute-start | bytes 2359304 | tf_op jit(solution)/shard_map/ppermute | solution.py:535
  828.7 68.8 %collective-permute-start.23 = (bf16[256,1536]{1,0:T(8,128)(2,1)}, bf16[256,1536]{1,0:T(8,128)(2,1)}, u32[]{:S(2)}, u32[]{:S(2)}) collective-permute-start(bf16[256,1536]{1,0:T(8,128)(2,1)} %get-tuple-element.162), channel_id=1, source_target_pairs={{0,8},{1,9},{2,10},{3,11},{4,12},{5,13},{6,14},{7,15},{8,16},{9,17... | collective-permute-start | bytes 2359304 | tf_op jit(solution)/shard_map/ppermute | solution.py:535
  947.2 82.6 %collective-permute-start.28 = (bf16[256,1536]{1,0:T(8,128)(2,1)S(1)}, bf16[256,1536]{1,0:T(8,128)(2,1)S(1)}, u32[]{:S(2)}, u32[]{:S(2)}) collective-permute-start(bf16[256,1536]{1,0:T(8,128)(2,1)S(1)} %copy-done.57), channel_id=1, source_target_pairs={{0,16},{1,17},{2,18},{3,19},{4,20},{5,21},{6,22},{7,23},{8,24},{9,... | collective-permute-start | bytes 2359304 | tf_op jit(solution)/shard_map/ppermute | solution.py:535
  948.7 81.1 %collective-permute-start.29 = (bf16[256,1536]{1,0:T(8,128)(2,1)S(1)}, bf16[256,1536]{1,0:T(8,128)(2,1)S(1)}, u32[]{:S(2)}, u32[]{:S(2)}) collective-permute-start(bf16[256,1536]{1,0:T(8,128)(2,1)S(1)} %copy-done.56), channel_id=1, source_target_pairs={{0,8},{1,9},{2,10},{3,11},{4,12},{5,13},{6,14},{7,15},{8,16},{9,17... | collective-permute-start | bytes 2359304 | tf_op jit(solution)/shard_map/ppermute | solution.py:535
  (83 other events, 1608.8 us)
Sparse Core Ops, SparseCore 0:
  14.0 194.1 all-gather.1
  926.9 153.4 reduce-scatter.1

commit v8 on v7

--- a/solution.py
+++ b/solution.py
@@ -771,7 +771,9 @@
     moved_grads1 = exchange(hold(grads1, pair_back))
     pair_blocks = pairs_home(pair_back)
     back0 = sums_of(0, moved_grads0)
-    moved_scaled0 = exchange(hold(scaled0, moved_grads1, back0, pair_blocks))
+    expert_w = [a + b for a, b in zip(weights0, weights1, strict=True)]
+    moved_scaled0 = exchange(hold(scaled0, moved_grads1, back0, pair_blocks, expert_w))
+    grad_gate_w, grad_up_w, grad_down_w = expert_w
     back1 = sums_of(1, moved_grads1)
     result0 = attend_back(
         0,
@@ -812,9 +814,6 @@
     )
     gain_second_w = (result0[4] + result1[4])[0]
     gain_first_w = (result0[5] + result1[5])[0]
-    grad_gate_w, grad_up_w, grad_down_w = (
-        a + b for a, b in zip(weights0, weights1, strict=True)
-    )
 
     small_w = jnp.concatenate([gain_first_w[:, None], gain_second_w[:, None], router_w], axis=1)
     small_w = jnp.pad(small_w, ((0, 0), (0, -small_w.shape[1] % 128)))

time: 1100 us -> 1100 us (level)
  waiting for transfers between devices: 583 us -> 569 us
    ppermute x15, waiting for transfers between devices: 182 us -> 168 us  [give_back(): lax.ppermute(blocks[step], 'dp', line_shift(-step))]
  transfers between devices with their start and end apart: 48 -> 48, of which waited for: 25 -> 26; matrix products, arithmetic and copies ran while one was open for 10% -> 10% of each run, Pallas kernels for 23% -> 23%
where the time goes in v8:
time: 1100 us; the launch traced here: 1090 us
  waiting for transfers between devices  569 us (52%)
  Pallas kernels  249 us (23%)
  starting transfers between devices  111 us (10%)
  local copies, waits for them, and re-layouts  54.2 us (5%)
  other arithmetic  46.9 us (4%)
  matrix products  24.7 us (2%)
  blocking collectives  15.6 us (1%)
  between operations  15.4 us (1%)
    ppermute x15, waiting for transfers between devices, spread(): lax.ppermute(block, 'dp', line_shift(step))  297 us
    ppermute x15, waiting for transfers between devices, give_back(): lax.ppermute(blocks[step], 'dp', line_shift(-step))  168 us
    pallas_call x2, Pallas kernels, run_experts(): pl.pallas_call(expert_kernel, grid=(count // block,), in_specs=[wide, wid...  93.2 us
    all_to_all x8, waiting for transfers between devices, exchange(): lax.all_to_all(block, 'dp', split_axis=0, concat_axis=0, tiled=True, axis...  48.2 us
    all_to_all x8, starting transfers between devices, exchange(): lax.all_to_all(block, 'dp', split_axis=0, concat_axis=0, tiled=True, axis...  40.1 us
    ppermute x5, waiting for transfers between devices, fold(): lax.ppermute(sent.astype(bf16), 'dp', [(i, i ^ bit) for i in range(device...  36.8 us
    pallas_call x2, Pallas kernels, run_attention_back(): pl.pallas_call(attend_back_kernel, grid=(1, KVH // 2), in_specs=[at(wide,...  33.8 us
    ppermute x15, starting transfers between devices, give_back(): lax.ppermute(blocks[step], 'dp', line_shift(-step))  29.2 us
  transfers between devices with their start and end apart: 48, of which 26 were waited for; matrix products, arithmetic and copies ran while one was open for 10% of the time, Pallas kernels for 23%

profile of v8, /device:TPU:0, one launch (start us, length us, event | category | flops | bytes accessed | tf_op | source)
XLA Modules:
  0.0 1086.8 jit_solution(375758371908842389)
XLA Ops:
  42.2 15.2 %collective-permute-done.5.refs_3_ = bf16[256,1536]{1,0:T(8,128)(2,1)S(1)} collective-permute-done((bf16[256,1536]{1,0:T(8,128)(2,1)S(1)}, bf16[256,1536]{1,0:T(8,128)(2,1)S(1)}, u32[]{:S(2)}, u32[]{:S(2)}) %collective-permute-start.5) | collective-permute-done | bytes 786464 | tf_op jit(solution)/shard_map/ppermute | solution.py:530
  57.4 67.3 %collective-permute-done.4.refs_2_ = bf16[256,1536]{1,0:T(8,128)(2,1)S(1)} collective-permute-done((bf16[256,1536]{1,0:T(8,128)(2,1)S(1)}, bf16[256,1536]{1,0:T(8,128)(2,1)S(1)}, u32[]{:S(2)}, u32[]{:S(2)}) %collective-permute-start.4) | collective-permute-done | bytes 786464 | tf_op jit(solution)/shard_map/ppermute | solution.py:530
  152.4 21.1 %collective-permute-done.8.refs_3_ = bf16[256,1536]{1,0:T(8,128)(2,1)} collective-permute-done((bf16[256,1536]{1,0:T(8,128)(2,1)}, bf16[256,1536]{1,0:T(8,128)(2,1)}, u32[]{:S(2)}, u32[]{:S(2)}) %collective-permute-start.8) | collective-permute-done | bytes 786464 | tf_op jit(solution)/shard_map/ppermute | solution.py:530
  173.5 55.2 %collective-permute-done.7.refs_2_ = bf16[256,1536]{1,0:T(8,128)(2,1)} collective-permute-done((bf16[256,1536]{1,0:T(8,128)(2,1)}, bf16[256,1536]{1,0:T(8,128)(2,1)}, u32[]{:S(2)}, u32[]{:S(2)}) %collective-permute-start.7) | collective-permute-done | bytes 786464 | tf_op jit(solution)/shard_map/ppermute | solution.py:530
  230.9 9.7 fusion.100.query_ref.key_ref.value_ref
  240.6 18.7 %attention.1 = (bf16[512,1536]{1,0:T(8,128)(2,1)}, bf16[512,512]{1,0:T(8,128)(2,1)}, bf16[512,512]{1,0:T(8,128)(2,1)}, bf16[512,1536]{1,0:T(8,128)(2,1)}) custom-call(f32[512,2560]{1,0:T(8,128)} %fusion.100.query_ref.key_ref.value_ref, f32[512,2560]{1,0:T(8,128)} %fusion.100.query_ref.key_ref.value_ref, f32[512,2560]{1,0:T(8,128)} %fusion.100.query_ref.key_ref.value_ref, ...), custom_call_target="tpu_custom_call" | custom-call | flops 1000 | bytes 1000 | tf_op jit(solution)/shard_map/attention/pallas_call | solution.py:280
  283.4 19.2 %collective-permute-done.11.refs_3_ = bf16[256,1536]{1,0:T(8,128)(2,1)S(1)} collective-permute-done((bf16[256,1536]{1,0:T(8,128)(2,1)S(1)}, bf16[256,1536]{1,0:T(8,128)(2,1)S(1)}, u32[]{:S(2)}, u32[]{:S(2)}) %collective-permute-start.11) | collective-permute-done | bytes 786464 | tf_op jit(solution)/shard_map/ppermute | solution.py:530
  302.6 47.3 %collective-permute-done.10.refs_2_ = bf16[256,1536]{1,0:T(8,128)(2,1)S(1)} collective-permute-done((bf16[256,1536]{1,0:T(8,128)(2,1)S(1)}, bf16[256,1536]{1,0:T(8,128)(2,1)S(1)}, u32[]{:S(2)}, u32[]{:S(2)}) %collective-permute-start.10) | collective-permute-done | bytes 786464 | tf_op jit(solution)/shard_map/ppermute | solution.py:530
  367.0 15.6 %collective-permute-done.14.refs_3_ = bf16[256,1536]{1,0:T(8,128)(2,1)} collective-permute-done((bf16[256,1536]{1,0:T(8,128)(2,1)}, bf16[256,1536]{1,0:T(8,128)(2,1)}, u32[]{:S(2)}, u32[]{:S(2)}) %collective-permute-start.14) | collective-permute-done | bytes 786464 | tf_op jit(solution)/shard_map/ppermute | solution.py:530
  382.6 51.3 %collective-permute-done.13.refs_2_ = bf16[256,1536]{1,0:T(8,128)(2,1)} collective-permute-done((bf16[256,1536]{1,0:T(8,128)(2,1)}, bf16[256,1536]{1,0:T(8,128)(2,1)}, u32[]{:S(2)}, u32[]{:S(2)}) %collective-permute-start.13) | collective-permute-done | bytes 786464 | tf_op jit(solution)/shard_map/ppermute | solution.py:530
  466.0 46.6 %experts.2 = (bf16[2304,1536]{1,0:T(8,128)(2,1)}, bf16[2304,1536]{1,0:T(8,128)(2,1)}, f32[2304,1]{1,0:T(8,128)}, f32[1536,512]{1,0:T(8,128)}, f32[1536,512]{1,0:T(8,128)}, /*index=5*/f32[512,1536]{1,0:T(8,128)}) custom-call(bf16[2304,1536]{1,0:T(8,128)(2,1)} %bitcast.18.rows_ref, bf16[2304,1536]{1,0:T(8,128)(2,1)} %bitcast.19.blend_ref, ...), custom_call_target="tpu_custom_call" | custom-call | flops 1000 | bytes 1000 | tf_op jit(solution)/shard_map/experts/pallas_call | solution.py:99
  512.6 31.3 %all-to-all-done.4 = bf16[8,288,1536]{2,1,0:T(8,128)(2,1)} async-done(((bf16[8,288,1536]{2,1,0:T(8,128)(2,1)}), bf16[8,288,1536]{2,1,0:T(8,128)(2,1)}, u32[]{:S(2)}, u32[]{:S(2)}) %all-to-all-start.4) | async-done | bytes 7077920 | tf_op jit(solution)/shard_map/all_to_all | solution.py:574
  564.3 46.6 %experts.3 = (bf16[2304,1536]{1,0:T(8,128)(2,1)}, bf16[2304,1536]{1,0:T(8,128)(2,1)}, f32[2304,1]{1,0:T(8,128)}, f32[1536,512]{1,0:T(8,128)}, f32[1536,512]{1,0:T(8,128)}, /*index=5*/f32[512,1536]{1,0:T(8,128)}) custom-call(bf16[2304,1536]{1,0:T(8,128)(2,1)} %bitcast.39.rows_ref, bf16[2304,1536]{1,0:T(8,128)(2,1)} %bitcast.40.blend_ref, ...), custom_call_target="tpu_custom_call" | custom-call | flops 1000 | bytes 1000 | tf_op jit(solution)/shard_map/experts/pallas_call | solution.py:99
  612.6 16.3 %all-to-all-done.5 = bf16[8,288,1536]{2,1,0:T(8,128)(2,1)} async-done(((bf16[8,288,1536]{2,1,0:T(8,128)(2,1)}), bf16[8,288,1536]{2,1,0:T(8,128)(2,1)}, u32[]{:S(2)}, u32[]{:S(2)}) %all-to-all-start.5) | async-done | bytes 7077920 | tf_op jit(solution)/shard_map/all_to_all | solution.py:574
  654.4 47.4 %collective-permute-done.20 = f32[2,8,256]{2,1,0:T(8,128)S(1)} collective-permute-done((f32[2,8,256]{2,1,0:T(8,128)S(1)}, f32[2,8,256]{2,1,0:T(8,128)S(1)}, u32[]{:S(2)}, u32[]{:S(2)}) %collective-permute-start.20) | collective-permute-done | bytes 16416 | tf_op jit(solution)/shard_map/ppermute | solution.py:535
  739.9 13.9 %collective-permute-start.24 = (bf16[256,1536]{1,0:T(8,128)(2,1)}, bf16[256,1536]{1,0:T(8,128)(2,1)S(1)}, u32[]{:S(2)}, u32[]{:S(2)}) collective-permute-start(bf16[256,1536]{1,0:T(8,128)(2,1)} %get-tuple-element.170), channel_id=1, source_target_pairs={{0,24},{1,25},{2,26},{3,27},{4,28},{5,29},{6,30},{7,31},{8,0},{9,1... | collective-permute-start | bytes 2359304 | tf_op jit(solution)/shard_map/ppermute | solution.py:535
  763.4 16.9 %attention_back.2 = (bf16[256,1536]{1,0:T(8,128)(2,1)}, bf16[256,512]{1,0:T(8,128)(2,1)}, bf16[256,512]{1,0:T(8,128)(2,1)}) custom-call(bf16[512,1536]{1,0:T(8,128)(2,1)} %get-tuple-element.142.query_ref, bf16[512,512]{1,0:T(8,128)(2,1)} %get-tuple-element.143.key_ref, bf16[512,512]{1,0:T(8,128)(2,1)} %get-tuple-element.144.value_ref, ...), custom_call_target="tpu_custom_call" | custom-call | flops 1000 | bytes 1000 | tf_op jit(solution)/shard_map/attention_back/pallas_call | solution.py:319
  788.6 32.4 %collective-permute-done.25.refs_2_ = bf16[256,1536]{1,0:T(8,128)(2,1)S(1)} collective-permute-done((bf16[256,1536]{1,0:T(8,128)(2,1)}, bf16[256,1536]{1,0:T(8,128)(2,1)S(1)}, u32[]{:S(2)}, u32[]{:S(2)}) %collective-permute-start.25) | collective-permute-done | bytes 786464 | tf_op jit(solution)/shard_map/ppermute | solution.py:535
  856.6 16.9 %attention_back.3 = (bf16[256,1536]{1,0:T(8,128)(2,1)}, bf16[256,512]{1,0:T(8,128)(2,1)}, bf16[256,512]{1,0:T(8,128)(2,1)}) custom-call(bf16[512,1536]{1,0:T(8,128)(2,1)} %get-tuple-element.142.query_ref, bf16[512,512]{1,0:T(8,128)(2,1)} %get-tuple-element.143.key_ref, bf16[512,512]{1,0:T(8,128)(2,1)} %get-tuple-element.144.value_ref, ...), custom_call_target="tpu_custom_call" | custom-call | flops 1000 | bytes 1000 | tf_op jit(solution)/shard_map/attention_back/pallas_call | solution.py:319
  881.9 25.4 %collective-permute-done.22 = bf16[256,1536]{1,0:T(8,128)(2,1)S(1)} collective-permute-done((bf16[256,1536]{1,0:T(8,128)(2,1)}, bf16[256,1536]{1,0:T(8,128)(2,1)S(1)}, u32[]{:S(2)}, u32[]{:S(2)}) %collective-permute-start.22) | collective-permute-done | bytes 786464 | tf_op jit(solution)/shard_map/ppermute | solution.py:535
  909.3 10.3 weights.3
  949.1 14.2 %collective-permute-done.31 = bf16[4,2,48,1280]{3,2,1,0:T(8,128)(2,1)S(1)} collective-permute-done((bf16[4,2,48,1280]{3,2,1,0:T(8,128)(2,1)S(1)}, bf16[4,2,48,1280]{3,2,1,0:T(8,128)(2,1)S(1)}, u32[]{:S(2)}, u32[]{:S(2)}) %collective-permute-start.31) | collective-permute-done | bytes 983072 | tf_op jit(solution)/shard_map/ppermute | solution.py:554
  969.5 57.9 %collective-permute-done.28 = bf16[256,1536]{1,0:T(8,128)(2,1)S(1)} collective-permute-done((bf16[256,1536]{1,0:T(8,128)(2,1)S(1)}, bf16[256,1536]{1,0:T(8,128)(2,1)S(1)}, u32[]{:S(2)}, u32[]{:S(2)}) %collective-permute-start.28) | collective-permute-done | bytes 786464 | tf_op jit(solution)/shard_map/ppermute | solution.py:535
  1031.2 10.9 %collective-permute-done.33 = bf16[4,48,1280]{2,1,0:T(8,128)(2,1)S(1)} collective-permute-done((bf16[4,48,1280]{2,1,0:T(8,128)(2,1)S(1)}, bf16[4,48,1280]{2,1,0:T(8,128)(2,1)S(1)}, u32[]{:S(2)}, u32[]{:S(2)}) %collective-permute-start.33) | collective-permute-done | bytes 491552 | tf_op jit(solution)/shard_map/ppermute | solution.py:554
  (330 shorter events, 363.8 us)
Async XLA Ops:
  7.2 221.8 %all-gather.2.cloned.1.call-start = ((), (), s32[]{:S(2)}) async-start(), calls=%async_computation.11 | async-start | bytes 13381632 | tf_op jit(solution)/shard_map/all_gather | solution.py:580
  35.7 89.0 %collective-permute-start.4 = (bf16[256,1536]{1,0:T(8,128)(2,1)S(1)}, bf16[256,1536]{1,0:T(8,128)(2,1)S(1)}, u32[]{:S(2)}, u32[]{:S(2)}) collective-permute-start(bf16[256,1536]{1,0:T(8,128)(2,1)S(1)} %get-tuple-element.107.refs_0_), channel_id=1, source_target_pairs={{0,16},{1,17},{2,18},{3,19},{4,20},{5,21},{6,22},{7,23},{8,24},{9,... | collective-permute-start | bytes 2359304 | tf_op jit(solution)/shard_map/ppermute | solution.py:530
  39.6 85.1 %collective-permute-start.3 = (bf16[256,1536]{1,0:T(8,128)(2,1)S(1)}, bf16[256,1536]{1,0:T(8,128)(2,1)S(1)}, u32[]{:S(2)}, u32[]{:S(2)}) collective-permute-start(bf16[256,1536]{1,0:T(8,128)(2,1)S(1)} %get-tuple-element.107.refs_0_), channel_id=1, source_target_pairs={{0,8},{1,9},{2,10},{3,11},{4,12},{5,13},{6,14},{7,15},{8,16},{9,17... | collective-permute-start | bytes 2359304 | tf_op jit(solution)/shard_map/ppermute | solution.py:530
  132.7 133.3 %all-to-all-start = ((bf16[8,288,1536]{2,1,0:T(8,128)(2,1)}), bf16[8,288,1536]{2,1,0:T(8,128)(2,1)}, u32[]{:S(2)}, u32[]{:S(2)}) async-start(bf16[8,288,1536]{2,1,0:T(8,128)(2,1)} %bitcast.173), calls=%async_computation | async-start | bytes 14155776 | tf_op jit(solution)/shard_map/all_to_all | solution.py:574
  137.8 90.8 %collective-permute-start.7 = (bf16[256,1536]{1,0:T(8,128)(2,1)}, bf16[256,1536]{1,0:T(8,128)(2,1)}, u32[]{:S(2)}, u32[]{:S(2)}) collective-permute-start(bf16[256,1536]{1,0:T(8,128)(2,1)} %get-tuple-element.111.refs_0_), channel_id=1, source_target_pairs={{0,16},{1,17},{2,18},{3,19},{4,20},{5,21},{6,22},{7,23},{8,24},{9,... | collective-permute-start | bytes 2359304 | tf_op jit(solution)/shard_map/ppermute | solution.py:530
  145.4 83.3 %collective-permute-start.6 = (bf16[256,1536]{1,0:T(8,128)(2,1)}, bf16[256,1536]{1,0:T(8,128)(2,1)}, u32[]{:S(2)}, u32[]{:S(2)}) collective-permute-start(bf16[256,1536]{1,0:T(8,128)(2,1)} %get-tuple-element.111.refs_0_), channel_id=1, source_target_pairs={{0,8},{1,9},{2,10},{3,11},{4,12},{5,13},{6,14},{7,15},{8,16},{9,17... | collective-permute-start | bytes 2359304 | tf_op jit(solution)/shard_map/ppermute | solution.py:530
  266.0 91.4 %all-to-all-start.1 = ((bf16[8,288,1536]{2,1,0:T(8,128)(2,1)}), bf16[8,288,1536]{2,1,0:T(8,128)(2,1)}, u32[]{:S(2)}, u32[]{:S(2)}) async-start(bf16[8,288,1536]{2,1,0:T(8,128)(2,1)} %bitcast.175), calls=%async_computation.1 | async-start | bytes 14155776 | tf_op jit(solution)/shard_map/all_to_all | solution.py:574
  282.3 68.5 %collective-permute-start.9 = (bf16[256,1536]{1,0:T(8,128)(2,1)S(1)}, bf16[256,1536]{1,0:T(8,128)(2,1)}, u32[]{:S(2)}, u32[]{:S(2)}) collective-permute-start(bf16[256,1536]{1,0:T(8,128)(2,1)S(1)} %get-tuple-element.306.refs_0_), channel_id=1, source_target_pairs={{0,8},{1,9},{2,10},{3,11},{4,12},{5,13},{6,14},{7,15},{8,16},{9,17... | collective-permute-start | bytes 2359304 | tf_op jit(solution)/shard_map/ppermute | solution.py:530
  357.4 92.8 %all-to-all-start.2 = ((bf16[8,288,1536]{2,1,0:T(8,128)(2,1)}), bf16[8,288,1536]{2,1,0:T(8,128)(2,1)}, u32[]{:S(2)}, u32[]{:S(2)}) async-start(bf16[8,288,1536]{2,1,0:T(8,128)(2,1)} %bitcast.172), calls=%async_computation.2 | async-start | bytes 14155776 | tf_op jit(solution)/shard_map/all_to_all | solution.py:574
  362.5 71.3 %collective-permute-start.13 = (bf16[256,1536]{1,0:T(8,128)(2,1)}, bf16[256,1536]{1,0:T(8,128)(2,1)}, u32[]{:S(2)}, u32[]{:S(2)}) collective-permute-start(bf16[256,1536]{1,0:T(8,128)(2,1)} %get-tuple-element.307.refs_0_), channel_id=1, source_target_pairs={{0,16},{1,17},{2,18},{3,19},{4,20},{5,21},{6,22},{7,23},{8,24},{9,... | collective-permute-start | bytes 2359304 | tf_op jit(solution)/shard_map/ppermute | solution.py:530
  365.0 68.8 %collective-permute-start.12 = (bf16[256,1536]{1,0:T(8,128)(2,1)}, bf16[256,1536]{1,0:T(8,128)(2,1)}, u32[]{:S(2)}, u32[]{:S(2)}) collective-permute-start(bf16[256,1536]{1,0:T(8,128)(2,1)} %get-tuple-element.307.refs_0_), channel_id=1, source_target_pairs={{0,8},{1,9},{2,10},{3,11},{4,12},{5,13},{6,14},{7,15},{8,16},{9,17... | collective-permute-start | bytes 2359304 | tf_op jit(solution)/shard_map/ppermute | solution.py:530
  458.7 85.2 %all-to-all-start.4 = ((bf16[8,288,1536]{2,1,0:T(8,128)(2,1)}), bf16[8,288,1536]{2,1,0:T(8,128)(2,1)}, u32[]{:S(2)}, u32[]{:S(2)}) async-start(bf16[8,288,1536]{2,1,0:T(8,128)(2,1)} %bitcast.174), calls=%async_computation.4 | async-start | bytes 14155776 | tf_op jit(solution)/shard_map/all_to_all | solution.py:574
  543.9 85.0 %all-to-all-start.5 = ((bf16[8,288,1536]{2,1,0:T(8,128)(2,1)}), bf16[8,288,1536]{2,1,0:T(8,128)(2,1)}, u32[]{:S(2)}, u32[]{:S(2)}) async-start(bf16[8,288,1536]{2,1,0:T(8,128)(2,1)} %bitcast.179), calls=%async_computation.5 | async-start | bytes 14155776 | tf_op jit(solution)/shard_map/all_to_all | solution.py:574
  636.1 84.9 %all-to-all-start.7 = ((bf16[8,288,1536]{2,1,0:T(8,128)(2,1)}), bf16[8,288,1536]{2,1,0:T(8,128)(2,1)}, u32[]{:S(2)}, u32[]{:S(2)}) async-start(bf16[8,288,1536]{2,1,0:T(8,128)(2,1)} %bitcast.178), calls=%async_computation.7 | async-start | bytes 14155776 | tf_op jit(solution)/shard_map/all_to_all | solution.py:574
  647.5 72.8 %collective-permute-start.15 = (bf16[256,1536]{1,0:T(8,128)(2,1)}, bf16[256,1536]{1,0:T(8,128)(2,1)}, u32[]{:S(2)}, u32[]{:S(2)}) collective-permute-start(bf16[256,1536]{1,0:T(8,128)(2,1)} %get-tuple-element.132), channel_id=1, source_target_pairs={{0,24},{1,25},{2,26},{3,27},{4,28},{5,29},{6,30},{7,31},{8,0},{9,1... | collective-permute-start | bytes 2359304 | tf_op jit(solution)/shard_map/ppermute | solution.py:535
  647.5 72.8 %collective-permute-start.16 = (bf16[256,1536]{1,0:T(8,128)(2,1)}, bf16[256,1536]{1,0:T(8,128)(2,1)}, u32[]{:S(2)}, u32[]{:S(2)}) collective-permute-start(bf16[256,1536]{1,0:T(8,128)(2,1)} %get-tuple-element.133), channel_id=1, source_target_pairs={{0,16},{1,17},{2,18},{3,19},{4,20},{5,21},{6,22},{7,23},{8,24},{9,... | collective-permute-start | bytes 2359304 | tf_op jit(solution)/shard_map/ppermute | solution.py:535
  648.0 72.3 %collective-permute-start.17 = (bf16[256,1536]{1,0:T(8,128)(2,1)}, bf16[256,1536]{1,0:T(8,128)(2,1)}, u32[]{:S(2)}, u32[]{:S(2)}) collective-permute-start(bf16[256,1536]{1,0:T(8,128)(2,1)} %get-tuple-element.134), channel_id=1, source_target_pairs={{0,8},{1,9},{2,10},{3,11},{4,12},{5,13},{6,14},{7,15},{8,16},{9,17... | collective-permute-start | bytes 2359304 | tf_op jit(solution)/shard_map/ppermute | solution.py:535
  721.0 100.1 %all-to-all-start.8 = ((bf16[8,288,1536]{2,1,0:T(8,128)(2,1)}), bf16[8,288,1536]{2,1,0:T(8,128)(2,1)}, u32[]{:S(2)}, u32[]{:S(2)}) async-start(bf16[8,288,1536]{2,1,0:T(8,128)(2,1)} %bitcast.177), calls=%async_computation.8 | async-start | bytes 14155776 | tf_op jit(solution)/shard_map/all_to_all | solution.py:574
  822.3 97.2 %all-to-all-start.9 = ((bf16[8,288,1536]{2,1,0:T(8,128)(2,1)}), bf16[8,288,1536]{2,1,0:T(8,128)(2,1)}, u32[]{:S(2)}, u32[]{:S(2)}) async-start(bf16[8,288,1536]{2,1,0:T(8,128)(2,1)} %bitcast.176), calls=%async_computation.9 | async-start | bytes 14155776 | tf_op jit(solution)/shard_map/all_to_all | solution.py:574
  827.2 250.2 %reduce-scatter.2.cloned.1.call-start = ((), (), s32[]{:S(2)}) async-start(), calls=%async_computation.12 | async-start | bytes 4866048 | tf_op jit(solution)/shard_map/reduce_scatter | solution.py:820
  835.6 71.7 %collective-permute-start.22 = (bf16[256,1536]{1,0:T(8,128)(2,1)}, bf16[256,1536]{1,0:T(8,128)(2,1)S(1)}, u32[]{:S(2)}, u32[]{:S(2)}) collective-permute-start(bf16[256,1536]{1,0:T(8,128)(2,1)} %get-tuple-element.167), channel_id=1, source_target_pairs={{0,16},{1,17},{2,18},{3,19},{4,20},{5,21},{6,22},{7,23},{8,24},{9,... | collective-permute-start | bytes 2359304 | tf_op jit(solution)/shard_map/ppermute | solution.py:535
  838.5 68.8 %collective-permute-start.23 = (bf16[256,1536]{1,0:T(8,128)(2,1)}, bf16[256,1536]{1,0:T(8,128)(2,1)}, u32[]{:S(2)}, u32[]{:S(2)}) collective-permute-start(bf16[256,1536]{1,0:T(8,128)(2,1)} %get-tuple-element.168), channel_id=1, source_target_pairs={{0,8},{1,9},{2,10},{3,11},{4,12},{5,13},{6,14},{7,15},{8,16},{9,17... | collective-permute-start | bytes 2359304 | tf_op jit(solution)/shard_map/ppermute | solution.py:535
  946.8 80.6 %collective-permute-start.28 = (bf16[256,1536]{1,0:T(8,128)(2,1)S(1)}, bf16[256,1536]{1,0:T(8,128)(2,1)S(1)}, u32[]{:S(2)}, u32[]{:S(2)}) collective-permute-start(bf16[256,1536]{1,0:T(8,128)(2,1)S(1)} %copy-done.52), channel_id=1, source_target_pairs={{0,16},{1,17},{2,18},{3,19},{4,20},{5,21},{6,22},{7,23},{8,24},{9,... | collective-permute-start | bytes 2359304 | tf_op jit(solution)/shard_map/ppermute | solution.py:535
  946.9 80.5 %collective-permute-start.29 = (bf16[256,1536]{1,0:T(8,128)(2,1)S(1)}, bf16[256,1536]{1,0:T(8,128)(2,1)S(1)}, u32[]{:S(2)}, u32[]{:S(2)}) collective-permute-start(bf16[256,1536]{1,0:T(8,128)(2,1)S(1)} %copy-done.51), channel_id=1, source_target_pairs={{0,8},{1,9},{2,10},{3,11},{4,12},{5,13},{6,14},{7,15},{8,16},{9,17... | collective-permute-start | bytes 2359304 | tf_op jit(solution)/shard_map/ppermute | solution.py:535
  (78 other events, 1544.8 us)
Sparse Core Ops, SparseCore 0:
  13.9 194.1 all-gather.1
  925.5 151.8 reduce-scatter.1
